TPU v7x, 32 devices: a whole 2x2x4 slice. The times are simulated.
32 devices in a mesh: section: 2 (over x), seq: 4 (over z), tensor: 4 (over y, core).
Axes of the slice: x: 2, y: 2, z: 4, core: 2. Of those that a mesh axis runs over, the one named last changes fastest.
Arguments:
- q_mant: bfloat16 [2, 256, 16384], P('section', 'seq', 'tensor'), may hold values from -32 to 32
- q_scale: int32 [2, 256, 512], P('section', 'seq', 'tensor'), may hold values from -2 to 2
- key_mantissa_block: bfloat16 [2, 256, 1024], P('section', 'seq', 'tensor'), may hold values from -32 to 32
- key_exponent_scale: int32 [2, 256, 32], P('section', 'seq', 'tensor'), may hold values from -2 to 2
- value_mantissa_block: bfloat16 [2, 256, 1024], P('section', 'seq', 'tensor'), may hold values from -6 to 6
- value_exponent_scale: int32 [2, 256, 32], P('section', 'seq', 'tensor'), may hold values from -1 to 1
- cached_key_rows: bfloat16 [2, 8, 512, 128], P('section', 'tensor', 'seq'), may hold values from -12 to 12
- cached_value_rows: bfloat16 [2, 8, 512, 128], P('section', 'tensor', 'seq'), may hold values from -8 to 8
- start: int32 [2], P('section'), may hold values from 256 to 512, as said below
Outputs:
- attended: bfloat16 [2, 256, 16384], P('section', 'seq', 'tensor')
Inputs may be any that keep to these rules, and one draw needn't show every extreme that they name: The first start[s] cached positions of section s hold earlier tokens; the cache of some section is full in every draw.
All inputs are finite; a program needn't handle non-finite values.
Results may differ from a plain program's by a relative error of at most 0.0023.
Values may be sent and summed in bfloat16 or wider, within the bound.
No kernel may reach another device: no remote copies, remote signals or barrier semaphores. Data moves between devices by JAX's collectives and lax.ppermute only.
A program may use at most 64 MiB of HBM per device.

v0:
```python
import math

import jax
import jax.numpy as jnp
from jax import lax
from jax.sharding import PartitionSpec as P


def shifted(block, axis, distance):
    devices = range(lax.axis_size(axis))
    route = [((i - distance) % len(devices), i) for i in devices]
    return lax.ppermute(block, axis, route)


def decode_mantissas(mantissa, exponent):
    row_count, feature_count = mantissa.shape
    blocks = mantissa.astype(jnp.float32).reshape(row_count, feature_count // 32, 32)
    factor = jnp.exp2(exponent.astype(jnp.float32))[:, :, None]
    return (blocks * factor).reshape(row_count, feature_count).astype(jnp.bfloat16)


def attend(running, queries, section_key_rows, section_value_rows, key_start, from_cache, limit):
    head_count, tokens, head_size = queries.shape
    key_count = section_key_rows.shape[1]
    block_rows = min(512, tokens)
    inv_root = 1.0 / math.sqrt(head_size)
    key_first = jnp.asarray(key_start, jnp.int32)
    key_index = lax.iota(jnp.int32, key_count)

    def one_block(number, running):
        first_row = number * block_rows

        def update(running):
            row_max, row_total, row_sum = running
            query_block = lax.dynamic_slice_in_dim(queries, first_row, block_rows, 1)
            scores = (
                jnp.einsum(
                    "hqd,hkd->hqk",
                    query_block,
                    section_key_rows,
                    preferred_element_type=jnp.float32,
                )
                * inv_root
            )
            if from_cache:
                allowed = jnp.broadcast_to((key_index < limit)[None, None, :], scores.shape)
            else:
                query_index = first_row + lax.iota(jnp.int32, block_rows)
                allowed = jnp.broadcast_to(
                    (key_index[None, :] <= query_index[:, None])[None], scores.shape
                )
            scores = jnp.where(allowed, scores, -1e30)
            old_max = lax.dynamic_slice_in_dim(row_max, first_row, block_rows, 1)
            new_max = jnp.maximum(old_max, jnp.max(scores, axis=2))
            weights = jnp.where(allowed, jnp.exp(scores - new_max[:, :, None]), 0.0)
            factor = jnp.exp(old_max - new_max)
            old_total = lax.dynamic_slice_in_dim(row_total, first_row, block_rows, 1)
            new_total = old_total * factor + jnp.sum(weights, axis=2)
            product = jnp.einsum(
                "hqk,hkd->hqd",
                weights.astype(jnp.bfloat16),
                section_value_rows,
                preferred_element_type=jnp.float32,
            )
            old_sum = lax.dynamic_slice_in_dim(row_sum, first_row, block_rows, 1)
            new_sum = old_sum * factor[:, :, None] + product
            return (
                lax.dynamic_update_slice_in_dim(row_max, new_max, first_row, 1),
                lax.dynamic_update_slice_in_dim(row_total, new_total, first_row, 1),
                lax.dynamic_update_slice_in_dim(row_sum, new_sum, first_row, 1),
            )

        if from_cache:
            visible = key_first < limit
        else:
            visible = key_first <= first_row + block_rows - 1
        return lax.cond(visible, update, lambda unchanged: unchanged, running)

    return lax.fori_loop(0, tokens // block_rows, one_block, running)


def body(
    q_mant,
    q_scale,
    key_mantissa_block,
    key_exponent_scale,
    value_mantissa_block,
    value_exponent_scale,
    cached_key_rows,
    cached_value_rows,
    start,
):
    arrived = shifted(
        (
            q_mant[0],
            key_mantissa_block[0],
            value_mantissa_block[0],
            q_scale[0].astype(jnp.bfloat16),
            key_exponent_scale[0].astype(jnp.bfloat16),
            value_exponent_scale[0].astype(jnp.bfloat16),
        ),
        "section",
        1,
    )
    row_count = q_mant.shape[1]
    kv_here = cached_key_rows.shape[1]
    head_size = cached_key_rows.shape[3]
    queries = decode_mantissas(arrived[0], arrived[3]).reshape(row_count, -1, head_size)
    section_key_rows = decode_mantissas(arrived[1], arrived[4]).reshape(
        row_count, kv_here, head_size
    )
    section_value_rows = decode_mantissas(arrived[2], arrived[5]).reshape(
        row_count, kv_here, head_size
    )
    heads_here = queries.shape[1]
    query_group_width = heads_here // kv_here
    seq_count = lax.axis_size("seq")
    local_heads = heads_here // seq_count
    tokens = row_count * seq_count
    limit = start[0]
    mine = lax.all_to_all(queries, "seq", split_axis=1, concat_axis=0, tiled=True)
    query_block = jnp.transpose(mine, (1, 0, 2))
    running = (
        jnp.full((local_heads, tokens), -1e30, jnp.float32),
        jnp.zeros((local_heads, tokens), jnp.float32),
        jnp.zeros((local_heads, tokens, head_size), jnp.float32),
    )
    head_ids = lax.axis_index("seq") * local_heads + lax.iota(jnp.int32, local_heads)
    kv_ids = head_ids // query_group_width
    pieces = (
        lax.all_gather(cached_key_rows[0], "seq", axis=1, tiled=True),
        lax.all_gather(cached_value_rows[0], "seq", axis=1, tiled=True),
    )
    running = attend(
        running,
        query_block,
        jnp.take(pieces[0], kv_ids, axis=0),
        jnp.take(pieces[1], kv_ids, axis=0),
        jnp.int32(0),
        True,
        limit,
    )
    pieces = (
        lax.all_gather(section_key_rows, "seq", axis=0, tiled=True),
        lax.all_gather(section_value_rows, "seq", axis=0, tiled=True),
    )
    picked_keys = jnp.swapaxes(jnp.take(pieces[0], kv_ids, axis=1), 0, 1)
    picked_values = jnp.swapaxes(jnp.take(pieces[1], kv_ids, axis=1), 0, 1)
    running = attend(running, query_block, picked_keys, picked_values, jnp.int32(0), False, limit)
    row_max, row_total, row_sum = running
    finished = (row_sum / row_total[:, :, None]).astype(jnp.bfloat16)
    finished = jnp.transpose(finished, (1, 0, 2))
    returned = lax.all_to_all(finished, "seq", split_axis=0, concat_axis=1, tiled=True)
    return returned.reshape(1, row_count, heads_here * head_size)


def solution(mesh):
    return jax.shard_map(
        body,
        mesh=mesh,
        in_specs=(
            P("section", "seq", "tensor"),
            P("section", "seq", "tensor"),
            P("section", "seq", "tensor"),
            P("section", "seq", "tensor"),
            P("section", "seq", "tensor"),
            P("section", "seq", "tensor"),
            P("section", "tensor", "seq", None),
            P("section", "tensor", "seq", None),
            P("section"),
        ),
        out_specs=P("section", "seq", "tensor"),
        check_vma=False,
    )
```

profile of v0, /device:TPU:0, one launch (start us, length us, event | category | flops | bytes accessed | tf_op | source)
XLA Modules:
  0.0 120.3 jit_solution(3274771388179172553)
XLA Ops:
  0.0 3.0 %collective-permute-start = (bf16[64,4096]{1,0:T(8,128)(2,1)}, bf16[64,4096]{1,0:T(8,128)(2,1)S(1)}, u32[]{:S(2)}, u32[]{:S(2)}) collective-permute-start(bf16[64,4096]{1,0:T(8,128)(2,1)} %bitcast.60), channel_id=1, source_target_pairs={{16,0},{0,16},{17,1},{1,17},{18,2},{2,18},{19,3},{3,19},{20,4},{4,... | collective-permute-start | bytes 1572872 | tf_op jit(solution)/shard_map/ppermute | solution.py:12
  4.6 2.1 %collective-permute-start.2 = (bf16[64,256]{0,1:T(8,128)(2,1)S(1)}, bf16[64,256]{0,1:T(8,128)(2,1)S(1)}, u32[]{:S(2)}, u32[]{:S(2)}) collective-permute-start(bf16[64,256]{0,1:T(8,128)(2,1)S(1)} %bitcast.59), channel_id=1, source_target_pairs={{16,0},{0,16},{17,1},{1,17},{18,2},{2,18},{19,3},{3,19},{20,4},{4,... | collective-permute-start | bytes 98312 | tf_op jit(solution)/shard_map/ppermute | solution.py:12
  8.3 2.1 %collective-permute-start.4 = (bf16[64,256]{0,1:T(8,128)(2,1)S(1)}, bf16[64,256]{0,1:T(8,128)(2,1)S(1)}, u32[]{:S(2)}, u32[]{:S(2)}) collective-permute-start(bf16[64,256]{0,1:T(8,128)(2,1)S(1)} %bitcast.58), channel_id=1, source_target_pairs={{16,0},{0,16},{17,1},{1,17},{18,2},{2,18},{19,3},{3,19},{20,4},{4,... | collective-permute-start | bytes 98312 | tf_op jit(solution)/shard_map/ppermute | solution.py:12
  11.1 5.2 %collective-permute-done.1 = bf16[64,128]{1,0:T(8,128)(2,1)S(1)} collective-permute-done((bf16[64,128]{1,0:T(8,128)(2,1)S(1)}, bf16[64,128]{1,0:T(8,128)(2,1)S(1)}, u32[]{:S(2)}, u32[]{:S(2)}) %collective-permute-start.1) | collective-permute-done | bytes 16416 | tf_op jit(solution)/shard_map/ppermute | solution.py:12
  16.3 2.0 %collective-permute-start.5 = (bf16[64,8]{0,1:T(8,128)(2,1)S(1)}, bf16[64,8]{0,1:T(8,128)(2,1)S(1)}, u32[]{:S(2)}, u32[]{:S(2)}) collective-permute-start(bf16[64,8]{0,1:T(8,128)(2,1)S(1)} %convert_bitcast_fusion.1), channel_id=1, source_target_pairs={{16,0},{0,16},{17,1},{1,17},{18,2},{2,18},{19,3},{3,19},{20,4},{4,... | collective-permute-start | bytes 3080 | tf_op jit(solution)/shard_map/ppermute | solution.py:12
  19.2 1.1 copy.36
  20.3 4.9 %all-to-all-start = ((bf16[64,32,128]{2,0,1:T(8,128)(2,1)}), bf16[64,32,128]{2,0,1:T(8,128)(2,1)S(1)}, u32[]{:S(2)}, u32[]{:S(2)}) async-start(bf16[64,32,128]{2,0,1:T(8,128)(2,1)} %copy.36), calls=%async_computation | async-start | bytes 1048576 | tf_op jit(solution)/shard_map/all_to_all | solution.py:121
  25.2 19.9 %all-gather = bf16[1,2,512,128]{3,2,1,0:T(8,128)(2,1)S(1)} all-gather(bf16[1,2,128,128]{3,2,1,0:T(8,128)(2,1)S(1)} %copy-done.5), channel_id=2, replica_groups=mesh['section'=2,'seq'=4,'tensor'=4] {'seq'}, dimensions={2}, use_global_device_ids=true | all-gather | bytes 327680 | tf_op jit(solution)/shard_map/all_gather | solution.py:131
  45.2 13.9 %all-gather.1 = bf16[1,2,512,128]{3,2,1,0:T(8,128)(2,1)S(1)} all-gather(bf16[1,2,128,128]{3,2,1,0:T(8,128)(2,1)S(1)} %copy-done.6), channel_id=3, replica_groups=mesh['section'=2,'seq'=4,'tensor'=4] {'seq'}, dimensions={2}, use_global_device_ids=true | all-gather | bytes 327680 | tf_op jit(solution)/shard_map/all_gather | solution.py:132
  59.8 1.7 %gather_fusion.1 = bf16[8,512,128]{2,1,0:T(8,128)(2,1)} fusion(bf16[2,512,128]{2,1,0:T(8,128)(2,1)S(1)} %bitcast.50, s32[1024]{0:T(1024)S(1)} %pad_clamp_fusion), kind=kCustom, calls=%fused_computation.2.clone | custom fusion | bytes 2097184 | tf_op jit(solution)/shard_map/jit(_take)/gather | solution.py:138
  62.2 1.1 broadcast_in_dim.78
  63.4 13.6 %all_gather.14 = bf16[256,2,128]{2,0,1:T(8,128)(2,1)S(1)} all-gather(bf16[64,2,128]{2,0,1:T(8,128)(2,1)S(1)} %copy.41), channel_id=1, replica_groups=mesh['section'=2,'seq'=4,'tensor'=4] {'seq'}, dimensions={0}, use_global_device_ids=true | all-gather | bytes 163840 | tf_op jit(solution)/shard_map/all_gather | solution.py:144
  77.1 1.4 %gather_fusion.2 = bf16[8,256,128]{2,1,0:T(8,128)(2,1)} fusion(bf16[256,2,128]{2,0,1:T(8,128)(2,1)S(1)} %all_gather.14, s32[1024]{0:T(1024)S(1)} %pad_clamp_fusion), kind=kCustom, calls=%fused_computation.1.clone | custom fusion | bytes 1048608 | tf_op jit(solution)/shard_map/jit(_take)/gather | solution.py:147
  78.6 13.3 %all_gather.15 = bf16[256,2,128]{2,0,1:T(8,128)(2,1)S(1)} all-gather(bf16[64,2,128]{2,0,1:T(8,128)(2,1)S(1)} %copy.44), channel_id=1, replica_groups=mesh['section'=2,'seq'=4,'tensor'=4] {'seq'}, dimensions={0}, use_global_device_ids=true | all-gather | bytes 163840 | tf_op jit(solution)/shard_map/all_gather | solution.py:145
  92.0 1.4 %gather_fusion.3 = bf16[8,256,128]{2,1,0:T(8,128)(2,1)} fusion(bf16[256,2,128]{2,0,1:T(8,128)(2,1)S(1)} %all_gather.15, s32[1024]{0:T(1024)S(1)} %pad_clamp_fusion), kind=kCustom, calls=%fused_computation.3.clone | custom fusion | bytes 1048608 | tf_op jit(solution)/shard_map/jit(_take)/gather | solution.py:148
  93.4 1.6 %fusion.18 = (f32[8,256]{1,0:T(8,128)S(1)}, f32[8,256,256]{1,2,0:T(8,128)S(1)}) fusion(pred[256,256]{0,1:T(8,128)(4,1)S(1)} %iota_compare_fusion, bf16[8,256,128]{2,1,0:T(8,128)(2,1)S(1)} %bitcast.52, bf16[8,256,128]{2,1,0:T(8,128)(2,1)} %gather_fusion.2, pred[8]{0:T(512)(128)(4,1)S(1)} %compare_and_fusion), kind=kOutput, calls=%fused_computation.27 | convolution fusion | flops 136050688 | bytes 3219464 | tf_op jit(solution)/shard_map/while/body/eval_jaxpr/cond/branch_1_fun/hqd,hkd->hqk/dot_general | solution.py:37
  95.2 5.8 %conditional.1 = ((f32[8,256]{1,0:T(8,128)S(1)}, f32[8,256]{1,0:T(8,128)S(1)}, f32[8,256,128]{2,1,0:T(8,128)})) conditional(s32[]{:T(128)} %convert_element_type.63, (f32[8,256]{1,0:T(8,128)S(1)}, f32[8,256]{1,0:T(8,128)S(1)}, f32[8,256,128]{2,1,0:T(8,128)}) %tuple.27, (s32[]{:T(128)}, s32[512]{0:T(512)S(1)}, ...), branch_computations={%region_0.2_spmd, %region_1.5_spmd.clone} | conditional | flops 552079872 | bytes 32116872 | solution.py:77
  95.8 0.9 fusion
  96.7 1.3 %fusion.2 = f32[8,256]{1,0:T(8,128)S(1)} fusion(f32[8,256,512]{2,1,0:T(8,128)S(1)} %get-tuple-element.183, f32[8,256]{1,0:T(8,128)S(1)} %max.10, pred[512]{0:T(512)(128)(4,1)S(1)} %broadcast_compare_fusion), kind=kLoop, calls=%fused_computation.8 | loop fusion | flops 5240832 | bytes 4211200 | tf_op jit(solution)/shard_map/while/body/eval_jaxpr/cond/branch_1_fun/reduce_sum | solution.py:58
  98.3 1.7 %fusion.6 = f32[8,256,128]{2,1,0:T(8,128)S(1)} fusion(f32[8,256,512]{2,1,0:T(8,128)S(1)} %get-tuple-element.183, f32[8,256]{1,0:T(8,128)S(1)} %max.10, pred[512]{0:T(512)(128)(4,1)S(1)} %broadcast_compare_fusion, bf16[8,512,128]{2,1,0:T(8,128)(2,1)S(1)} %copy-done, bf16[8,512,128]{2,1,0:T(8,128)(2,1)S(1)} %get-tuple-element.164, ...), kind=kOutput, calls=%fused_computation.11 | convolution fusion | flops 274726912 | bytes 8405512 | tf_op jit(solution)/shard_map/while/body/eval_jaxpr/cond/branch_1_fun/hqk,hkd->hqd/dot_general | solution.py:59
  100.0 1.0 copy-done.2
  102.3 1.4 %fusion.23 = bf16[256,8,128]{2,0,1:T(8,128)(2,1)S(1)} fusion(f32[8,256,256]{1,2,0:T(8,128)S(1)} %get-tuple-element.185, f32[8,256]{1,0:T(8,128)S(1)} %max.9, f32[8,256,128]{2,1,0:T(8,128)S(1)} %copy-done.3, pred[256,256]{0,1:T(8,128)(4,1)S(1)} %iota_compare_fusion, bf16[8,256,128]{2,1,0:T(8,128)(2,1)S(1)} %copy-done.4, ...), kind=kOutput, calls=%fused_computation.33 | convolution fusion | flops 138149888 | bytes 4284424 | tf_op jit(solution)/shard_map/while/body/eval_jaxpr/cond/branch_1_fun/hqk,hkd->hqd/dot_general | solution.py:59
  104.1 15.0 %all_to_all.33 = bf16[256,8,128]{2,1,0:T(8,128)(2,1)S(1)} all-to-all(bf16[256,8,128]{2,1,0:T(8,128)(2,1)S(1)} %copy.46), channel_id=1, replica_groups=mesh['section'=2,'seq'=4,'tensor'=4] {'seq'}, dimensions={0} | all-to-all | bytes 1048576 | tf_op jit(solution)/shard_map/all_to_all | solution.py:153
  119.3 1.0 reshape.69
  (55 shorter events, 8.6 us)
Async XLA Ops:
  0.0 18.4 %collective-permute-start = (bf16[64,4096]{1,0:T(8,128)(2,1)}, bf16[64,4096]{1,0:T(8,128)(2,1)S(1)}, u32[]{:S(2)}, u32[]{:S(2)}) collective-permute-start(bf16[64,4096]{1,0:T(8,128)(2,1)} %bitcast.60), channel_id=1, source_target_pairs={{16,0},{0,16},{17,1},{1,17},{18,2},{2,18},{19,3},{3,19},{20,4},{4,... | collective-permute-start | bytes 1572872 | tf_op jit(solution)/shard_map/ppermute | solution.py:12
  3.7 12.6 %collective-permute-start.1 = (bf16[64,128]{1,0:T(8,128)(2,1)S(1)}, bf16[64,128]{1,0:T(8,128)(2,1)S(1)}, u32[]{:S(2)}, u32[]{:S(2)}) collective-permute-start(bf16[64,128]{1,0:T(8,128)(2,1)S(1)} %convert_bitcast_fusion), channel_id=1, source_target_pairs={{16,0},{0,16},{17,1},{1,17},{18,2},{2,18},{19,3},{3,19},{20,4},{4,... | collective-permute-start | bytes 49160 | tf_op jit(solution)/shard_map/ppermute | solution.py:12
  4.6 58.7 %collective-permute-start.2 = (bf16[64,256]{0,1:T(8,128)(2,1)S(1)}, bf16[64,256]{0,1:T(8,128)(2,1)S(1)}, u32[]{:S(2)}, u32[]{:S(2)}) collective-permute-start(bf16[64,256]{0,1:T(8,128)(2,1)S(1)} %bitcast.59), channel_id=1, source_target_pairs={{16,0},{0,16},{17,1},{1,17},{18,2},{2,18},{19,3},{3,19},{20,4},{4,... | collective-permute-start | bytes 98312 | tf_op jit(solution)/shard_map/ppermute | solution.py:12
  7.4 55.9 %collective-permute-start.3 = (bf16[64,8]{0,1:T(8,128)(2,1)S(1)}, bf16[64,8]{0,1:T(8,128)(2,1)S(1)}, u32[]{:S(2)}, u32[]{:S(2)}) collective-permute-start(bf16[64,8]{0,1:T(8,128)(2,1)S(1)} %convert_bitcast_fusion.2), channel_id=1, source_target_pairs={{16,0},{0,16},{17,1},{1,17},{18,2},{2,18},{19,3},{3,19},{20,4},{4,... | collective-permute-start | bytes 3080 | tf_op jit(solution)/shard_map/ppermute | solution.py:12
  8.3 70.2 %collective-permute-start.4 = (bf16[64,256]{0,1:T(8,128)(2,1)S(1)}, bf16[64,256]{0,1:T(8,128)(2,1)S(1)}, u32[]{:S(2)}, u32[]{:S(2)}) collective-permute-start(bf16[64,256]{0,1:T(8,128)(2,1)S(1)} %bitcast.58), channel_id=1, source_target_pairs={{16,0},{0,16},{17,1},{1,17},{18,2},{2,18},{19,3},{3,19},{20,4},{4,... | collective-permute-start | bytes 98312 | tf_op jit(solution)/shard_map/ppermute | solution.py:12
  16.3 47.0 %collective-permute-start.5 = (bf16[64,8]{0,1:T(8,128)(2,1)S(1)}, bf16[64,8]{0,1:T(8,128)(2,1)S(1)}, u32[]{:S(2)}, u32[]{:S(2)}) collective-permute-start(bf16[64,8]{0,1:T(8,128)(2,1)S(1)} %convert_bitcast_fusion.1), channel_id=1, source_target_pairs={{16,0},{0,16},{17,1},{1,17},{18,2},{2,18},{19,3},{3,19},{20,4},{4,... | collective-permute-start | bytes 3080 | tf_op jit(solution)/shard_map/ppermute | solution.py:12
  18.9 6.2 %copy-start.5 = (bf16[1,2,128,128]{3,2,1,0:T(8,128)(2,1)S(1)}, bf16[1,2,128,128]{3,2,1,0:T(8,128)(2,1)}, u32[]{:S(2)}) copy-start(bf16[1,2,128,128]{3,2,1,0:T(8,128)(2,1)} %param.21) | copy-start | bytes 196612
  18.9 26.2 %copy-start.6 = (bf16[1,2,128,128]{3,2,1,0:T(8,128)(2,1)S(1)}, bf16[1,2,128,128]{3,2,1,0:T(8,128)(2,1)}, u32[]{:S(2)}) copy-start(bf16[1,2,128,128]{3,2,1,0:T(8,128)(2,1)} %param.22) | copy-start | bytes 196612
  20.3 73.1 %all-to-all-start = ((bf16[64,32,128]{2,0,1:T(8,128)(2,1)}), bf16[64,32,128]{2,0,1:T(8,128)(2,1)S(1)}, u32[]{:S(2)}, u32[]{:S(2)}) async-start(bf16[64,32,128]{2,0,1:T(8,128)(2,1)} %copy.36), calls=%async_computation | async-start | bytes 1048576 | tf_op jit(solution)/shard_map/all_to_all | solution.py:121
  96.7 1.3 %copy-start = (bf16[8,512,128]{2,1,0:T(8,128)(2,1)S(1)}, bf16[8,512,128]{2,1,0:T(8,128)(2,1)}, u32[]{:S(2)}) copy-start(bf16[8,512,128]{2,1,0:T(8,128)(2,1)} %get-tuple-element.165) | copy-start | bytes 3145732 | tf_op jit(solution)/shard_map/while/body/eval_jaxpr/cond
  96.7 1.5 %copy-start.1 = (f32[8,256,128]{2,1,0:T(8,128)S(1)}, f32[8,256,128]{2,1,0:T(8,128)}, u32[]{:S(2)}) copy-start(f32[8,256,128]{2,1,0:T(8,128)} %get-tuple-element.162) | copy-start | bytes 3145732 | tf_op jit(solution)/shard_map/while/body/eval_jaxpr/cond
  100.0 1.0 copy-start.2
  101.0 1.2 %copy-start.3 = (f32[8,256,128]{2,1,0:T(8,128)S(1)}, f32[8,256,128]{2,1,0:T(8,128)}, u32[]{:S(2)}) copy-start(f32[8,256,128]{2,1,0:T(8,128)} %get-tuple-element.147) | copy-start | bytes 3145732
  101.0 1.4 %copy-start.4 = (bf16[8,256,128]{2,1,0:T(8,128)(2,1)S(1)}, bf16[8,256,128]{2,1,0:T(8,128)(2,1)}, u32[]{:S(2)}) copy-start(bf16[8,256,128]{2,1,0:T(8,128)(2,1)} %gather_fusion.3) | copy-start | bytes 1572868
where the time goes:
time: 121 us; the launch traced here: 120 us
  blocking collectives  75.9 us (63%)
  starting transfers between devices  14 us (12%)
  local copies, waits for them, and re-layouts  13.7 us (11%)
  matrix products  5.59 us (5%)
  waiting for transfers between devices  5.23 us (4%)
  other arithmetic  4.94 us (4%)
    all_gather x1, blocking collectives, body(): lax.all_gather(cached_key_rows[0], 'seq', axis=1, tiled=True)  19.9 us
    all_to_all x1, blocking collectives, body(): lax.all_to_all(finished, 'seq', split_axis=0, concat_axis=1, tiled=True)  15 us
    all_gather x1, blocking collectives, body(): lax.all_gather(cached_value_rows[0], 'seq', axis=1, tiled=True)  13.9 us
    all_gather x1, blocking collectives, body(): lax.all_gather(section_key_rows, 'seq', axis=0, tiled=True)  13.6 us
    all_gather x1, blocking collectives, body(): lax.all_gather(section_value_rows, 'seq', axis=0, tiled=True)  13.3 us
    ppermute x6, starting transfers between devices, shifted(): return lax.ppermute(block, axis, route)  9.17 us
    ppermute x6, waiting for transfers between devices, shifted(): return lax.ppermute(block, axis, route)  5.23 us
    all_to_all x1, starting transfers between devices, body(): lax.all_to_all(queries, 'seq', split_axis=1, concat_axis=0, tiled=True)  4.87 us
  transfers between devices with their start and end apart: 7, of which 1 were waited for; matrix products, arithmetic and copies ran while one was open for 10% of the time, Pallas kernels for 0%

commit v1 on v0

v1 whole, which is shorter than its diff:
```python
import functools
import math

import jax
import jax.numpy as jnp
from jax import lax
from jax.experimental import pallas as pl
from jax.experimental.pallas import tpu as pltpu
from jax.sharding import PartitionSpec as P

NEG = -1e30
VMEM = pltpu.MemorySpace.VMEM


def spread(scale, first, width):
    lanes = lax.broadcasted_iota(jnp.int32, scale.shape, 1)
    return jnp.take_along_axis(scale, first + lanes // 32, axis=1)


def pack_kernel(start_ref, km_ref, ks_ref, vm_ref, vs_ref, qs_ref, ck_ref, cv_ref, kv_ref, sc_ref, c_ref, bias_ref, *, count, width):
    kv_heads = ck_ref.shape[1]
    per = width // 32
    rows = km_ref.shape[1]
    pad = jnp.zeros((rows, width - ks_ref.shape[2]), jnp.float32)
    for part, (mant, exponent) in enumerate(((km_ref, ks_ref), (vm_ref, vs_ref))):
        scale = jnp.concatenate([jnp.exp2(exponent[0].astype(jnp.float32)), pad], axis=1)
        for g in range(kv_heads):
            cols = pl.ds(g * width, width)
            value = mant[0, :, cols].astype(jnp.float32) * spread(scale, g * per, width)
            kv_ref[:, pl.ds((part * kv_heads + g) * width, width)] = value.astype(jnp.bfloat16)
    sc_ref[...] = qs_ref[0].astype(jnp.float32).astype(jnp.bfloat16)
    for g in range(kv_heads):
        c_ref[g] = ck_ref[0, g]
        c_ref[kv_heads + g] = cv_ref[0, g]
    here = lax.axis_index("seq")
    held = ck_ref.shape[2]
    shape = (held, width)
    key = lax.broadcasted_iota(jnp.int32, shape, 0)
    for d in range(count):
        source = lax.rem(here - d + count, count)
        bias_ref[pl.ds(d * held, held), :] = jnp.where(source * held + key < start_ref[0], 0.0, NEG).astype(jnp.bfloat16)
    shape = (rows, width)
    key = lax.broadcasted_iota(jnp.int32, shape, 0)
    token = lax.broadcasted_iota(jnp.int32, shape, 1)
    for d in range(count):
        source = lax.rem(here - d + count, count)
        bias_ref[pl.ds(count * held + d * rows, rows), :] = jnp.where(
            source * rows + key <= here * rows + token, 0.0, NEG
        ).astype(jnp.bfloat16)


def attend_kernel(*refs, count, kv_heads, width, group):
    q_ref, sc_ref, bias_ref = refs[:3]
    c_refs = refs[3 : 3 + count]
    b_refs = refs[3 + count : 3 + 2 * count]
    out_ref = refs[3 + 2 * count]
    k_all, v_all, staged, sem = refs[4 + 2 * count :]
    rows = q_ref.shape[0]
    held = c_refs[0].shape[1]
    heads = q_ref.shape[1] // width
    per_kv = heads // kv_heads
    per = width // 32
    factor = math.log2(math.e) / math.sqrt(width)
    for g in range(kv_heads):
        for d in range(count):
            k_all[g, pl.ds(d * held, held), pl.ds(0, width)] = c_refs[d][g]
            v_all[g, pl.ds(d * held, held), :] = c_refs[d][kv_heads + g]
            at = pl.ds(count * held + d * rows, rows)
            k_all[g, at, pl.ds(0, width)] = b_refs[d][:, pl.ds(g * width, width)]
            v_all[g, at, :] = b_refs[d][:, pl.ds((kv_heads + g) * width, width)]
        k_all[g, :, pl.ds(width, width)] = bias_ref[...]
    scale = jnp.exp2(sc_ref[...].astype(jnp.float32))
    mark = jnp.where(
        lax.broadcasted_iota(jnp.int32, (rows, width), 0)
        == lax.broadcasted_iota(jnp.int32, (rows, width), 1),
        1.0,
        0.0,
    ).astype(jnp.bfloat16)
    copies = []
    for step in range(heads // group):
        g = step * group // per_kv
        blocks = []
        for k in range(group):
            head = step * group + k
            value = q_ref[:, pl.ds(head * width, width)].astype(jnp.float32)
            value = (value * spread(scale, head * per, width)).astype(jnp.bfloat16)
            blocks.append(jnp.concatenate([value, mark], axis=1))
        q = jnp.concatenate(blocks, axis=0)
        s = lax.dot_general(q, k_all[g], (((1,), (1,)), ((), ())), preferred_element_type=jnp.float32)
        top = jnp.max(s, axis=1, keepdims=True)
        w = jnp.exp2((s - top) * factor)
        total = jnp.sum(w, axis=1, keepdims=True)
        o = jnp.dot(w.astype(jnp.bfloat16), v_all[g], preferred_element_type=jnp.float32)
        o = (o / total).astype(jnp.bfloat16)
        for k in range(group):
            staged[:, pl.ds((step * group + k) * width, width)] = o[k * rows : (k + 1) * rows]
        cols = pl.ds(step * group * width, group * width)
        copy = pltpu.make_async_copy(staged.at[:, cols], out_ref.at[0, :, cols], sem.at[step])
        copy.start()
        copies.append(copy)
    for copy in copies:
        copy.wait()


def shift(x, axis, distance):
    size = lax.axis_size(axis)
    return lax.ppermute(x, axis, [(i, (i + distance) % size) for i in range(size)])


def vmem():
    return pl.BlockSpec(memory_space=VMEM)


def body(q_mant, q_scale, key_m, key_e, value_m, value_e, cached_k, cached_v, start):
    _, rows, features = q_mant.shape
    _, kv_heads, held, width = cached_k.shape
    count = lax.axis_size("seq")
    heads = features // width
    keys = count * (held + rows)
    bf16 = jnp.bfloat16
    kv, sc, cached, bias = pl.pallas_call(
        functools.partial(pack_kernel, count=count, width=width),
        out_shape=(
            jax.ShapeDtypeStruct((rows, 2 * kv_heads * width), bf16),
            jax.ShapeDtypeStruct((rows, q_scale.shape[2]), bf16),
            jax.ShapeDtypeStruct((2 * kv_heads, held, width), bf16),
            jax.ShapeDtypeStruct((keys, width), bf16),
        ),
        in_specs=[pl.BlockSpec(memory_space=pltpu.SMEM)] + [vmem()] * 7,
        out_specs=(vmem(),) * 4,
        name="pack",
    )(start, key_m, key_e, value_m, value_e, q_scale, cached_k, cached_v)
    kv = shift(kv, "section", 1)
    sc = shift(sc, "section", 1)
    q = shift(q_mant[0], "section", 1)
    if count <= 4:
        c = [cached] + [shift(cached, "seq", d) for d in range(1, count)]
        b = [kv] + [shift(kv, "seq", d) for d in range(1, count)]
    else:
        here = lax.axis_index("seq")
        order = (here - jnp.arange(count)) % count
        c = lax.all_gather(cached, "seq", axis=0)[order]
        b = lax.all_gather(kv, "seq", axis=0)[order]
        c = [c[d] for d in range(count)]
        b = [b[d] for d in range(count)]
    group = 4
    return pl.pallas_call(
        functools.partial(attend_kernel, count=count, kv_heads=kv_heads, width=width, group=group),
        out_shape=jax.ShapeDtypeStruct((1, rows, features), bf16),
        in_specs=[vmem()] * (3 + 2 * count),
        out_specs=pl.BlockSpec(memory_space=pl.ANY),
        scratch_shapes=[
            pltpu.VMEM((kv_heads, keys, 2 * width), bf16),
            pltpu.VMEM((kv_heads, keys, width), bf16),
            pltpu.VMEM((rows, features), bf16),
            pltpu.SemaphoreType.DMA((heads // group,)),
        ],
        name="attend",
    )(q, sc, bias, *c, *b)


def solution(mesh):
    rows = P("section", "seq", "tensor")
    return jax.shard_map(
        body,
        mesh=mesh,
        in_specs=(rows,) * 6 + (P("section", "tensor", "seq", None),) * 2 + (P("section"),),
        out_specs=rows,
        check_vma=False,
    )
```

time: 121 us -> 47.2 us (0.39)
  blocking collectives: 75.9 us -> 0 us
  waiting for transfers between devices: 5.23 us -> 24.6 us
  local copies, waits for them, and re-layouts: 13.7 us -> 2.95 us
  Pallas kernels: 0 us -> 7.48 us
  matrix products: 5.59 us -> 0 us
  other arithmetic: 4.94 us -> 0 us
  starting transfers between devices: 14 us -> 11.3 us
    all_gather x4 -> x0, blocking collectives: 60.9 us -> none  [the longest x1 19.9 us: body(): lax.all_gather(cached_key_rows[0], 'seq', axis=1, tiled=True)]
    ppermute x6 -> x9, waiting for transfers between devices: 5.23 us -> 24.6 us  [shift(): lax.ppermute(x, axis, [(i, (i + distance) % size) for i in range(size)])]
    all_to_all x1 -> x0, blocking collectives: 15 us -> none  [body(): lax.all_to_all(finished, 'seq', split_axis=0, concat_axis=1, tiled=True)]
    pallas_call x0 -> x2, Pallas kernels: none -> 7.48 us  [the longest x1 5.71 us: body(): pl.pallas_call(functools.partial(attend_kernel, count=count, kv_heads=kv_...]
    dot_general x4 -> x0, matrix products: 5.59 us -> none  [the longest x2 3.13 us: update(): jnp.einsum('hqk,hkd->hqd', weights.astype(jnp.bfloat16), section_value_ro...]
    gather x4 -> x0, local copies, waits for them, and re-layouts: 5.23 us -> none  [the longest x1 1.66 us: body(): jnp.take(pieces[1], kv_ids, axis=0)]
    all_to_all x1 -> x0, starting transfers between devices: 4.87 us -> none  [body(): lax.all_to_all(queries, 'seq', split_axis=1, concat_axis=0, tiled=True)]
    convert_element_type x6 -> x0, other arithmetic: 2.38 us -> none  [the longest x1 0.76 us: body(): q_scale[0].astype(jnp.bfloat16)]
  transfers between devices with their start and end apart: 7 -> 9, of which waited for: 1 -> 4; matrix products, arithmetic and copies ran while one was open for 10% -> 4% of each run, Pallas kernels for 0% -> 4%
where the time goes in v1:
time: 47.2 us; the launch traced here: 47 us
  waiting for transfers between devices  24.6 us (52%)
  starting transfers between devices  11.3 us (24%)
  Pallas kernels  7.48 us (16%)
  local copies, waits for them, and re-layouts  2.95 us (6%)
  between operations  0.75 us (2%)
    ppermute x9, waiting for transfers between devices, shift(): lax.ppermute(x, axis, [(i, (i + distance) % size) for i in range(size)])  24.6 us
    ppermute x9, starting transfers between devices, shift(): lax.ppermute(x, axis, [(i, (i + distance) % size) for i in range(size)])  11.3 us
    pallas_call x1, Pallas kernels, body(): pl.pallas_call(functools.partial(attend_kernel, count=count, kv_heads=kv_...  5.71 us
    unnamed x22, local copies, waits for them, and re-layouts  2.95 us
    pallas_call x1, Pallas kernels, body(): pl.pallas_call(functools.partial(pack_kernel, count=count, width=width),...  1.78 us
  transfers between devices with their start and end apart: 9, of which 4 were waited for; matrix products, arithmetic and copies ran while one was open for 4% of the time, Pallas kernels for 4%

profile of v1, /device:TPU:0, one launch (start us, length us, event | category | flops | bytes accessed | tf_op | source)
XLA Modules:
  0.0 47.0 jit_solution(6129637763363970594)
XLA Ops:
  0.0 3.0 %collective-permute-start = (bf16[64,4096]{1,0:T(8,128)(2,1)}, bf16[64,4096]{1,0:T(8,128)(2,1)S(1)}, u32[]{:S(2)}, u32[]{:S(2)}) collective-permute-start(bf16[64,4096]{1,0:T(8,128)(2,1)} %bitcast.1), channel_id=1, source_target_pairs={{0,16},{16,0},{1,17},{17,1},{2,18},{18,2},{3,19},{19,3},{4,20},{20... | collective-permute-start | bytes 1572872 | tf_op jit(solution)/shard_map/ppermute | solution.py:107
  3.6 1.4 %copy.10.ks_ref = s32[1,64,8]{2,1,0:T(8,128)} copy(s32[1,64,8]{1,2,0:T(8,128)} %param.12) | data formatting | bytes 4096 | tf_op args[3]
  5.0 0.7 %copy.11.vs_ref = s32[1,64,8]{2,1,0:T(8,128)} copy(s32[1,64,8]{1,2,0:T(8,128)S(1)} %copy-done.9) | data formatting | bytes 4096 | tf_op args[5]
  5.7 1.8 %pack.1 = (bf16[64,512]{1,0:T(8,128)(2,1)}, bf16[64,128]{1,0:T(8,128)(2,1)}, bf16[4,128,128]{2,1,0:T(8,128)(2,1)}, bf16[768,128]{1,0:T(8,128)(2,1)}) custom-call(s32[1]{0:T(128)S(6)} %copy.12.start_ref, bf16[1,64,256]{2,1,0:T(8,128)(2,1)} %km_ref.1, s32[1,64,8]{2,1,0:T(8,128)} %copy.10.ks_ref, bf16[1,64,256]{2,1,0:T(8,128)(2,1)} %vm_ref.1, ...), custom_call_target="tpu_custom_call" | custom-call | tf_op jit(solution)/shard_map/pack/pallas_call | solution.py:121
  7.5 0.0 collective-permute-start.5
  7.5 9.0 %collective-permute-done.5.refs_7_ = bf16[64,512]{1,0:T(8,128)(2,1)S(1)} collective-permute-done((bf16[64,512]{1,0:T(8,128)(2,1)}, bf16[64,512]{1,0:T(8,128)(2,1)S(1)}, u32[]{:S(2)}, u32[]{:S(2)}) %collective-permute-start.5) | collective-permute-done | bytes 65568 | tf_op jit(solution)/shard_map/ppermute | solution.py:107
  16.5 3.9 %collective-permute-start.8 = (bf16[64,512]{1,0:T(8,128)(2,1)S(1)}, bf16[64,512]{1,0:T(8,128)(2,1)S(1)}, u32[]{:S(2)}, u32[]{:S(2)}) collective-permute-start(bf16[64,512]{1,0:T(8,128)(2,1)S(1)} %collective-permute-done.5.refs_7_), channel_id=1, source_target_pairs={{0,12},{4,0},{8,4},{12,8},{1,13},{5,1},{9,5},{13,9},{2,14},{6,2},{... | collective-permute-start | bytes 196616 | tf_op jit(solution)/shard_map/ppermute | solution.py:107
  20.4 1.5 %collective-permute-start.1 = (bf16[64,128]{1,0:T(8,128)(2,1)}, bf16[64,128]{1,0:T(8,128)(2,1)S(1)}, u32[]{:S(2)}, u32[]{:S(2)}) collective-permute-start(bf16[64,128]{1,0:T(8,128)(2,1)} %get-tuple-element.9), channel_id=1, source_target_pairs={{0,16},{16,0},{1,17},{17,1},{2,18},{18,2},{3,19},{19,3},{4,20},{20... | collective-permute-start | bytes 49160 | tf_op jit(solution)/shard_map/ppermute | solution.py:107
  21.9 0.4 collective-permute-start.4
  22.3 0.0 collective-permute-start.7
  22.3 2.0 %collective-permute-done.1.refs_1_ = bf16[64,128]{1,0:T(8,128)(2,1)S(1)} collective-permute-done((bf16[64,128]{1,0:T(8,128)(2,1)}, bf16[64,128]{1,0:T(8,128)(2,1)S(1)}, u32[]{:S(2)}, u32[]{:S(2)}) %collective-permute-start.1) | collective-permute-done | bytes 16416 | tf_op jit(solution)/shard_map/ppermute | solution.py:107
  24.3 0.9 %collective-permute-start.3 = (bf16[4,128,128]{2,1,0:T(8,128)(2,1)}, bf16[4,128,128]{2,1,0:T(8,128)(2,1)S(1)}, u32[]{:S(2)}, u32[]{:S(2)}) collective-permute-start(bf16[4,128,128]{2,1,0:T(8,128)(2,1)} %get-tuple-element.11.refs_3_), channel_id=1, source_target_pairs={{0,8},{4,12},{8,0},{12,4},{1,9},{5,13},{9,1},{13,5},{2,10},{6,14},... | collective-permute-start | bytes 393224 | tf_op jit(solution)/shard_map/ppermute | solution.py:107
  25.2 0.0 collective-permute-done.8.refs_10_
  25.2 1.6 %collective-permute-start.2 = (bf16[4,128,128]{2,1,0:T(8,128)(2,1)}, bf16[4,128,128]{2,1,0:T(8,128)(2,1)S(1)}, u32[]{:S(2)}, u32[]{:S(2)}) collective-permute-start(bf16[4,128,128]{2,1,0:T(8,128)(2,1)} %get-tuple-element.11.refs_3_), channel_id=1, source_target_pairs={{0,4},{4,8},{8,12},{12,0},{1,5},{5,9},{9,13},{13,1},{2,6},{6,10},{... | collective-permute-start | bytes 393224 | tf_op jit(solution)/shard_map/ppermute | solution.py:107
  26.8 7.5 %collective-permute-done.7.refs_9_ = bf16[64,512]{1,0:T(8,128)(2,1)S(1)} collective-permute-done((bf16[64,512]{1,0:T(8,128)(2,1)S(1)}, bf16[64,512]{1,0:T(8,128)(2,1)S(1)}, u32[]{:S(2)}, u32[]{:S(2)}) %collective-permute-start.7) | collective-permute-done | bytes 65568 | tf_op jit(solution)/shard_map/ppermute | solution.py:107
  34.3 6.1 %collective-permute-done.6.refs_8_ = bf16[64,512]{1,0:T(8,128)(2,1)S(1)} collective-permute-done((bf16[64,512]{1,0:T(8,128)(2,1)S(1)}, bf16[64,512]{1,0:T(8,128)(2,1)S(1)}, u32[]{:S(2)}, u32[]{:S(2)}) %collective-permute-start.6) | collective-permute-done | bytes 65568 | tf_op jit(solution)/shard_map/ppermute | solution.py:107
  40.3 0.0 collective-permute-done.4.refs_6_
  40.4 0.0 collective-permute-done.2.refs_4_
  40.4 0.5 %copy-done.7 = bf16[64,512]{1,0:T(8,128)(2,1)} copy-done((bf16[64,512]{1,0:T(8,128)(2,1)}, bf16[64,512]{1,0:T(8,128)(2,1)S(1)}, u32[]{:S(2)}) %copy-start.7) | copy-done | bytes 65560
  41.0 0.1 copy-done.1
  41.0 0.1 copy-done.2
  41.1 0.1 copy-done.3
  41.1 0.2 copy-done
  41.3 5.7 %attend.1 = bf16[1,64,4096]{2,1,0:T(8,128)(2,1)} custom-call(bf16[64,4096]{1,0:T(8,128)(2,1)} %copy-done, bf16[64,128]{1,0:T(8,128)(2,1)} %copy-done.8, bf16[768,128]{1,0:T(8,128)(2,1)} %get-tuple-element.10.refs_2_, bf16[4,128,128]{2,1,0:T(8,128)(2,1)} %get-tuple-element.11.refs_3_, bf16[4,128,128]{2,1,0:T(8,128)(2,1)} %copy-done.3, ...), custom_call_target="tpu_custom_call" | custom-call | tf_op jit(solution)/shard_map/attend/pallas_call | solution.py:147
  (18 shorter events, 0.0 us)
Async XLA Ops:
  0.0 40.4 %collective-permute-start = (bf16[64,4096]{1,0:T(8,128)(2,1)}, bf16[64,4096]{1,0:T(8,128)(2,1)S(1)}, u32[]{:S(2)}, u32[]{:S(2)}) collective-permute-start(bf16[64,4096]{1,0:T(8,128)(2,1)} %bitcast.1), channel_id=1, source_target_pairs={{0,16},{16,0},{1,17},{17,1},{2,18},{18,2},{3,19},{19,3},{4,20},{20... | collective-permute-start | bytes 1572872 | tf_op jit(solution)/shard_map/ppermute | solution.py:107
  3.6 1.4 %copy-start.9 = (s32[1,64,8]{1,2,0:T(8,128)S(1)}, s32[1,64,8]{1,2,0:T(8,128)}, u32[]{:S(2)}) copy-start(s32[1,64,8]{1,2,0:T(8,128)} %param.14) | copy-start | bytes 6148
  7.5 9.0 %collective-permute-start.5 = (bf16[64,512]{1,0:T(8,128)(2,1)}, bf16[64,512]{1,0:T(8,128)(2,1)S(1)}, u32[]{:S(2)}, u32[]{:S(2)}) collective-permute-start(bf16[64,512]{1,0:T(8,128)(2,1)} %get-tuple-element.12), channel_id=1, source_target_pairs={{0,16},{16,0},{1,17},{17,1},{2,18},{18,2},{3,19},{19,3},{4,20},{20... | collective-permute-start | bytes 196616 | tf_op jit(solution)/shard_map/ppermute | solution.py:107
  16.5 23.9 %copy-start.4 = (bf16[64,512]{1,0:T(8,128)(2,1)}, bf16[64,512]{1,0:T(8,128)(2,1)S(1)}, u32[]{:S(2)}) copy-start(bf16[64,512]{1,0:T(8,128)(2,1)S(1)} %collective-permute-done.5.refs_7_) | copy-start | bytes 196612
  16.5 8.7 %collective-permute-start.8 = (bf16[64,512]{1,0:T(8,128)(2,1)S(1)}, bf16[64,512]{1,0:T(8,128)(2,1)S(1)}, u32[]{:S(2)}, u32[]{:S(2)}) collective-permute-start(bf16[64,512]{1,0:T(8,128)(2,1)S(1)} %collective-permute-done.5.refs_7_), channel_id=1, source_target_pairs={{0,12},{4,0},{8,4},{12,8},{1,13},{5,1},{9,5},{13,9},{2,14},{6,2},{... | collective-permute-start | bytes 196616 | tf_op jit(solution)/shard_map/ppermute | solution.py:107
  20.4 3.9 %collective-permute-start.1 = (bf16[64,128]{1,0:T(8,128)(2,1)}, bf16[64,128]{1,0:T(8,128)(2,1)S(1)}, u32[]{:S(2)}, u32[]{:S(2)}) collective-permute-start(bf16[64,128]{1,0:T(8,128)(2,1)} %get-tuple-element.9), channel_id=1, source_target_pairs={{0,16},{16,0},{1,17},{17,1},{2,18},{18,2},{3,19},{19,3},{4,20},{20... | collective-permute-start | bytes 49160 | tf_op jit(solution)/shard_map/ppermute | solution.py:107
  21.9 18.5 %collective-permute-start.4 = (bf16[4,128,128]{2,1,0:T(8,128)(2,1)}, bf16[4,128,128]{2,1,0:T(8,128)(2,1)S(1)}, u32[]{:S(2)}, u32[]{:S(2)}) collective-permute-start(bf16[4,128,128]{2,1,0:T(8,128)(2,1)} %get-tuple-element.11.refs_3_), channel_id=1, source_target_pairs={{0,12},{4,0},{8,4},{12,8},{1,13},{5,1},{9,5},{13,9},{2,14},{6,2},{... | collective-permute-start | bytes 393224 | tf_op jit(solution)/shard_map/ppermute | solution.py:107
  22.3 12.0 %collective-permute-start.7 = (bf16[64,512]{1,0:T(8,128)(2,1)S(1)}, bf16[64,512]{1,0:T(8,128)(2,1)S(1)}, u32[]{:S(2)}, u32[]{:S(2)}) collective-permute-start(bf16[64,512]{1,0:T(8,128)(2,1)S(1)} %collective-permute-done.5.refs_7_), channel_id=1, source_target_pairs={{0,8},{4,12},{8,0},{12,4},{1,9},{5,13},{9,1},{13,5},{2,10},{6,14},... | collective-permute-start | bytes 196616 | tf_op jit(solution)/shard_map/ppermute | solution.py:107
  24.3 16.1 %copy-start.8 = (bf16[64,128]{1,0:T(8,128)(2,1)}, bf16[64,128]{1,0:T(8,128)(2,1)S(1)}, u32[]{:S(2)}) copy-start(bf16[64,128]{1,0:T(8,128)(2,1)S(1)} %collective-permute-done.1.refs_1_) | copy-start | bytes 49156
  24.3 16.0 %collective-permute-start.3 = (bf16[4,128,128]{2,1,0:T(8,128)(2,1)}, bf16[4,128,128]{2,1,0:T(8,128)(2,1)S(1)}, u32[]{:S(2)}, u32[]{:S(2)}) collective-permute-start(bf16[4,128,128]{2,1,0:T(8,128)(2,1)} %get-tuple-element.11.refs_3_), channel_id=1, source_target_pairs={{0,8},{4,12},{8,0},{12,4},{1,9},{5,13},{9,1},{13,5},{2,10},{6,14},... | collective-permute-start | bytes 393224 | tf_op jit(solution)/shard_map/ppermute | solution.py:107
  25.2 15.2 %copy-start.5 = (bf16[64,512]{1,0:T(8,128)(2,1)}, bf16[64,512]{1,0:T(8,128)(2,1)S(1)}, u32[]{:S(2)}) copy-start(bf16[64,512]{1,0:T(8,128)(2,1)S(1)} %collective-permute-done.8.refs_10_) | copy-start | bytes 196612
  25.2 15.1 %collective-permute-start.2 = (bf16[4,128,128]{2,1,0:T(8,128)(2,1)}, bf16[4,128,128]{2,1,0:T(8,128)(2,1)S(1)}, u32[]{:S(2)}, u32[]{:S(2)}) collective-permute-start(bf16[4,128,128]{2,1,0:T(8,128)(2,1)} %get-tuple-element.11.refs_3_), channel_id=1, source_target_pairs={{0,4},{4,8},{8,12},{12,0},{1,5},{5,9},{9,13},{13,1},{2,6},{6,10},{... | collective-permute-start | bytes 393224 | tf_op jit(solution)/shard_map/ppermute | solution.py:107
  34.3 6.2 %copy-start.6 = (bf16[64,512]{1,0:T(8,128)(2,1)}, bf16[64,512]{1,0:T(8,128)(2,1)S(1)}, u32[]{:S(2)}) copy-start(bf16[64,512]{1,0:T(8,128)(2,1)S(1)} %collective-permute-done.7.refs_9_) | copy-start | bytes 196612
  34.3 6.1 %collective-permute-start.6 = (bf16[64,512]{1,0:T(8,128)(2,1)S(1)}, bf16[64,512]{1,0:T(8,128)(2,1)S(1)}, u32[]{:S(2)}, u32[]{:S(2)}) collective-permute-start(bf16[64,512]{1,0:T(8,128)(2,1)S(1)} %collective-permute-done.5.refs_7_), channel_id=1, source_target_pairs={{0,4},{4,8},{8,12},{12,0},{1,5},{5,9},{9,13},{13,1},{2,6},{6,10},{... | collective-permute-start | bytes 196616 | tf_op jit(solution)/shard_map/ppermute | solution.py:107
  40.3 0.6 %copy-start.7 = (bf16[64,512]{1,0:T(8,128)(2,1)}, bf16[64,512]{1,0:T(8,128)(2,1)S(1)}, u32[]{:S(2)}) copy-start(bf16[64,512]{1,0:T(8,128)(2,1)S(1)} %collective-permute-done.6.refs_8_) | copy-start | bytes 196612
  40.3 0.7 %copy-start.1 = (bf16[4,128,128]{2,1,0:T(8,128)(2,1)}, bf16[4,128,128]{2,1,0:T(8,128)(2,1)S(1)}, u32[]{:S(2)}) copy-start(bf16[4,128,128]{2,1,0:T(8,128)(2,1)S(1)} %collective-permute-done.4.refs_6_) | copy-start | bytes 393220
  40.4 0.7 %copy-start.2 = (bf16[4,128,128]{2,1,0:T(8,128)(2,1)}, bf16[4,128,128]{2,1,0:T(8,128)(2,1)S(1)}, u32[]{:S(2)}) copy-start(bf16[4,128,128]{2,1,0:T(8,128)(2,1)S(1)} %collective-permute-done.3.refs_5_) | copy-start | bytes 393220
  40.4 0.8 %copy-start.3 = (bf16[4,128,128]{2,1,0:T(8,128)(2,1)}, bf16[4,128,128]{2,1,0:T(8,128)(2,1)S(1)}, u32[]{:S(2)}) copy-start(bf16[4,128,128]{2,1,0:T(8,128)(2,1)S(1)} %collective-permute-done.2.refs_4_) | copy-start | bytes 393220
  40.4 0.9 %copy-start = (bf16[64,4096]{1,0:T(8,128)(2,1)}, bf16[64,4096]{1,0:T(8,128)(2,1)S(1)}, u32[]{:S(2)}) copy-start(bf16[64,4096]{1,0:T(8,128)(2,1)S(1)} %collective-permute-done.refs_0_) | copy-start | bytes 1572868

commit v2 on v1

v2 whole, which is shorter than its diff:
```python
import functools
import math

import jax
import jax.numpy as jnp
from jax import lax
from jax.experimental import pallas as pl
from jax.experimental.pallas import tpu as pltpu
from jax.sharding import PartitionSpec as P


NEG = -1e30
VMEM = pl.BlockSpec(memory_space=pltpu.MemorySpace.VMEM)
HBM = pl.BlockSpec(memory_space=pltpu.MemorySpace.HBM)
BLOCK = 32
bf16, f32 = jnp.bfloat16, jnp.float32


def spread(scale, first):
    lanes = lax.broadcasted_iota(jnp.int32, scale.shape, 1)
    return jnp.take_along_axis(scale, first + lanes // BLOCK, axis=1)


def decoded(mantissa, scale, first):
    return (mantissa.astype(f32) * spread(scale, first)).astype(bf16)


def first_kernel(qs, km, ks, vm, vs, ck, cv, kv_ref, c_ref, qsb, kmb, ksb, vmb, vsb, sem, *, width):
    _, kv_heads, _, _ = ck.shape
    rows = kv_ref.shape[0]
    pairs = (
        (qs.at[0], qsb),
        (ks.at[0], ksb),
        (vs.at[0], vsb),
        (km.at[0], kmb),
        (vm.at[0], vmb),
        (ck.at[0], c_ref.at[pl.ds(0, kv_heads)]),
        (cv.at[0], c_ref.at[pl.ds(kv_heads, kv_heads)]),
    )
    copies = [pltpu.make_async_copy(a, b, sem.at[i]) for i, (a, b) in enumerate(pairs)]
    for copy in copies:
        copy.start()
    for copy in copies[:5]:
        copy.wait()
    per = width // BLOCK
    pad = jnp.zeros((width - ksb.shape[0], rows), f32)
    for part, (mant, exponent) in enumerate(((kmb, ksb), (vmb, vsb))):
        scale = jnp.concatenate([jnp.exp2(exponent[...].astype(f32)), pad], axis=0).T
        for g in range(kv_heads):
            kv_ref[:, pl.ds((part * kv_heads + g) * width, width)] = decoded(mant[:, pl.ds(g * width, width)], scale, g * per)
    kv_ref[:, pl.ds(2 * kv_heads * width, qsb.shape[1])] = qsb[...].astype(f32).astype(bf16)
    for copy in copies[5:]:
        copy.wait()


def bias_kernel(start, bias_ref, at, sem, *, count, held, rows, source):
    width = bias_ref.shape[1]
    copy = pltpu.make_async_copy(start, at, sem)
    copy.start()
    here = lax.axis_index("seq")
    key = lax.broadcasted_iota(jnp.int32, (rows, width), 0)
    token = lax.broadcasted_iota(jnp.int32, (rows, width), 1)
    for d in range(count):
        bias_ref[pl.ds(count * held + d * rows, rows), :] = jnp.where(
            source(here, d) * rows + key <= here * rows + token, 0.0, NEG
        ).astype(bf16)
    copy.wait()
    key = lax.broadcasted_iota(jnp.int32, (held, width), 0)
    for d in range(count):
        bias_ref[pl.ds(d * held, held), :] = jnp.where(source(here, d) * held + key < at[0], 0.0, NEG).astype(bf16)


def attend_kernel(*refs, cs, bs, pick, kv_heads, width, group):
    q_ref, sc_ref, bias_ref = refs[:3]
    c_refs = refs[3 : 3 + cs]
    b_refs = refs[3 + cs : 3 + cs + bs]
    out_ref, k_all, v_all, staged, sem = refs[3 + cs + bs :]
    rows = q_ref.shape[0]
    held = c_refs[0].shape[-2]
    heads = out_ref.shape[2] // width
    per_kv = heads // kv_heads
    factor = math.log2(math.e) / math.sqrt(width)
    c_keys, c_values, blocks_kv = pick(c_refs, b_refs)
    count = len(c_keys)
    for g in range(kv_heads):
        for d in range(count):
            k_all[g, pl.ds(d * held, held), pl.ds(0, width)] = c_keys[d](g)
            v_all[g, pl.ds(d * held, held), :] = c_values[d](g)
            at = pl.ds(count * held + d * rows, rows)
            k_all[g, at, pl.ds(0, width)] = blocks_kv[d][:, pl.ds(g * width, width)]
            v_all[g, at, :] = blocks_kv[d][:, pl.ds((kv_heads + g) * width, width)]
        k_all[g, :, pl.ds(width, width)] = bias_ref[...]
    mark = jnp.where(
        lax.broadcasted_iota(jnp.int32, (rows, width), 0) == lax.broadcasted_iota(jnp.int32, (rows, width), 1),
        1.0,
        0.0,
    ).astype(bf16)
    scale = jnp.exp2(sc_ref[...].astype(f32))
    per = width // BLOCK
    copies = []

    def scores(step):
        g = step * group // per_kv
        blocks = []
        for k in range(group):
            head = step * group + k
            value = decoded(q_ref[:, pl.ds(head * width, width)], scale, head * per)
            blocks.append(jnp.concatenate([value, mark], axis=1))
        return lax.dot_general(jnp.concatenate(blocks, axis=0), k_all[g], (((1,), (1,)), ((), ())), preferred_element_type=f32)

    steps = heads // group
    s = scores(0)
    for step in range(steps):
        g = step * group // per_kv
        later = scores(step + 1) if step + 1 < steps else None
        top = jnp.max(s, axis=1, keepdims=True)
        w = jnp.exp2((s - top) * factor)
        total = jnp.sum(w, axis=1, keepdims=True)
        o = jnp.dot(w.astype(bf16), v_all[g], preferred_element_type=f32)
        o = (o / total).astype(bf16)
        s = later
        for k in range(group):
            staged[:, pl.ds((step * group + k) * width, width)] = o[k * rows : (k + 1) * rows]
        cols = pl.ds(step * group * width, group * width)
        copy = pltpu.make_async_copy(staged.at[:, cols], out_ref.at[0, :, cols], sem.at[step])
        copy.start()
        copies.append(copy)
    for copy in copies:
        copy.wait()


def natural(here, d):
    return jnp.int32(d)


def mirrored(here, d):
    return lax.bitwise_xor(here, d)


NEAR = [(0, 1), (1, 0), (2, 3), (3, 2)]
FAR = [(0, 2), (2, 0), (1, 3), (3, 1)]


def pick_natural(c_refs, b_refs):
    c, b = c_refs[0], b_refs[0]
    count = c.shape[0]
    kv_heads = c.shape[1] // 2
    keys = [lambda g, d=d: c[d, g] for d in range(count)]
    values = [lambda g, d=d: c[d, kv_heads + g] for d in range(count)]
    return keys, values, [b.at[d] for d in range(count)]


def pick_mirrored(c_refs, b_refs):
    kv_heads = c_refs[0].shape[0] // 2
    keys = [lambda g, c=c: c[g] for c in c_refs]
    values = [lambda g, c=c: c[kv_heads + g] for c in c_refs]
    return keys, values, b_refs


def body(q_mant, q_scale, key_m, key_e, value_m, value_e, cached_k, cached_v, start):
    _, rows, features = q_mant.shape
    _, kv_heads, held, width = cached_k.shape
    count = lax.axis_size("seq")
    sections = lax.axis_size("section")
    heads = features // width
    keys = count * (held + rows)
    mirror = count == len(NEAR)
    kv, cached = pl.pallas_call(
        functools.partial(first_kernel, width=width),
        out_shape=(
            jax.ShapeDtypeStruct((rows, 2 * kv_heads * width + q_scale.shape[2]), bf16),
            jax.ShapeDtypeStruct((2 * kv_heads, held, width), bf16),
        ),
        in_specs=[HBM] * 7,
        out_specs=(VMEM,) * 2,
        scratch_shapes=[
            pltpu.VMEM(q_scale.shape[1:], jnp.int32),
            pltpu.VMEM(key_m.shape[1:], bf16),
            pltpu.VMEM((key_e.shape[2], rows), jnp.int32),
            pltpu.VMEM(value_m.shape[1:], bf16),
            pltpu.VMEM((value_e.shape[2], rows), jnp.int32),
            pltpu.SemaphoreType.DMA((7,)),
        ],
        compiler_params=pltpu.CompilerParams(vmem_limit_bytes=60 << 20),
        name="first",
    )(q_scale, key_m, jnp.swapaxes(key_e, 1, 2), value_m, jnp.swapaxes(value_e, 1, 2), cached_k, cached_v)
    bias = pl.pallas_call(
        functools.partial(bias_kernel, count=count, held=held, rows=rows, source=mirrored if mirror else natural),
        out_shape=jax.ShapeDtypeStruct((keys, width), bf16),
        in_specs=[HBM],
        out_specs=VMEM,
        scratch_shapes=[pltpu.SMEM((1,), jnp.int32), pltpu.SemaphoreType.DMA],
        compiler_params=pltpu.CompilerParams(vmem_limit_bytes=8 << 20),
        name="bias",
    )(start)
    relay = [(i, (i + 1) % sections) for i in range(sections)]
    kv = lax.ppermute(kv, "section", relay)
    kv, scale = kv[:, : 2 * kv_heads * width], kv[:, 2 * kv_heads * width :]
    q = lax.ppermute(q_mant[0], "section", relay)
    if mirror:
        near = lax.ppermute(cached, "seq", NEAR)
        far = lax.ppermute(cached, "seq", FAR)
        c = [cached, near, far, lax.ppermute(far, "seq", NEAR)]
        far = lax.ppermute(kv, "seq", FAR)
        near = lax.ppermute(kv, "seq", NEAR)
        b = [kv, near, far, lax.ppermute(far, "seq", NEAR)]
    else:
        c = [lax.all_gather(cached, "seq", axis=0)]
        b = [lax.all_gather(kv, "seq", axis=0)]
    group = 4
    limit = (8 << 20) + keys * width * kv_heads * 8 + keys * group * rows * 12 + 4 * rows * features
    return pl.pallas_call(
        functools.partial(
            attend_kernel,
            cs=len(c),
            bs=len(b),
            pick=pick_mirrored if mirror else pick_natural,
            kv_heads=kv_heads,
            width=width,
            group=group,
        ),
        out_shape=jax.ShapeDtypeStruct((1, rows, features), bf16),
        in_specs=[VMEM] * (3 + len(c) + len(b)),
        out_specs=pl.BlockSpec(memory_space=pl.ANY),
        scratch_shapes=[
            pltpu.VMEM((kv_heads, keys, 2 * width), bf16),
            pltpu.VMEM((kv_heads, keys, width), bf16),
            pltpu.VMEM((rows, features), bf16),
            pltpu.SemaphoreType.DMA((heads // group,)),
        ],
        compiler_params=pltpu.CompilerParams(vmem_limit_bytes=limit),
        name="attend",
    )(q, scale, bias, *c, *b)


def solution(mesh):
    rows = P("section", "seq", "tensor")

    return jax.shard_map(
        body,
        mesh=mesh,
        in_specs=(rows,) * 6 + (P("section", "tensor", "seq", None),) * 2 + (P("section"),),
        out_specs=rows,
        check_vma=False,
    )
```

time: 47.2 us -> 30.9 us (0.65)
  waiting for transfers between devices: 24.6 us -> 9.3 us
  starting transfers between devices: 11.3 us -> 15 us
  local copies, waits for them, and re-layouts: 2.95 us -> 0.01 us
  Pallas kernels: 7.48 us -> 5.68 us
    ppermute x9 -> x8, waiting for transfers between devices: 24.6 us -> 9.3 us  [the longest x1 7.35 us: body(): kv = lax.ppermute(kv, 'section', relay)]
    ppermute x9 -> x8, starting transfers between devices: 11.3 us -> 15 us  [the longest x1 2.97 us: body(): q = lax.ppermute(q_mant[0], 'section', relay)]
    unnamed x22 -> x2, local copies, waits for them, and re-layouts: 2.95 us -> 0.01 us
    pallas_call x2 -> x3, Pallas kernels: 7.48 us -> 5.68 us  [the longest x1 3.32 us: body(): pl.pallas_call(functools.partial(attend_kernel, cs=len(c), bs=len(b), pic...]
  transfers between devices with their start and end apart: 9 -> 8, of which waited for: 4 -> 4; matrix products, arithmetic and copies ran while one was open for 4% -> 0% of each run, Pallas kernels for 4% -> 8%
where the time goes in v2:
time: 30.9 us; the launch traced here: 30.7 us
  starting transfers between devices  15 us (49%)
  waiting for transfers between devices  9.3 us (30%)
  Pallas kernels  5.68 us (18%)
  between operations  0.7 us (2%)
    ppermute x1, waiting for transfers between devices, body(): kv = lax.ppermute(kv, 'section', relay)  7.35 us
    pallas_call x1, Pallas kernels, body(): pl.pallas_call(functools.partial(attend_kernel, cs=len(c), bs=len(b), pic...  3.32 us
    ppermute x1, starting transfers between devices, body(): q = lax.ppermute(q_mant[0], 'section', relay)  2.97 us
    ppermute x1, starting transfers between devices, body(): far = lax.ppermute(kv, 'seq', FAR)  2.91 us
    ppermute x1, starting transfers between devices, body(): far = lax.ppermute(cached, 'seq', FAR)  2.65 us
    ppermute x1, starting transfers between devices, body(): b = [kv, near, far, lax.ppermute(far, 'seq', NEAR)]  2.37 us
    pallas_call x1, Pallas kernels, body(): pl.pallas_call(functools.partial(first_kernel, width=width), out_shape=(j...  1.77 us
    ppermute x1, starting transfers between devices, body(): c = [cached, near, far, lax.ppermute(far, 'seq', NEAR)]  1.58 us
  transfers between devices with their start and end apart: 8, of which 4 were waited for; matrix products, arithmetic and copies ran while one was open for 0% of the time, Pallas kernels for 8%

profile of v2, /device:TPU:0, one launch (start us, length us, event | category | flops | bytes accessed | tf_op | source)
XLA Modules:
  0.0 30.7 jit_solution(8280406482984386818)
XLA Ops:
  0.0 3.0 %collective-permute-start = (bf16[64,4096]{1,0:T(8,128)(2,1)}, bf16[64,4096]{1,0:T(8,128)(2,1)S(1)}, u32[]{:S(2)}, u32[]{:S(2)}) collective-permute-start(bf16[64,4096]{1,0:T(8,128)(2,1)} %bitcast.5), channel_id=1, source_target_pairs={{0,16},{16,0},{1,17},{17,1},{2,18},{18,2},{3,19},{19,3},{4,20},{20... | collective-permute-start | bytes 1572872 | tf_op jit(solution)/shard_map/ppermute | solution.py:199
  3.0 1.8 %first.1 = (bf16[64,640]{1,0:T(8,128)(2,1)}, bf16[4,128,128]{2,1,0:T(8,128)(2,1)}) custom-call(s32[1,64,128]{2,1,0:T(8,128)} %qs.1, bf16[1,64,256]{2,1,0:T(8,128)(2,1)} %km.1, s32[1,8,64]{2,1,0:T(8,128)} %bitcast.3, bf16[1,64,256]{2,1,0:T(8,128)(2,1)} %vm.1, s32[1,8,64]{2,1,0:T(8,128)} %bitcast.4, bf16[1,2,128,128]{3,2,1,0:T(8,128)(2,1)} %ck.1, ...), custom_call_target="tpu_custom_call" | custom-call | tf_op jit(solution)/shard_map/first/pallas_call | solution.py:168
  4.7 2.7 %collective-permute-start.3 = (bf16[4,128,128]{2,1,0:T(8,128)(2,1)}, bf16[4,128,128]{2,1,0:T(8,128)(2,1)S(1)}, u32[]{:S(2)}, u32[]{:S(2)}) collective-permute-start(bf16[4,128,128]{2,1,0:T(8,128)(2,1)} %get-tuple-element.8.refs_3_), channel_id=1, source_target_pairs={{0,8},{8,0},{4,12},{12,4},{1,9},{9,1},{5,13},{13,5},{2,10},{10,2},... | collective-permute-start | bytes 393224 | tf_op jit(solution)/shard_map/ppermute | solution.py:202
  7.4 0.5 %collective-permute-start.1 = (bf16[64,640]{1,0:T(8,128)(2,1)}, bf16[64,640]{1,0:T(8,128)(2,1)S(1)}, u32[]{:S(2)}, u32[]{:S(2)}) collective-permute-start(bf16[64,640]{1,0:T(8,128)(2,1)} %get-tuple-element.7), channel_id=1, source_target_pairs={{0,16},{16,0},{1,17},{17,1},{2,18},{18,2},{3,19},{19,3},{4,20},{20... | collective-permute-start | bytes 245768 | tf_op jit(solution)/shard_map/ppermute | solution.py:197
  7.9 1.6 %collective-permute-start.2 = (bf16[4,128,128]{2,1,0:T(8,128)(2,1)}, bf16[4,128,128]{2,1,0:T(8,128)(2,1)S(1)}, u32[]{:S(2)}, u32[]{:S(2)}) collective-permute-start(bf16[4,128,128]{2,1,0:T(8,128)(2,1)} %get-tuple-element.8.refs_3_), channel_id=1, source_target_pairs={{0,4},{4,0},{8,12},{12,8},{1,5},{5,1},{9,13},{13,9},{2,6},{6,2},{1... | collective-permute-start | bytes 393224 | tf_op jit(solution)/shard_map/ppermute | solution.py:201
  9.5 7.3 %collective-permute-done.1 = bf16[64,640]{1,0:T(8,128)(2,1)S(1)} collective-permute-done((bf16[64,640]{1,0:T(8,128)(2,1)}, bf16[64,640]{1,0:T(8,128)(2,1)S(1)}, u32[]{:S(2)}, u32[]{:S(2)}) %collective-permute-start.1) | collective-permute-done | bytes 81952 | tf_op jit(solution)/shard_map/ppermute | solution.py:197
  16.9 0.0 copy-start
  16.9 2.9 %collective-permute-start.6 = (bf16[64,512]{1,0:T(8,128)(2,1)S(1)}, bf16[64,512]{1,0:T(8,128)(2,1)S(1)}, u32[]{:S(2)}, u32[]{:S(2)}) collective-permute-start(bf16[64,512]{1,0:T(8,128)(2,1)S(1)} %slice.9.refs_7_), channel_id=1, source_target_pairs={{0,8},{8,0},{4,12},{12,4},{1,9},{9,1},{5,13},{13,5},{2,10},{10,2},... | collective-permute-start | bytes 196616 | tf_op jit(solution)/shard_map/ppermute | solution.py:204
  19.8 0.0 collective-permute-done.3.refs_5_
  19.8 1.6 %collective-permute-start.4 = (bf16[4,128,128]{2,1,0:T(8,128)(2,1)S(1)}, bf16[4,128,128]{2,1,0:T(8,128)(2,1)S(1)}, u32[]{:S(2)}, u32[]{:S(2)}) collective-permute-start(bf16[4,128,128]{2,1,0:T(8,128)(2,1)S(1)} %collective-permute-done.3.refs_5_), channel_id=1, source_target_pairs={{0,4},{4,0},{8,12},{12,8},{1,5},{5,1},{9,13},{13,9},{2,6},{6,2},{1... | collective-permute-start | bytes 393224 | tf_op jit(solution)/shard_map/ppermute | solution.py:203
  21.4 0.4 %collective-permute-start.5 = (bf16[64,512]{1,0:T(8,128)(2,1)S(1)}, bf16[64,512]{1,0:T(8,128)(2,1)S(1)}, u32[]{:S(2)}, u32[]{:S(2)}) collective-permute-start(bf16[64,512]{1,0:T(8,128)(2,1)S(1)} %slice.9.refs_7_), channel_id=1, source_target_pairs={{0,4},{4,0},{8,12},{12,8},{1,5},{5,1},{9,13},{13,9},{2,6},{6,2},{1... | collective-permute-start | bytes 196616 | tf_op jit(solution)/shard_map/ppermute | solution.py:205
  21.8 0.5 %collective-permute-done.6.refs_9_ = bf16[64,512]{1,0:T(8,128)(2,1)S(1)} collective-permute-done((bf16[64,512]{1,0:T(8,128)(2,1)S(1)}, bf16[64,512]{1,0:T(8,128)(2,1)S(1)}, u32[]{:S(2)}, u32[]{:S(2)}) %collective-permute-start.6) | collective-permute-done | bytes 65568 | tf_op jit(solution)/shard_map/ppermute | solution.py:204
  22.3 2.4 %collective-permute-start.7 = (bf16[64,512]{1,0:T(8,128)(2,1)S(1)}, bf16[64,512]{1,0:T(8,128)(2,1)S(1)}, u32[]{:S(2)}, u32[]{:S(2)}) collective-permute-start(bf16[64,512]{1,0:T(8,128)(2,1)S(1)} %collective-permute-done.6.refs_9_), channel_id=1, source_target_pairs={{0,4},{4,0},{8,12},{12,8},{1,5},{5,1},{9,13},{13,9},{2,6},{6,2},{1... | collective-permute-start | bytes 196616 | tf_op jit(solution)/shard_map/ppermute | solution.py:206
  25.3 0.6 %bias.1.refs_2_ = bf16[768,128]{1,0:T(8,128)(2,1)S(1)} custom-call(s32[1]{0:T(128)S(6)} %copy.10.start), custom_call_target="tpu_custom_call" | custom-call | tf_op jit(solution)/shard_map/bias/pallas_call | solution.py:187
  25.9 0.0 collective-permute-done.2.refs_4_
  25.9 0.8 %collective-permute-done.5.refs_8_ = bf16[64,512]{1,0:T(8,128)(2,1)S(1)} collective-permute-done((bf16[64,512]{1,0:T(8,128)(2,1)S(1)}, bf16[64,512]{1,0:T(8,128)(2,1)S(1)}, u32[]{:S(2)}, u32[]{:S(2)}) %collective-permute-start.5) | collective-permute-done | bytes 65568 | tf_op jit(solution)/shard_map/ppermute | solution.py:205
  26.7 0.7 %collective-permute-done.7.refs_10_ = bf16[64,512]{1,0:T(8,128)(2,1)S(1)} collective-permute-done((bf16[64,512]{1,0:T(8,128)(2,1)S(1)}, bf16[64,512]{1,0:T(8,128)(2,1)S(1)}, u32[]{:S(2)}, u32[]{:S(2)}) %collective-permute-start.7) | collective-permute-done | bytes 65568 | tf_op jit(solution)/shard_map/ppermute | solution.py:206
  27.4 0.0 collective-permute-done.4.refs_6_
  27.4 0.0 collective-permute-done.refs_0_
  27.4 0.0 copy-done
  27.4 3.3 %attend.1 = bf16[1,64,4096]{2,1,0:T(8,128)(2,1)} custom-call(bf16[64,4096]{1,0:T(8,128)(2,1)S(1)} %collective-permute-done.refs_0_, bf16[64,128]{1,0:T(8,128)(2,1)S(1)} %slice.8.refs_1_, bf16[768,128]{1,0:T(8,128)(2,1)S(1)} %bias.1.refs_2_, bf16[4,128,128]{2,1,0:T(8,128)(2,1)S(1)} %copy-done, bf16[4,128,128]{2,1,0:T(8,128)(2,1)S(1)} %collective-permute-done.2.refs_4_, ...), custom_call_target="tpu_custom_call" | custom-call | tf_op jit(solution)/shard_map/attend/pallas_call | solution.py:212
  (2 shorter events, 0.0 us)
Async XLA Ops:
  0.0 27.4 %collective-permute-start = (bf16[64,4096]{1,0:T(8,128)(2,1)}, bf16[64,4096]{1,0:T(8,128)(2,1)S(1)}, u32[]{:S(2)}, u32[]{:S(2)}) collective-permute-start(bf16[64,4096]{1,0:T(8,128)(2,1)} %bitcast.5), channel_id=1, source_target_pairs={{0,16},{16,0},{1,17},{17,1},{2,18},{18,2},{3,19},{19,3},{4,20},{20... | collective-permute-start | bytes 1572872 | tf_op jit(solution)/shard_map/ppermute | solution.py:199
  4.7 15.0 %collective-permute-start.3 = (bf16[4,128,128]{2,1,0:T(8,128)(2,1)}, bf16[4,128,128]{2,1,0:T(8,128)(2,1)S(1)}, u32[]{:S(2)}, u32[]{:S(2)}) collective-permute-start(bf16[4,128,128]{2,1,0:T(8,128)(2,1)} %get-tuple-element.8.refs_3_), channel_id=1, source_target_pairs={{0,8},{8,0},{4,12},{12,4},{1,9},{9,1},{5,13},{13,5},{2,10},{10,2},... | collective-permute-start | bytes 393224 | tf_op jit(solution)/shard_map/ppermute | solution.py:202
  7.4 9.5 %collective-permute-start.1 = (bf16[64,640]{1,0:T(8,128)(2,1)}, bf16[64,640]{1,0:T(8,128)(2,1)S(1)}, u32[]{:S(2)}, u32[]{:S(2)}) collective-permute-start(bf16[64,640]{1,0:T(8,128)(2,1)} %get-tuple-element.7), channel_id=1, source_target_pairs={{0,16},{16,0},{1,17},{17,1},{2,18},{18,2},{3,19},{19,3},{4,20},{20... | collective-permute-start | bytes 245768 | tf_op jit(solution)/shard_map/ppermute | solution.py:197
  7.9 18.0 %collective-permute-start.2 = (bf16[4,128,128]{2,1,0:T(8,128)(2,1)}, bf16[4,128,128]{2,1,0:T(8,128)(2,1)S(1)}, u32[]{:S(2)}, u32[]{:S(2)}) collective-permute-start(bf16[4,128,128]{2,1,0:T(8,128)(2,1)} %get-tuple-element.8.refs_3_), channel_id=1, source_target_pairs={{0,4},{4,0},{8,12},{12,8},{1,5},{5,1},{9,13},{13,9},{2,6},{6,2},{1... | collective-permute-start | bytes 393224 | tf_op jit(solution)/shard_map/ppermute | solution.py:201
  16.9 10.5 %copy-start = (bf16[4,128,128]{2,1,0:T(8,128)(2,1)S(1)}, bf16[4,128,128]{2,1,0:T(8,128)(2,1)}, u32[]{:S(2)}) copy-start(bf16[4,128,128]{2,1,0:T(8,128)(2,1)} %get-tuple-element.8.refs_3_) | copy-start | bytes 393220
  16.9 5.4 %collective-permute-start.6 = (bf16[64,512]{1,0:T(8,128)(2,1)S(1)}, bf16[64,512]{1,0:T(8,128)(2,1)S(1)}, u32[]{:S(2)}, u32[]{:S(2)}) collective-permute-start(bf16[64,512]{1,0:T(8,128)(2,1)S(1)} %slice.9.refs_7_), channel_id=1, source_target_pairs={{0,8},{8,0},{4,12},{12,4},{1,9},{9,1},{5,13},{13,5},{2,10},{10,2},... | collective-permute-start | bytes 196616 | tf_op jit(solution)/shard_map/ppermute | solution.py:204
  19.8 7.6 %collective-permute-start.4 = (bf16[4,128,128]{2,1,0:T(8,128)(2,1)S(1)}, bf16[4,128,128]{2,1,0:T(8,128)(2,1)S(1)}, u32[]{:S(2)}, u32[]{:S(2)}) collective-permute-start(bf16[4,128,128]{2,1,0:T(8,128)(2,1)S(1)} %collective-permute-done.3.refs_5_), channel_id=1, source_target_pairs={{0,4},{4,0},{8,12},{12,8},{1,5},{5,1},{9,13},{13,9},{2,6},{6,2},{1... | collective-permute-start | bytes 393224 | tf_op jit(solution)/shard_map/ppermute | solution.py:203
  21.4 5.3 %collective-permute-start.5 = (bf16[64,512]{1,0:T(8,128)(2,1)S(1)}, bf16[64,512]{1,0:T(8,128)(2,1)S(1)}, u32[]{:S(2)}, u32[]{:S(2)}) collective-permute-start(bf16[64,512]{1,0:T(8,128)(2,1)S(1)} %slice.9.refs_7_), channel_id=1, source_target_pairs={{0,4},{4,0},{8,12},{12,8},{1,5},{5,1},{9,13},{13,9},{2,6},{6,2},{1... | collective-permute-start | bytes 196616 | tf_op jit(solution)/shard_map/ppermute | solution.py:205
  22.3 5.1 %collective-permute-start.7 = (bf16[64,512]{1,0:T(8,128)(2,1)S(1)}, bf16[64,512]{1,0:T(8,128)(2,1)S(1)}, u32[]{:S(2)}, u32[]{:S(2)}) collective-permute-start(bf16[64,512]{1,0:T(8,128)(2,1)S(1)} %collective-permute-done.6.refs_9_), channel_id=1, source_target_pairs={{0,4},{4,0},{8,12},{12,8},{1,5},{5,1},{9,13},{13,9},{2,6},{6,2},{1... | collective-permute-start | bytes 196616 | tf_op jit(solution)/shard_map/ppermute | solution.py:206

commit v3 on v2

--- a/solution.py
+++ b/solution.py
@@ -129,6 +129,10 @@
         copy.wait()
 
 
+def in_hbm(x):
+    return pltpu.with_memory_space_constraint(x, pltpu.MemorySpace.HBM)
+
+
 def natural(here, d):
     return jnp.int32(d)
 
@@ -181,9 +185,12 @@
             pltpu.VMEM((value_e.shape[2], rows), jnp.int32),
             pltpu.SemaphoreType.DMA((7,)),
         ],
-        compiler_params=pltpu.CompilerParams(vmem_limit_bytes=60 << 20),
+        compiler_params=pltpu.CompilerParams(vmem_limit_bytes=8 << 20),
         name="first",
-    )(q_scale, key_m, jnp.swapaxes(key_e, 1, 2), value_m, jnp.swapaxes(value_e, 1, 2), cached_k, cached_v)
+    )(*(
+        in_hbm(x)
+        for x in (q_scale, key_m, jnp.swapaxes(key_e, 1, 2), value_m, jnp.swapaxes(value_e, 1, 2), cached_k, cached_v)
+    ))
     bias = pl.pallas_call(
         functools.partial(bias_kernel, count=count, held=held, rows=rows, source=mirrored if mirror else natural),
         out_shape=jax.ShapeDtypeStruct((keys, width), bf16),
@@ -236,10 +243,13 @@
 def solution(mesh):
     rows = P("section", "seq", "tensor")
 
-    return jax.shard_map(
+    step = jax.shard_map(
         body,
         mesh=mesh,
         in_specs=(rows,) * 6 + (P("section", "tensor", "seq", None),) * 2 + (P("section"),),
         out_specs=rows,
         check_vma=False,
     )
+    if mesh.shape["seq"] != len(NEAR):
+        return step
+    return step

time: 30.9 us -> 30.8 us (level)
  Pallas kernels: 5.68 us -> 4.99 us
  waiting for transfers between devices: 9.3 us -> 9.98 us
    ppermute x1, waiting for transfers between devices: 7.35 us -> 8.03 us  [body(): kv = lax.ppermute(kv, 'section', relay)]
    pallas_call x1, Pallas kernels: 1.77 us -> 1.08 us  [body(): pl.pallas_call(functools.partial(first_kernel, width=width), out_shape=(j...]
  transfers between devices with their start and end apart: 8 -> 8, of which waited for: 4 -> 4; matrix products, arithmetic and copies ran while one was open for 0% -> 0% of each run, Pallas kernels for 8% -> 5%
where the time goes in v3:
time: 30.8 us; the launch traced here: 30.6 us
  starting transfers between devices  15 us (49%)
  waiting for transfers between devices  9.98 us (32%)
  Pallas kernels  4.99 us (16%)
  between operations  0.69 us (2%)
    ppermute x1, waiting for transfers between devices, body(): kv = lax.ppermute(kv, 'section', relay)  8.03 us
    pallas_call x1, Pallas kernels, body(): pl.pallas_call(functools.partial(attend_kernel, cs=len(c), bs=len(b), pic...  3.31 us
    ppermute x1, starting transfers between devices, body(): q = lax.ppermute(q_mant[0], 'section', relay)  2.97 us
    ppermute x1, starting transfers between devices, body(): far = lax.ppermute(kv, 'seq', FAR)  2.84 us
    ppermute x1, starting transfers between devices, body(): far = lax.ppermute(cached, 'seq', FAR)  2.65 us
    ppermute x1, starting transfers between devices, body(): b = [kv, near, far, lax.ppermute(far, 'seq', NEAR)]  2.37 us
    ppermute x1, starting transfers between devices, body(): c = [cached, near, far, lax.ppermute(far, 'seq', NEAR)]  1.58 us
    ppermute x1, starting transfers between devices, body(): near = lax.ppermute(cached, 'seq', NEAR)  1.58 us
  transfers between devices with their start and end apart: 8, of which 4 were waited for; matrix products, arithmetic and copies ran while one was open for 0% of the time, Pallas kernels for 5%

profile of v3, /device:TPU:0, one launch (start us, length us, event | category | flops | bytes accessed | tf_op | source)
XLA Modules:
  0.0 30.6 jit_solution(1910077966757432413)
XLA Ops:
  0.0 3.0 %collective-permute-start = (bf16[64,4096]{1,0:T(8,128)(2,1)}, bf16[64,4096]{1,0:T(8,128)(2,1)S(1)}, u32[]{:S(2)}, u32[]{:S(2)}) collective-permute-start(bf16[64,4096]{1,0:T(8,128)(2,1)} %bitcast.5), channel_id=1, source_target_pairs={{0,16},{16,0},{1,17},{17,1},{2,18},{18,2},{3,19},{19,3},{4,20},{20... | collective-permute-start | bytes 1572872 | tf_op jit(solution)/shard_map/ppermute | solution.py:206
  3.0 1.1 %first.1 = (bf16[64,640]{1,0:T(8,128)(2,1)S(1)}, bf16[4,128,128]{2,1,0:T(8,128)(2,1)S(1)}) custom-call(s32[1,64,128]{2,1,0:T(8,128)} %qs.1, bf16[1,64,256]{2,1,0:T(8,128)(2,1)} %km.1, s32[1,8,64]{2,1,0:T(8,128)} %bitcast.3, bf16[1,64,256]{2,1,0:T(8,128)(2,1)} %vm.1, s32[1,8,64]{2,1,0:T(8,128)} %bitcast.4, bf16[1,2,128,128]{3,2,1,0:T(8,128)(2,1)} %ck.1, ...), custom_call_target="tpu_custom_call" | custom-call | tf_op jit(solution)/shard_map/first/pallas_call | solution.py:172
  4.1 2.7 %collective-permute-start.3 = (bf16[4,128,128]{2,1,0:T(8,128)(2,1)S(1)}, bf16[4,128,128]{2,1,0:T(8,128)(2,1)S(1)}, u32[]{:S(2)}, u32[]{:S(2)}) collective-permute-start(bf16[4,128,128]{2,1,0:T(8,128)(2,1)S(1)} %get-tuple-element.8.refs_3_), channel_id=1, source_target_pairs={{0,8},{8,0},{4,12},{12,4},{1,9},{9,1},{5,13},{13,5},{2,10},{10,2},... | collective-permute-start | bytes 393224 | tf_op jit(solution)/shard_map/ppermute | solution.py:209
  6.7 0.5 %collective-permute-start.1 = (bf16[64,640]{1,0:T(8,128)(2,1)S(1)}, bf16[64,640]{1,0:T(8,128)(2,1)S(1)}, u32[]{:S(2)}, u32[]{:S(2)}) collective-permute-start(bf16[64,640]{1,0:T(8,128)(2,1)S(1)} %get-tuple-element.7), channel_id=1, source_target_pairs={{0,16},{16,0},{1,17},{17,1},{2,18},{18,2},{3,19},{19,3},{4,20},{20... | collective-permute-start | bytes 245768 | tf_op jit(solution)/shard_map/ppermute | solution.py:204
  7.2 1.6 %collective-permute-start.2 = (bf16[4,128,128]{2,1,0:T(8,128)(2,1)S(1)}, bf16[4,128,128]{2,1,0:T(8,128)(2,1)S(1)}, u32[]{:S(2)}, u32[]{:S(2)}) collective-permute-start(bf16[4,128,128]{2,1,0:T(8,128)(2,1)S(1)} %get-tuple-element.8.refs_3_), channel_id=1, source_target_pairs={{0,4},{4,0},{8,12},{12,8},{1,5},{5,1},{9,13},{13,9},{2,6},{6,2},{1... | collective-permute-start | bytes 393224 | tf_op jit(solution)/shard_map/ppermute | solution.py:208
  8.8 8.0 %collective-permute-done.1 = bf16[64,640]{1,0:T(8,128)(2,1)S(1)} collective-permute-done((bf16[64,640]{1,0:T(8,128)(2,1)S(1)}, bf16[64,640]{1,0:T(8,128)(2,1)S(1)}, u32[]{:S(2)}, u32[]{:S(2)}) %collective-permute-start.1) | collective-permute-done | bytes 81952 | tf_op jit(solution)/shard_map/ppermute | solution.py:204
  16.9 2.8 %collective-permute-start.6 = (bf16[64,512]{1,0:T(8,128)(2,1)S(1)}, bf16[64,512]{1,0:T(8,128)(2,1)S(1)}, u32[]{:S(2)}, u32[]{:S(2)}) collective-permute-start(bf16[64,512]{1,0:T(8,128)(2,1)S(1)} %slice.9.refs_7_), channel_id=1, source_target_pairs={{0,8},{8,0},{4,12},{12,4},{1,9},{9,1},{5,13},{13,5},{2,10},{10,2},... | collective-permute-start | bytes 196616 | tf_op jit(solution)/shard_map/ppermute | solution.py:211
  19.7 0.0 collective-permute-done.3.refs_5_
  19.7 1.6 %collective-permute-start.4 = (bf16[4,128,128]{2,1,0:T(8,128)(2,1)S(1)}, bf16[4,128,128]{2,1,0:T(8,128)(2,1)S(1)}, u32[]{:S(2)}, u32[]{:S(2)}) collective-permute-start(bf16[4,128,128]{2,1,0:T(8,128)(2,1)S(1)} %collective-permute-done.3.refs_5_), channel_id=1, source_target_pairs={{0,4},{4,0},{8,12},{12,8},{1,5},{5,1},{9,13},{13,9},{2,6},{6,2},{1... | collective-permute-start | bytes 393224 | tf_op jit(solution)/shard_map/ppermute | solution.py:210
  21.3 0.4 %collective-permute-start.5 = (bf16[64,512]{1,0:T(8,128)(2,1)S(1)}, bf16[64,512]{1,0:T(8,128)(2,1)S(1)}, u32[]{:S(2)}, u32[]{:S(2)}) collective-permute-start(bf16[64,512]{1,0:T(8,128)(2,1)S(1)} %slice.9.refs_7_), channel_id=1, source_target_pairs={{0,4},{4,0},{8,12},{12,8},{1,5},{5,1},{9,13},{13,9},{2,6},{6,2},{1... | collective-permute-start | bytes 196616 | tf_op jit(solution)/shard_map/ppermute | solution.py:212
  21.7 0.5 %collective-permute-done.6.refs_9_ = bf16[64,512]{1,0:T(8,128)(2,1)S(1)} collective-permute-done((bf16[64,512]{1,0:T(8,128)(2,1)S(1)}, bf16[64,512]{1,0:T(8,128)(2,1)S(1)}, u32[]{:S(2)}, u32[]{:S(2)}) %collective-permute-start.6) | collective-permute-done | bytes 65568 | tf_op jit(solution)/shard_map/ppermute | solution.py:211
  22.2 2.4 %collective-permute-start.7 = (bf16[64,512]{1,0:T(8,128)(2,1)S(1)}, bf16[64,512]{1,0:T(8,128)(2,1)S(1)}, u32[]{:S(2)}, u32[]{:S(2)}) collective-permute-start(bf16[64,512]{1,0:T(8,128)(2,1)S(1)} %collective-permute-done.6.refs_9_), channel_id=1, source_target_pairs={{0,4},{4,0},{8,12},{12,8},{1,5},{5,1},{9,13},{13,9},{2,6},{6,2},{1... | collective-permute-start | bytes 196616 | tf_op jit(solution)/shard_map/ppermute | solution.py:213
  25.2 0.6 %bias.1.refs_2_ = bf16[768,128]{1,0:T(8,128)(2,1)S(1)} custom-call(s32[1]{0:T(128)S(6)} %copy.10.start), custom_call_target="tpu_custom_call" | custom-call | tf_op jit(solution)/shard_map/bias/pallas_call | solution.py:194
  25.8 0.0 collective-permute-done.2.refs_4_
  25.8 0.8 %collective-permute-done.5.refs_8_ = bf16[64,512]{1,0:T(8,128)(2,1)S(1)} collective-permute-done((bf16[64,512]{1,0:T(8,128)(2,1)S(1)}, bf16[64,512]{1,0:T(8,128)(2,1)S(1)}, u32[]{:S(2)}, u32[]{:S(2)}) %collective-permute-start.5) | collective-permute-done | bytes 65568 | tf_op jit(solution)/shard_map/ppermute | solution.py:212
  26.6 0.7 %collective-permute-done.7.refs_10_ = bf16[64,512]{1,0:T(8,128)(2,1)S(1)} collective-permute-done((bf16[64,512]{1,0:T(8,128)(2,1)S(1)}, bf16[64,512]{1,0:T(8,128)(2,1)S(1)}, u32[]{:S(2)}, u32[]{:S(2)}) %collective-permute-start.7) | collective-permute-done | bytes 65568 | tf_op jit(solution)/shard_map/ppermute | solution.py:213
  27.3 0.0 collective-permute-done.4.refs_6_
  27.3 0.0 collective-permute-done.refs_0_
  27.3 3.3 %attend.1 = bf16[1,64,4096]{2,1,0:T(8,128)(2,1)} custom-call(bf16[64,4096]{1,0:T(8,128)(2,1)S(1)} %collective-permute-done.refs_0_, bf16[64,128]{1,0:T(8,128)(2,1)S(1)} %slice.8.refs_1_, bf16[768,128]{1,0:T(8,128)(2,1)S(1)} %bias.1.refs_2_, bf16[4,128,128]{2,1,0:T(8,128)(2,1)S(1)} %get-tuple-element.8.refs_3_, ...), custom_call_target="tpu_custom_call" | custom-call | tf_op jit(solution)/shard_map/attend/pallas_call | solution.py:219
  (2 shorter events, 0.0 us)
Async XLA Ops:
  0.0 27.3 %collective-permute-start = (bf16[64,4096]{1,0:T(8,128)(2,1)}, bf16[64,4096]{1,0:T(8,128)(2,1)S(1)}, u32[]{:S(2)}, u32[]{:S(2)}) collective-permute-start(bf16[64,4096]{1,0:T(8,128)(2,1)} %bitcast.5), channel_id=1, source_target_pairs={{0,16},{16,0},{1,17},{17,1},{2,18},{18,2},{3,19},{19,3},{4,20},{20... | collective-permute-start | bytes 1572872 | tf_op jit(solution)/shard_map/ppermute | solution.py:206
  4.1 15.6 %collective-permute-start.3 = (bf16[4,128,128]{2,1,0:T(8,128)(2,1)S(1)}, bf16[4,128,128]{2,1,0:T(8,128)(2,1)S(1)}, u32[]{:S(2)}, u32[]{:S(2)}) collective-permute-start(bf16[4,128,128]{2,1,0:T(8,128)(2,1)S(1)} %get-tuple-element.8.refs_3_), channel_id=1, source_target_pairs={{0,8},{8,0},{4,12},{12,4},{1,9},{9,1},{5,13},{13,5},{2,10},{10,2},... | collective-permute-start | bytes 393224 | tf_op jit(solution)/shard_map/ppermute | solution.py:209
  6.7 10.1 %collective-permute-start.1 = (bf16[64,640]{1,0:T(8,128)(2,1)S(1)}, bf16[64,640]{1,0:T(8,128)(2,1)S(1)}, u32[]{:S(2)}, u32[]{:S(2)}) collective-permute-start(bf16[64,640]{1,0:T(8,128)(2,1)S(1)} %get-tuple-element.7), channel_id=1, source_target_pairs={{0,16},{16,0},{1,17},{17,1},{2,18},{18,2},{3,19},{19,3},{4,20},{20... | collective-permute-start | bytes 245768 | tf_op jit(solution)/shard_map/ppermute | solution.py:204
  7.2 18.6 %collective-permute-start.2 = (bf16[4,128,128]{2,1,0:T(8,128)(2,1)S(1)}, bf16[4,128,128]{2,1,0:T(8,128)(2,1)S(1)}, u32[]{:S(2)}, u32[]{:S(2)}) collective-permute-start(bf16[4,128,128]{2,1,0:T(8,128)(2,1)S(1)} %get-tuple-element.8.refs_3_), channel_id=1, source_target_pairs={{0,4},{4,0},{8,12},{12,8},{1,5},{5,1},{9,13},{13,9},{2,6},{6,2},{1... | collective-permute-start | bytes 393224 | tf_op jit(solution)/shard_map/ppermute | solution.py:208
  16.9 5.3 %collective-permute-start.6 = (bf16[64,512]{1,0:T(8,128)(2,1)S(1)}, bf16[64,512]{1,0:T(8,128)(2,1)S(1)}, u32[]{:S(2)}, u32[]{:S(2)}) collective-permute-start(bf16[64,512]{1,0:T(8,128)(2,1)S(1)} %slice.9.refs_7_), channel_id=1, source_target_pairs={{0,8},{8,0},{4,12},{12,4},{1,9},{9,1},{5,13},{13,5},{2,10},{10,2},... | collective-permute-start | bytes 196616 | tf_op jit(solution)/shard_map/ppermute | solution.py:211
  19.7 7.6 %collective-permute-start.4 = (bf16[4,128,128]{2,1,0:T(8,128)(2,1)S(1)}, bf16[4,128,128]{2,1,0:T(8,128)(2,1)S(1)}, u32[]{:S(2)}, u32[]{:S(2)}) collective-permute-start(bf16[4,128,128]{2,1,0:T(8,128)(2,1)S(1)} %collective-permute-done.3.refs_5_), channel_id=1, source_target_pairs={{0,4},{4,0},{8,12},{12,8},{1,5},{5,1},{9,13},{13,9},{2,6},{6,2},{1... | collective-permute-start | bytes 393224 | tf_op jit(solution)/shard_map/ppermute | solution.py:210
  21.3 5.3 %collective-permute-start.5 = (bf16[64,512]{1,0:T(8,128)(2,1)S(1)}, bf16[64,512]{1,0:T(8,128)(2,1)S(1)}, u32[]{:S(2)}, u32[]{:S(2)}) collective-permute-start(bf16[64,512]{1,0:T(8,128)(2,1)S(1)} %slice.9.refs_7_), channel_id=1, source_target_pairs={{0,4},{4,0},{8,12},{12,8},{1,5},{5,1},{9,13},{13,9},{2,6},{6,2},{1... | collective-permute-start | bytes 196616 | tf_op jit(solution)/shard_map/ppermute | solution.py:212
  22.2 5.1 %collective-permute-start.7 = (bf16[64,512]{1,0:T(8,128)(2,1)S(1)}, bf16[64,512]{1,0:T(8,128)(2,1)S(1)}, u32[]{:S(2)}, u32[]{:S(2)}) collective-permute-start(bf16[64,512]{1,0:T(8,128)(2,1)S(1)} %collective-permute-done.6.refs_9_), channel_id=1, source_target_pairs={{0,4},{4,0},{8,12},{12,8},{1,5},{5,1},{9,13},{13,9},{2,6},{6,2},{1... | collective-permute-start | bytes 196616 | tf_op jit(solution)/shard_map/ppermute | solution.py:213

commit v4 on v3

v4 whole, which is shorter than its diff:
```python
import functools
import math

import jax
import jax.numpy as jnp
from jax import lax
from jax.experimental import pallas as pl
from jax.experimental.pallas import tpu as pltpu
from jax.sharding import PartitionSpec as P


NEG = -1e30
VMEM = pl.BlockSpec(memory_space=pltpu.MemorySpace.VMEM)
HBM = pl.BlockSpec(memory_space=pltpu.MemorySpace.HBM)
BLOCK = 32
bf16, f32 = jnp.bfloat16, jnp.float32


def spread(scale, first):
    lanes = lax.broadcasted_iota(jnp.int32, scale.shape, 1)
    return jnp.take_along_axis(scale, first + lanes // BLOCK, axis=1)


def decoded(mantissa, scale, first):
    return (mantissa.astype(f32) * spread(scale, first)).astype(bf16)


def first_kernel(*refs, width):
    q, qs, km, ks, vm, vs, ck, cv, kv_ref, c_ref = refs[:10]
    q_refs = refs[10:-6]
    qsb, kmb, ksb, vmb, vsb, sem = refs[-6:]
    _, kv_heads, _, _ = ck.shape
    rows = kv_ref.shape[0]
    pairs = [
        (qs.at[0], qsb),
        (ks.at[0], ksb),
        (vs.at[0], vsb),
        (km.at[0], kmb),
        (vm.at[0], vmb),
        (ck.at[0], c_ref.at[pl.ds(0, kv_heads)]),
        (cv.at[0], c_ref.at[pl.ds(kv_heads, kv_heads)]),
    ]
    done = 0
    for ref in q_refs:
        pairs.append((q.at[0, :, pl.ds(done, ref.shape[1])], ref))
        done += ref.shape[1]
    copies = [pltpu.make_async_copy(a, b, sem.at[i]) for i, (a, b) in enumerate(pairs)]
    for copy in copies:
        copy.start()
    for copy in copies[:5]:
        copy.wait()
    per = width // BLOCK
    pad = jnp.zeros((width - ksb.shape[0], rows), f32)
    for part, (mant, exponent) in enumerate(((kmb, ksb), (vmb, vsb))):
        scale = jnp.concatenate([jnp.exp2(exponent[...].astype(f32)), pad], axis=0).T
        for g in range(kv_heads):
            kv_ref[:, pl.ds((part * kv_heads + g) * width, width)] = decoded(mant[:, pl.ds(g * width, width)], scale, g * per)
    kv_ref[:, pl.ds(2 * kv_heads * width, qsb.shape[1])] = qsb[...].astype(f32).astype(bf16)
    for copy in copies[5:]:
        copy.wait()


def bias_kernel(limit_ref, bias_ref, *, pieces, held, rows, source):
    width = bias_ref.shape[1]
    here = lax.axis_index("seq")
    limit = limit_ref[pl.ds(0, 1), :]
    done = 0
    for cached, d in pieces:
        size = held if cached else rows
        key = lax.broadcasted_iota(jnp.int32, (size, width), 0)
        token = lax.broadcasted_iota(jnp.int32, (size, width), 1)
        if cached:
            seen = source(here, d) * held + key < limit
        else:
            seen = source(here, d) * rows + key <= here * rows + token
        bias_ref[pl.ds(done, size), :] = jnp.where(seen, 0.0, NEG).astype(bf16)
        done += size


def attend_kernel(*refs, cs, bs, pick, kv_heads, width, group, first):
    q_ref, sc_ref, bias_ref = refs[:3]
    c_refs = refs[3 : 3 + cs]
    b_refs = refs[3 + cs : 3 + cs + bs]
    out_ref, k_all, v_all, staged, sem = refs[-5:]
    rows = q_ref.shape[0]
    held = c_refs[0].shape[-2]
    heads = q_ref.shape[1] // width
    per_kv = out_ref.shape[2] // width // kv_heads
    factor = math.log2(math.e) / math.sqrt(width)
    c_keys, c_values, blocks_kv = pick(c_refs, b_refs)
    count = len(c_keys)
    lowest = first // per_kv
    for n in range(k_all.shape[0]):
        g = lowest + n
        for d in range(count):
            k_all[n, pl.ds(d * held, held), pl.ds(0, width)] = c_keys[d](g)
            v_all[n, pl.ds(d * held, held), :] = c_values[d](g)
            at = pl.ds(count * held + d * rows, rows)
            k_all[n, at, pl.ds(0, width)] = blocks_kv[d][:, pl.ds(g * width, width)]
            v_all[n, at, :] = blocks_kv[d][:, pl.ds((kv_heads + g) * width, width)]
        k_all[n, :, pl.ds(width, width)] = bias_ref[...]
    mark = jnp.where(
        lax.broadcasted_iota(jnp.int32, (rows, width), 0) == lax.broadcasted_iota(jnp.int32, (rows, width), 1),
        1.0,
        0.0,
    ).astype(bf16)
    scale = jnp.exp2(sc_ref[...].astype(f32))
    per = width // BLOCK
    copies = []

    def scores(step):
        g = (first + step * group) // per_kv - lowest
        blocks = []
        for k in range(group):
            head = step * group + k
            value = decoded(q_ref[:, pl.ds(head * width, width)], scale, (first + head) * per)
            blocks.append(jnp.concatenate([value, mark], axis=1))
        return lax.dot_general(jnp.concatenate(blocks, axis=0), k_all[g], (((1,), (1,)), ((), ())), preferred_element_type=f32)

    steps = heads // group
    s = scores(0)
    for step in range(steps):
        g = (first + step * group) // per_kv - lowest
        later = scores(step + 1) if step + 1 < steps else None
        top = jnp.max(s, axis=1, keepdims=True)
        w = jnp.exp2((s - top) * factor)
        total = jnp.sum(w, axis=1, keepdims=True)
        o = jnp.dot(w.astype(bf16), v_all[g], preferred_element_type=f32)
        o = (o / total).astype(bf16)
        s = later
        for k in range(group):
            staged[:, pl.ds((step * group + k) * width, width)] = o[k * rows : (k + 1) * rows]
        cols = pl.ds(step * group * width, group * width)
        to = pl.ds((first + step * group) * width, group * width)
        copy = pltpu.make_async_copy(staged.at[:, cols], out_ref.at[0, :, to], sem.at[step])
        copy.start()
        copies.append(copy)
    for copy in copies:
        copy.wait()


def blocks_of(q_ref, group, step, width, mark):
    return jnp.concatenate(
        [jnp.concatenate([q_ref[:, pl.ds((step * group + k) * width, width)], mark], axis=1) for k in range(group)], axis=0
    )


def token_marks(rows, width):
    shape = (rows, width)
    return jnp.where(lax.broadcasted_iota(jnp.int32, shape, 0) == lax.broadcasted_iota(jnp.int32, shape, 1), 1.0, 0.0).astype(bf16)


def product(q, k):
    return lax.dot_general(q, k, (((1,), (1,)), ((), ())), preferred_element_type=f32)


def send(staged, out_ref, sem, step, group, width, first, o):
    rows = staged.shape[0]
    for k in range(group):
        staged[:, pl.ds((step * group + k) * width, width)] = o[k * rows : (k + 1) * rows]
    here = pl.ds(step * group * width, group * width)
    there = pl.ds((first + step * group) * width, group * width)
    return pltpu.make_async_copy(staged.at[:, here], out_ref.at[0, :, there], sem.at[step])


def gather(k_all, v_all, c_refs, b_refs, bias_ref, lowest, first, kv_heads):
    width = v_all.shape[2]
    for n in range(k_all.shape[0]):
        g = lowest + n
        done = 0
        for ref in c_refs:
            at = pl.ds(done, ref.shape[1])
            k_all[n, at, pl.ds(0, width)] = ref[g]
            v_all[n, at, :] = ref[kv_heads + g]
            done += ref.shape[1]
        for ref in b_refs:
            at = pl.ds(done, ref.shape[0])
            k_all[n, at, pl.ds(0, width)] = ref[:, pl.ds(g * width, width)]
            v_all[n, at, :] = ref[:, pl.ds((kv_heads + g) * width, width)]
            done += ref.shape[0]
        k_all[n, :, pl.ds(width, width)] = bias_ref[pl.ds(first, done), :]


def early_kernel(*refs, cs, bs, heads, kv_heads, width, group, first):
    q_ref, sc_ref, bias_ref = refs[:3]
    c_refs, b_refs = refs[3 : 3 + cs], refs[3 + cs : 3 + cs + bs]
    qd, acc, top_ref, total_ref, k_all, v_all = refs[3 + cs + bs :]
    rows = q_ref.shape[0]
    here = q_ref.shape[1] // width
    per_kv = heads // kv_heads
    factor = math.log2(math.e) / math.sqrt(width)
    lowest = first // per_kv
    gather(k_all, v_all, c_refs, b_refs, bias_ref, lowest, 0, kv_heads)
    mark = token_marks(rows, width)
    scale = jnp.exp2(sc_ref[...].astype(f32))
    for head in range(here):
        cols = pl.ds(head * width, width)
        qd[:, cols] = decoded(q_ref[:, cols], scale, (first + head) * (width // BLOCK))
    steps = here // group
    s = product(blocks_of(qd, group, 0, width, mark), k_all[0])
    for step in range(steps):
        g = (first + step * group) // per_kv - lowest
        later = None
        if step + 1 < steps:
            later = product(blocks_of(qd, group, step + 1, width, mark), k_all[(first + (step + 1) * group) // per_kv - lowest])
        top = jnp.max(s, axis=1, keepdims=True)
        w = jnp.exp2((s - top) * factor)
        total = jnp.sum(w, axis=1, keepdims=True)
        at = pl.ds(step * group * rows, group * rows)
        acc[at, :] = jnp.dot(w.astype(bf16), v_all[g], preferred_element_type=f32)
        top_ref[at, :] = jnp.broadcast_to(top, (group * rows, width))
        total_ref[at, :] = jnp.broadcast_to(total, (group * rows, width))
        s = later


def late_kernel(*refs, cs, bs, parts, kv_heads, width, group):
    bias_ref = refs[0]
    c_refs, b_refs = refs[1 : 1 + cs], refs[1 + cs : 1 + cs + bs]
    states = [refs[1 + cs + bs + 4 * n : 5 + cs + bs + 4 * n] for n in range(parts)]
    out_ref, k_all, v_all, staged, sem = refs[-5:]
    rows = staged.shape[0]
    per_kv = out_ref.shape[2] // width // kv_heads
    factor = math.log2(math.e) / math.sqrt(width)
    keys = k_all.shape[1]
    gather(k_all, v_all, c_refs, b_refs, bias_ref, 0, bias_ref.shape[0] - keys, kv_heads)
    mark = token_marks(rows, width)
    todo = []
    for state in states:
        for step in range(state[0].shape[1] // width // group):
            todo.append((state, step, len(todo) * group // per_kv))
    state, step, g = todo[0]
    s = product(blocks_of(state[0], group, step, width, mark), k_all[g])
    copies = []
    for n, (state, step, g) in enumerate(todo):
        later = None
        if n + 1 < len(todo):
            later = product(blocks_of(todo[n + 1][0][0], group, todo[n + 1][1], width, mark), k_all[todo[n + 1][2]])
        _, acc, top_ref, total_ref = state
        at = pl.ds(step * group * rows, group * rows)
        old = top_ref[at, :]
        top = jnp.maximum(old, jnp.broadcast_to(jnp.max(s, axis=1, keepdims=True), old.shape))
        keep = jnp.exp2((old - top) * factor)
        w = jnp.exp2((s - jnp.concatenate([top] * pl.cdiv(keys, width), axis=1)[:, :keys]) * factor)
        total = total_ref[at, :] * keep + jnp.sum(w, axis=1, keepdims=True)
        o = acc[at, :] * keep + jnp.dot(w.astype(bf16), v_all[g], preferred_element_type=f32)
        copies.append(send(staged, out_ref, sem, n, group, width, 0, (o / total).astype(bf16)))
        copies[-1].start()
        s = later
    for copy in copies:
        copy.wait()


def in_hbm(x):
    return pltpu.with_memory_space_constraint(x, pltpu.MemorySpace.HBM)


def natural(here, d):
    return jnp.int32(d)


def mirrored(here, d):
    return lax.bitwise_xor(here, d)


NEAR = [(0, 1), (1, 0), (2, 3), (3, 2)]
FAR = [(0, 2), (2, 0), (1, 3), (3, 1)]


def pick_natural(c_refs, b_refs):
    c, b = c_refs[0], b_refs[0]
    count = c.shape[0]
    kv_heads = c.shape[1] // 2
    keys = [lambda g, d=d: c[d, g] for d in range(count)]
    values = [lambda g, d=d: c[d, kv_heads + g] for d in range(count)]
    return keys, values, [b.at[d] for d in range(count)]


def pick_mirrored(c_refs, b_refs):
    kv_heads = c_refs[0].shape[0] // 2
    keys = [lambda g, c=c: c[g] for c in c_refs]
    values = [lambda g, c=c: c[kv_heads + g] for c in c_refs]
    return keys, values, b_refs


def body(q_mant, q_scale, key_m, key_e, value_m, value_e, cached_k, cached_v, start):
    _, rows, features = q_mant.shape
    _, kv_heads, held, width = cached_k.shape
    count = lax.axis_size("seq")
    sections = lax.axis_size("section")
    heads = features // width
    keys = count * (held + rows)
    mirror = count == len(NEAR)
    slots = range(count)
    if mirror:
        early, late = slots[:-1], slots[-1:]
    else:
        early, late = slots, ()
    pieces = [(cached, d) for part in (early, late) for cached in (True, False) for d in part]
    sizes = [heads * n // sum(SHARES) for n in SHARES]
    kv, cached, *q = pl.pallas_call(
        functools.partial(first_kernel, width=width),
        out_shape=(
            jax.ShapeDtypeStruct((rows, 2 * kv_heads * width + q_scale.shape[2]), bf16),
            jax.ShapeDtypeStruct((2 * kv_heads, held, width), bf16),
            *(jax.ShapeDtypeStruct((rows, n * width), bf16) for n in sizes),
        ),
        in_specs=[HBM] * 8,
        out_specs=(VMEM,) * (2 + len(sizes)),
        scratch_shapes=[
            pltpu.VMEM(q_scale.shape[1:], jnp.int32),
            pltpu.VMEM(key_m.shape[1:], bf16),
            pltpu.VMEM((key_e.shape[2], rows), jnp.int32),
            pltpu.VMEM(value_m.shape[1:], bf16),
            pltpu.VMEM((value_e.shape[2], rows), jnp.int32),
            pltpu.SemaphoreType.DMA((7 + len(sizes),)),
        ],
        compiler_params=pltpu.CompilerParams(vmem_limit_bytes=8 << 20),
        name="first",
    )(*(
        in_hbm(x)
        for x in (q_mant, q_scale, key_m, jnp.swapaxes(key_e, 1, 2), value_m, jnp.swapaxes(value_e, 1, 2), cached_k, cached_v)
    ))
    limits = jnp.broadcast_to(start.reshape(1, 1), (8, width))
    bias = pl.pallas_call(
        functools.partial(bias_kernel, pieces=pieces, held=held, rows=rows, source=mirrored if mirror else natural),
        out_shape=jax.ShapeDtypeStruct((keys, width), bf16),
        in_specs=[VMEM],
        out_specs=VMEM,
        compiler_params=pltpu.CompilerParams(vmem_limit_bytes=8 << 20),
        name="bias",
    )(limits)
    relay = [(i, (i + 1) % sections) for i in range(sections)]
    kv = lax.ppermute(kv, "section", relay)
    kv, scale = kv[:, : 2 * kv_heads * width], kv[:, 2 * kv_heads * width :]
    q = [lax.ppermute(x, "section", relay) for x in q]
    if mirror:
        near = lax.ppermute(cached, "seq", NEAR)
        far = lax.ppermute(cached, "seq", FAR)
        c = [cached, near, far, lax.ppermute(far, "seq", NEAR)]
        far = lax.ppermute(kv, "seq", FAR)
        near = lax.ppermute(kv, "seq", NEAR)
        b = [kv, near, far, lax.ppermute(far, "seq", NEAR)]
    else:
        c = [lax.all_gather(cached, "seq", axis=0)]
        b = [lax.all_gather(kv, "seq", axis=0)]
    group = 4
    limit = (8 << 20) + keys * width * kv_heads * 8 + keys * group * rows * 12 + 4 * rows * features
    if mirror:
        first, states = 0, []
        most = len(early) * (held + rows)
        for x, n in zip(q, sizes):
            held_heads = max(1, n * kv_heads // heads)
            call = pl.pallas_call(
                functools.partial(
                    early_kernel, cs=len(early), bs=len(early), heads=heads, kv_heads=kv_heads, width=width, group=group, first=first
                ),
                out_shape=(jax.ShapeDtypeStruct((rows, n * width), bf16),) + (jax.ShapeDtypeStruct((n * rows, width), f32),) * 3,
                in_specs=[VMEM] * (3 + 2 * len(early)),
                out_specs=(VMEM,) * 4,
                scratch_shapes=[pltpu.VMEM((held_heads, most, 2 * width), bf16), pltpu.VMEM((held_heads, most, width), bf16)],
                compiler_params=pltpu.CompilerParams(vmem_limit_bytes=limit),
                name="early",
            )
            states += call(x, scale, bias, *c[: len(early)], *b[: len(early)])
            first += n
        return pl.pallas_call(
            functools.partial(
                late_kernel, cs=len(late), bs=len(late), parts=len(sizes), kv_heads=kv_heads, width=width, group=group
            ),
            out_shape=jax.ShapeDtypeStruct((1, rows, features), bf16),
            in_specs=[VMEM] * (1 + 2 * len(late) + len(states)),
            out_specs=pl.BlockSpec(memory_space=pl.ANY),
            scratch_shapes=[
                pltpu.VMEM((kv_heads, keys - most, 2 * width), bf16),
                pltpu.VMEM((kv_heads, keys - most, width), bf16),
                pltpu.VMEM((rows, features), bf16),
                pltpu.SemaphoreType.DMA((heads // group,)),
            ],
            compiler_params=pltpu.CompilerParams(vmem_limit_bytes=limit),
            name="late",
        )(bias, *c[len(early) :], *b[len(early) :], *states)
    out, first = (), 0
    for x, n in zip(q, sizes):
        held_heads = max(1, n * kv_heads // heads)
        out = (
            pl.pallas_call(
                functools.partial(
                    attend_kernel,
                    cs=len(c),
                    bs=len(b),
                    pick=pick_mirrored if mirror else pick_natural,
                    kv_heads=kv_heads,
                    width=width,
                    group=group,
                    first=first,
                ),
                out_shape=jax.ShapeDtypeStruct((1, rows, features), bf16),
                in_specs=[VMEM] * (3 + len(c) + len(b)) + [pl.BlockSpec(memory_space=pl.ANY)] * len(out),
                out_specs=pl.BlockSpec(memory_space=pl.ANY),
                scratch_shapes=[
                    pltpu.VMEM((held_heads, keys, 2 * width), bf16),
                    pltpu.VMEM((held_heads, keys, width), bf16),
                    pltpu.VMEM((rows, n * width), bf16),
                    pltpu.SemaphoreType.DMA((n // group,)),
                ],
                input_output_aliases={3 + len(c) + len(b): 0} if out else {},
                compiler_params=pltpu.CompilerParams(vmem_limit_bytes=limit),
            )(x, scale, bias, *c, *b, *out),
        )
        first += n
    return out[0]


SHARES = (1, 1)


def solution(mesh):
    rows = P("section", "seq", "tensor")

    step = jax.shard_map(
        body,
        mesh=mesh,
        in_specs=(rows,) * 6 + (P("section", "tensor", "seq", None),) * 2 + (P("section"),),
        out_specs=rows,
        check_vma=False,
    )
    if mesh.shape["seq"] != len(NEAR):
        return step
    return step
```

time: 30.8 us -> 32.6 us (1.058)
  starting transfers between devices: 15 us -> 16.5 us
  Pallas kernels: 4.99 us -> 6.01 us
  waiting for transfers between devices: 9.98 us -> 9.27 us
    ppermute x1, starting transfers between devices: 0.53 us -> 1.49 us  [body(): kv = lax.ppermute(kv, 'section', relay)]
    pallas_call x2 -> x4, Pallas kernels: 3.91 us -> 4.75 us  [the longest x2 2.8 us: body(): states += call(x, scale, bias, *c[:len(early)], *b[:len(early)])]
    ppermute x1, waiting for transfers between devices: 0.7 us -> 0.01 us  [body(): b = [kv, near, far, lax.ppermute(far, 'seq', NEAR)]]
    ppermute x1, waiting for transfers between devices: 8.03 us -> 7.49 us  [body(): kv = lax.ppermute(kv, 'section', relay)]
    ppermute x1, waiting for transfers between devices: 0.79 us -> 1.32 us  [body(): near = lax.ppermute(kv, 'seq', NEAR)]
    ppermute x1, starting transfers between devices: 2.65 us -> 3.05 us  [body(): far = lax.ppermute(cached, 'seq', FAR)]
    ppermute x1 -> x2, starting transfers between devices: 2.97 us -> 3.11 us  [body(): q = [lax.ppermute(x, 'section', relay) for x in q]]
  transfers between devices with their start and end apart: 8 -> 9, of which waited for: 4 -> 3; matrix products, arithmetic and copies ran while one was open for 0% -> 0% of each run, Pallas kernels for 5% -> 9%
where the time goes in v4:
time: 32.6 us; the launch traced here: 32.5 us
  starting transfers between devices  16.5 us (51%)
  waiting for transfers between devices  9.27 us (28%)
  Pallas kernels  6.01 us (18%)
  between operations  0.73 us (2%)
    ppermute x1, waiting for transfers between devices, body(): kv = lax.ppermute(kv, 'section', relay)  7.49 us
    ppermute x2, starting transfers between devices, body(): q = [lax.ppermute(x, 'section', relay) for x in q]  3.11 us
    ppermute x1, starting transfers between devices, body(): far = lax.ppermute(cached, 'seq', FAR)  3.05 us
    ppermute x1, starting transfers between devices, body(): far = lax.ppermute(kv, 'seq', FAR)  2.84 us
    pallas_call x2, Pallas kernels, body(): states += call(x, scale, bias, *c[:len(early)], *b[:len(early)])  2.8 us
    ppermute x1, starting transfers between devices, body(): b = [kv, near, far, lax.ppermute(far, 'seq', NEAR)]  2.37 us
    pallas_call x1, Pallas kernels, body(): pl.pallas_call(functools.partial(late_kernel, cs=len(late), bs=len(late),...  1.89 us
    ppermute x1, starting transfers between devices, body(): c = [cached, near, far, lax.ppermute(far, 'seq', NEAR)]  1.58 us
  transfers between devices with their start and end apart: 9, of which 3 were waited for; matrix products, arithmetic and copies ran while one was open for 0% of the time, Pallas kernels for 9%

profile of v4, /device:TPU:0, one launch (start us, length us, event | category | flops | bytes accessed | tf_op | source)
XLA Modules:
  0.0 32.5 jit_solution(15141992212903497251)
XLA Ops:
  0.0 1.3 %first.1 = (bf16[64,640]{1,0:T(8,128)(2,1)S(1)}, bf16[4,128,128]{2,1,0:T(8,128)(2,1)S(1)}, bf16[64,2048]{1,0:T(8,128)(2,1)S(1)}, bf16[64,2048]{1,0:T(8,128)(2,1)S(1)}) custom-call(bf16[1,64,4096]{2,1,0:T(8,128)(2,1)} %refs_0_.1, s32[1,64,128]{2,1,0:T(8,128)} %refs_1_.1, bf16[1,64,256]{2,1,0:T(8,128)(2,1)} %refs_2_.1, s32[1,8,64]{2,1,0:T(8,128)} %bitcast.4, ...), custom_call_target="tpu_custom_call" | custom-call | tf_op jit(solution)/shard_map/first/pallas_call | solution.py:300
  1.3 3.0 %collective-permute-start.8 = (bf16[64,2048]{1,0:T(8,128)(2,1)S(1)}, bf16[64,2048]{1,0:T(8,128)(2,1)S(1)}, u32[]{:S(2)}, u32[]{:S(2)}) collective-permute-start(bf16[64,2048]{1,0:T(8,128)(2,1)S(1)} %get-tuple-element.24), channel_id=1, source_target_pairs={{0,16},{16,0},{1,17},{17,1},{2,18},{18,2},{3,19},{19,3},{4,20},{20... | collective-permute-start | bytes 786440 | tf_op jit(solution)/shard_map/ppermute | solution.py:335
  4.3 0.1 collective-permute-start.5
  4.4 3.0 %collective-permute-start = (bf16[4,128,128]{2,1,0:T(8,128)(2,1)S(1)}, bf16[4,128,128]{2,1,0:T(8,128)(2,1)S(1)}, u32[]{:S(2)}, u32[]{:S(2)}) collective-permute-start(bf16[4,128,128]{2,1,0:T(8,128)(2,1)S(1)} %get-tuple-element.17.refs_3_), channel_id=1, source_target_pairs={{0,8},{8,0},{4,12},{12,4},{1,9},{9,1},{5,13},{13,5},{2,10},{10,2},... | collective-permute-start | bytes 393224 | tf_op jit(solution)/shard_map/ppermute | solution.py:338
  7.4 1.5 %collective-permute-start.2 = (bf16[64,640]{1,0:T(8,128)(2,1)S(1)}, bf16[64,640]{1,0:T(8,128)(2,1)S(1)}, u32[]{:S(2)}, u32[]{:S(2)}) collective-permute-start(bf16[64,640]{1,0:T(8,128)(2,1)S(1)} %get-tuple-element.18), channel_id=1, source_target_pairs={{0,16},{16,0},{1,17},{17,1},{2,18},{18,2},{3,19},{19,3},{4,20},{20... | collective-permute-start | bytes 245768 | tf_op jit(solution)/shard_map/ppermute | solution.py:333
  8.9 1.6 %collective-permute-start.6 = (bf16[4,128,128]{2,1,0:T(8,128)(2,1)S(1)}, bf16[4,128,128]{2,1,0:T(8,128)(2,1)S(1)}, u32[]{:S(2)}, u32[]{:S(2)}) collective-permute-start(bf16[4,128,128]{2,1,0:T(8,128)(2,1)S(1)} %get-tuple-element.17.refs_3_), channel_id=1, source_target_pairs={{0,4},{4,0},{8,12},{12,8},{1,5},{5,1},{9,13},{13,9},{2,6},{6,2},{1... | collective-permute-start | bytes 393224 | tf_op jit(solution)/shard_map/ppermute | solution.py:337
  10.5 7.5 %collective-permute-done.2 = bf16[64,640]{1,0:T(8,128)(2,1)S(1)} collective-permute-done((bf16[64,640]{1,0:T(8,128)(2,1)S(1)}, bf16[64,640]{1,0:T(8,128)(2,1)S(1)}, u32[]{:S(2)}, u32[]{:S(2)}) %collective-permute-start.2) | collective-permute-done | bytes 81952 | tf_op jit(solution)/shard_map/ppermute | solution.py:333
  18.0 2.8 %collective-permute-start.3 = (bf16[64,512]{1,0:T(8,128)(2,1)S(1)}, bf16[64,512]{1,0:T(8,128)(2,1)S(1)}, u32[]{:S(2)}, u32[]{:S(2)}) collective-permute-start(bf16[64,512]{1,0:T(8,128)(2,1)S(1)} %slice.8.refs_6_), channel_id=1, source_target_pairs={{0,8},{8,0},{4,12},{12,4},{1,9},{9,1},{5,13},{13,5},{2,10},{10,2},... | collective-permute-start | bytes 196616 | tf_op jit(solution)/shard_map/ppermute | solution.py:340
  20.8 0.0 collective-permute-done.refs_5_
  20.8 1.6 %collective-permute-start.1 = (bf16[4,128,128]{2,1,0:T(8,128)(2,1)S(1)}, bf16[4,128,128]{2,1,0:T(8,128)(2,1)S(1)}, u32[]{:S(2)}, u32[]{:S(2)}) collective-permute-start(bf16[4,128,128]{2,1,0:T(8,128)(2,1)S(1)} %collective-permute-done.refs_5_), channel_id=1, source_target_pairs={{0,4},{4,0},{8,12},{12,8},{1,5},{5,1},{9,13},{13,9},{2,6},{6,2},{1... | collective-permute-start | bytes 393224 | tf_op jit(solution)/shard_map/ppermute | solution.py:339
  22.4 0.0 collective-permute-done.6.refs_4_
  22.4 0.5 %collective-permute-start.7 = (bf16[64,512]{1,0:T(8,128)(2,1)S(1)}, bf16[64,512]{1,0:T(8,128)(2,1)S(1)}, u32[]{:S(2)}, u32[]{:S(2)}) collective-permute-start(bf16[64,512]{1,0:T(8,128)(2,1)S(1)} %slice.8.refs_6_), channel_id=1, source_target_pairs={{0,4},{4,0},{8,12},{12,8},{1,5},{5,1},{9,13},{13,9},{2,6},{6,2},{1... | collective-permute-start | bytes 196616 | tf_op jit(solution)/shard_map/ppermute | solution.py:341
  22.9 0.4 %collective-permute-done.3.refs_8_ = bf16[64,512]{1,0:T(8,128)(2,1)S(1)} collective-permute-done((bf16[64,512]{1,0:T(8,128)(2,1)S(1)}, bf16[64,512]{1,0:T(8,128)(2,1)S(1)}, u32[]{:S(2)}, u32[]{:S(2)}) %collective-permute-start.3) | collective-permute-done | bytes 65568 | tf_op jit(solution)/shard_map/ppermute | solution.py:340
  23.3 2.4 %collective-permute-start.4 = (bf16[64,512]{1,0:T(8,128)(2,1)S(1)}, bf16[64,512]{1,0:T(8,128)(2,1)S(1)}, u32[]{:S(2)}, u32[]{:S(2)}) collective-permute-start(bf16[64,512]{1,0:T(8,128)(2,1)S(1)} %collective-permute-done.3.refs_8_), channel_id=1, source_target_pairs={{0,4},{4,0},{8,12},{12,8},{1,5},{5,1},{9,13},{13,9},{2,6},{6,2},{1... | collective-permute-start | bytes 196616 | tf_op jit(solution)/shard_map/ppermute | solution.py:342
  26.3 0.1 bias.1.refs_2_.refs_0_
  26.4 1.3 %collective-permute-done.7.refs_7_ = bf16[64,512]{1,0:T(8,128)(2,1)S(1)} collective-permute-done((bf16[64,512]{1,0:T(8,128)(2,1)S(1)}, bf16[64,512]{1,0:T(8,128)(2,1)S(1)}, u32[]{:S(2)}, u32[]{:S(2)}) %collective-permute-start.7) | collective-permute-done | bytes 65568 | tf_op jit(solution)/shard_map/ppermute | solution.py:341
  27.7 0.0 collective-permute-done.8.refs_0_
  27.7 1.4 %early.3 = (bf16[64,2048]{1,0:T(8,128)(2,1)S(1)}, f32[1024,128]{1,0:T(8,128)S(1)}, f32[1024,128]{1,0:T(8,128)S(1)}, f32[1024,128]{1,0:T(8,128)S(1)}) custom-call(bf16[64,2048]{1,0:T(8,128)(2,1)S(1)} %collective-permute-done.8.refs_0_, bf16[64,128]{1,0:T(8,128)(2,1)S(1)} %slice.9.refs_1_, bf16[768,128]{1,0:T(8,128)(2,1)S(1)} %bias.1.refs_2_.refs_0_, ...), custom_call_target="tpu_custom_call" | custom-call | tf_op jit(solution)/shard_map/early/pallas_call | solution.py:364
  29.1 0.0 collective-permute-done.5.refs_0_
  29.2 1.4 %early.2 = (bf16[64,2048]{1,0:T(8,128)(2,1)S(1)}, f32[1024,128]{1,0:T(8,128)S(1)}, f32[1024,128]{1,0:T(8,128)S(1)}, f32[1024,128]{1,0:T(8,128)S(1)}) custom-call(bf16[64,2048]{1,0:T(8,128)(2,1)S(1)} %collective-permute-done.5.refs_0_, bf16[64,128]{1,0:T(8,128)(2,1)S(1)} %slice.9.refs_1_, bf16[768,128]{1,0:T(8,128)(2,1)S(1)} %bias.1.refs_2_.refs_0_, ...), custom_call_target="tpu_custom_call" | custom-call | tf_op jit(solution)/shard_map/early/pallas_call | solution.py:364
  30.6 0.0 collective-permute-done.4.refs_2_
  30.6 0.0 collective-permute-done.1.refs_1_
  30.6 1.9 %late.1 = bf16[1,64,4096]{2,1,0:T(8,128)(2,1)} custom-call(bf16[768,128]{1,0:T(8,128)(2,1)S(1)} %bias.1.refs_2_.refs_0_, bf16[4,128,128]{2,1,0:T(8,128)(2,1)S(1)} %collective-permute-done.1.refs_1_, bf16[64,512]{1,0:T(8,128)(2,1)S(1)} %collective-permute-done.4.refs_2_, bf16[64,2048]{1,0:T(8,128)(2,1)S(1)} %get-tuple-element.20.refs_3_, ...), custom_call_target="tpu_custom_call" | custom-call | tf_op jit(solution)/shard_map/late/pallas_call | solution.py:366
  (3 shorter events, 0.0 us)
Async XLA Ops:
  1.3 26.5 %collective-permute-start.8 = (bf16[64,2048]{1,0:T(8,128)(2,1)S(1)}, bf16[64,2048]{1,0:T(8,128)(2,1)S(1)}, u32[]{:S(2)}, u32[]{:S(2)}) collective-permute-start(bf16[64,2048]{1,0:T(8,128)(2,1)S(1)} %get-tuple-element.24), channel_id=1, source_target_pairs={{0,16},{16,0},{1,17},{17,1},{2,18},{18,2},{3,19},{19,3},{4,20},{20... | collective-permute-start | bytes 786440 | tf_op jit(solution)/shard_map/ppermute | solution.py:335
  4.3 24.9 %collective-permute-start.5 = (bf16[64,2048]{1,0:T(8,128)(2,1)S(1)}, bf16[64,2048]{1,0:T(8,128)(2,1)S(1)}, u32[]{:S(2)}, u32[]{:S(2)}) collective-permute-start(bf16[64,2048]{1,0:T(8,128)(2,1)S(1)} %get-tuple-element.19), channel_id=1, source_target_pairs={{0,16},{16,0},{1,17},{17,1},{2,18},{18,2},{3,19},{19,3},{4,20},{20... | collective-permute-start | bytes 786440 | tf_op jit(solution)/shard_map/ppermute | solution.py:335
  4.4 16.4 %collective-permute-start = (bf16[4,128,128]{2,1,0:T(8,128)(2,1)S(1)}, bf16[4,128,128]{2,1,0:T(8,128)(2,1)S(1)}, u32[]{:S(2)}, u32[]{:S(2)}) collective-permute-start(bf16[4,128,128]{2,1,0:T(8,128)(2,1)S(1)} %get-tuple-element.17.refs_3_), channel_id=1, source_target_pairs={{0,8},{8,0},{4,12},{12,4},{1,9},{9,1},{5,13},{13,5},{2,10},{10,2},... | collective-permute-start | bytes 393224 | tf_op jit(solution)/shard_map/ppermute | solution.py:338
  7.4 10.6 %collective-permute-start.2 = (bf16[64,640]{1,0:T(8,128)(2,1)S(1)}, bf16[64,640]{1,0:T(8,128)(2,1)S(1)}, u32[]{:S(2)}, u32[]{:S(2)}) collective-permute-start(bf16[64,640]{1,0:T(8,128)(2,1)S(1)} %get-tuple-element.18), channel_id=1, source_target_pairs={{0,16},{16,0},{1,17},{17,1},{2,18},{18,2},{3,19},{19,3},{4,20},{20... | collective-permute-start | bytes 245768 | tf_op jit(solution)/shard_map/ppermute | solution.py:333
  8.9 13.5 %collective-permute-start.6 = (bf16[4,128,128]{2,1,0:T(8,128)(2,1)S(1)}, bf16[4,128,128]{2,1,0:T(8,128)(2,1)S(1)}, u32[]{:S(2)}, u32[]{:S(2)}) collective-permute-start(bf16[4,128,128]{2,1,0:T(8,128)(2,1)S(1)} %get-tuple-element.17.refs_3_), channel_id=1, source_target_pairs={{0,4},{4,0},{8,12},{12,8},{1,5},{5,1},{9,13},{13,9},{2,6},{6,2},{1... | collective-permute-start | bytes 393224 | tf_op jit(solution)/shard_map/ppermute | solution.py:337
  18.0 5.3 %collective-permute-start.3 = (bf16[64,512]{1,0:T(8,128)(2,1)S(1)}, bf16[64,512]{1,0:T(8,128)(2,1)S(1)}, u32[]{:S(2)}, u32[]{:S(2)}) collective-permute-start(bf16[64,512]{1,0:T(8,128)(2,1)S(1)} %slice.8.refs_6_), channel_id=1, source_target_pairs={{0,8},{8,0},{4,12},{12,4},{1,9},{9,1},{5,13},{13,5},{2,10},{10,2},... | collective-permute-start | bytes 196616 | tf_op jit(solution)/shard_map/ppermute | solution.py:340
  20.8 9.8 %collective-permute-start.1 = (bf16[4,128,128]{2,1,0:T(8,128)(2,1)S(1)}, bf16[4,128,128]{2,1,0:T(8,128)(2,1)S(1)}, u32[]{:S(2)}, u32[]{:S(2)}) collective-permute-start(bf16[4,128,128]{2,1,0:T(8,128)(2,1)S(1)} %collective-permute-done.refs_5_), channel_id=1, source_target_pairs={{0,4},{4,0},{8,12},{12,8},{1,5},{5,1},{9,13},{13,9},{2,6},{6,2},{1... | collective-permute-start | bytes 393224 | tf_op jit(solution)/shard_map/ppermute | solution.py:339
  22.4 5.3 %collective-permute-start.7 = (bf16[64,512]{1,0:T(8,128)(2,1)S(1)}, bf16[64,512]{1,0:T(8,128)(2,1)S(1)}, u32[]{:S(2)}, u32[]{:S(2)}) collective-permute-start(bf16[64,512]{1,0:T(8,128)(2,1)S(1)} %slice.8.refs_6_), channel_id=1, source_target_pairs={{0,4},{4,0},{8,12},{12,8},{1,5},{5,1},{9,13},{13,9},{2,6},{6,2},{1... | collective-permute-start | bytes 196616 | tf_op jit(solution)/shard_map/ppermute | solution.py:341
  23.3 7.3 %collective-permute-start.4 = (bf16[64,512]{1,0:T(8,128)(2,1)S(1)}, bf16[64,512]{1,0:T(8,128)(2,1)S(1)}, u32[]{:S(2)}, u32[]{:S(2)}) collective-permute-start(bf16[64,512]{1,0:T(8,128)(2,1)S(1)} %collective-permute-done.3.refs_8_), channel_id=1, source_target_pairs={{0,4},{4,0},{8,12},{12,8},{1,5},{5,1},{9,13},{13,9},{2,6},{6,2},{1... | collective-permute-start | bytes 196616 | tf_op jit(solution)/shard_map/ppermute | solution.py:342

commit v5 on v4

--- a/solution.py
+++ b/solution.py
@@ -178,7 +178,12 @@
             k_all[n, at, pl.ds(0, width)] = ref[:, pl.ds(g * width, width)]
             v_all[n, at, :] = ref[:, pl.ds((kv_heads + g) * width, width)]
             done += ref.shape[0]
-        k_all[n, :, pl.ds(width, width)] = bias_ref[pl.ds(first, done), :]
+        k_all[n, pl.ds(0, done), pl.ds(width, width)] = bias_ref[pl.ds(first, done), :]
+        if done < k_all.shape[1]:
+            rest = pl.ds(done, k_all.shape[1] - done)
+            k_all[n, rest, pl.ds(0, width)] = jnp.zeros((rest.size, width), bf16)
+            k_all[n, rest, pl.ds(width, width)] = jnp.full((rest.size, width), NEG, bf16)
+            v_all[n, rest, :] = jnp.zeros((rest.size, width), bf16)
 
 
 def early_kernel(*refs, cs, bs, heads, kv_heads, width, group, first):
@@ -213,7 +218,14 @@
         s = later
 
 
-def late_kernel(*refs, cs, bs, parts, kv_heads, width, group):
+def late_kernel(*refs, cs, bs, parts, kv_heads, width, group, lead, skip):
+    first_tokens = lax.axis_index("seq") == 0
+    pl.when(first_tokens if lead else jnp.logical_not(first_tokens))(
+        functools.partial(finish, refs, cs, bs, parts, kv_heads, width, group, skip)
+    )
+
+
+def finish(refs, cs, bs, parts, kv_heads, width, group, skip):
     bias_ref = refs[0]
     c_refs, b_refs = refs[1 : 1 + cs], refs[1 + cs : 1 + cs + bs]
     states = [refs[1 + cs + bs + 4 * n : 5 + cs + bs + 4 * n] for n in range(parts)]
@@ -222,7 +234,7 @@
     per_kv = out_ref.shape[2] // width // kv_heads
     factor = math.log2(math.e) / math.sqrt(width)
     keys = k_all.shape[1]
-    gather(k_all, v_all, c_refs, b_refs, bias_ref, 0, bias_ref.shape[0] - keys, kv_heads)
+    gather(k_all, v_all, c_refs, b_refs, bias_ref, 0, skip, kv_heads)
     mark = token_marks(rows, width)
     todo = []
     for state in states:
@@ -363,22 +375,38 @@
             )
             states += call(x, scale, bias, *c[: len(early)], *b[: len(early)])
             first += n
-        return pl.pallas_call(
-            functools.partial(
-                late_kernel, cs=len(late), bs=len(late), parts=len(sizes), kv_heads=kv_heads, width=width, group=group
-            ),
-            out_shape=jax.ShapeDtypeStruct((1, rows, features), bf16),
-            in_specs=[VMEM] * (1 + 2 * len(late) + len(states)),
-            out_specs=pl.BlockSpec(memory_space=pl.ANY),
-            scratch_shapes=[
-                pltpu.VMEM((kv_heads, keys - most, 2 * width), bf16),
-                pltpu.VMEM((kv_heads, keys - most, width), bf16),
-                pltpu.VMEM((rows, features), bf16),
-                pltpu.SemaphoreType.DMA((heads // group,)),
-            ],
-            compiler_params=pltpu.CompilerParams(vmem_limit_bytes=limit),
-            name="late",
-        )(bias, *c[len(early) :], *b[len(early) :], *states)
+        out = []
+        for lead in (True, False):
+            blocks = [] if lead else b[len(early) :]
+            fresh = len(late) * held + len(blocks) * rows
+            padded = pl.cdiv(fresh, width) * width
+            call = pl.pallas_call(
+                functools.partial(
+                    late_kernel,
+                    cs=len(late),
+                    bs=len(blocks),
+                    parts=len(sizes),
+                    kv_heads=kv_heads,
+                    width=width,
+                    group=2 * group,
+                    lead=lead,
+                    skip=most,
+                ),
+                out_shape=jax.ShapeDtypeStruct((1, rows, features), bf16),
+                in_specs=[VMEM] * (1 + len(late) + len(blocks) + len(states)) + [pl.BlockSpec(memory_space=pl.ANY)] * len(out),
+                out_specs=pl.BlockSpec(memory_space=pl.ANY),
+                scratch_shapes=[
+                    pltpu.VMEM((kv_heads, padded, 2 * width), bf16),
+                    pltpu.VMEM((kv_heads, padded, width), bf16),
+                    pltpu.VMEM((rows, features), bf16),
+                    pltpu.SemaphoreType.DMA((heads // group,)),
+                ],
+                input_output_aliases={} if lead else {1 + len(late) + len(blocks) + len(states): 0},
+                compiler_params=pltpu.CompilerParams(vmem_limit_bytes=limit),
+                name="late",
+            )
+            out = [call(bias, *c[len(early) :], *blocks, *states, *out)]
+        return out[0]
     out, first = (), 0
     for x, n in zip(q, sizes):
         held_heads = max(1, n * kv_heads // heads)

time: 32.6 us -> 30.6 us (0.939)
  waiting for transfers between devices: 9.27 us -> 7.58 us
  starting transfers between devices: 16.5 us -> 16.1 us
    ppermute x1, waiting for transfers between devices: 7.49 us -> 4.04 us  [body(): kv = lax.ppermute(kv, 'section', relay)]
    ppermute x1, waiting for transfers between devices: 0.01 us -> 2.67 us  [body(): far = lax.ppermute(cached, 'seq', FAR)]
    ppermute x1, waiting for transfers between devices: 1.32 us -> 0.01 us  [body(): near = lax.ppermute(kv, 'seq', NEAR)]
    ppermute x1, starting transfers between devices: 0.45 us -> 1.58 us  [body(): near = lax.ppermute(kv, 'seq', NEAR)]
    ppermute x1, starting transfers between devices: 1.58 us -> 0.77 us  [body(): c = [cached, near, far, lax.ppermute(far, 'seq', NEAR)]]
    ppermute x1, starting transfers between devices: 2.37 us -> 1.72 us  [body(): b = [kv, near, far, lax.ppermute(far, 'seq', NEAR)]]
    ppermute x1, waiting for transfers between devices: 0.45 us -> 0.85 us  [body(): far = lax.ppermute(kv, 'seq', FAR)]
    pallas_call x1 -> x2, Pallas kernels: 1.89 us -> 1.82 us  [body(): out = [call(bias, *c[len(early):], *blocks, *states, *out)]]
  transfers between devices with their start and end apart: 9 -> 9, of which waited for: 3 -> 3; matrix products, arithmetic and copies ran while one was open for 0% -> 0% of each run, Pallas kernels for 9% -> 15%
where the time goes in v5:
time: 30.6 us; the launch traced here: 30.4 us
  starting transfers between devices  16.1 us (53%)
  waiting for transfers between devices  7.58 us (25%)
  Pallas kernels  5.94 us (19%)
  between operations  0.75 us (2%)
    ppermute x1, waiting for transfers between devices, body(): kv = lax.ppermute(kv, 'section', relay)  4.04 us
    ppermute x2, starting transfers between devices, body(): q = [lax.ppermute(x, 'section', relay) for x in q]  3.11 us
    ppermute x1, starting transfers between devices, body(): far = lax.ppermute(cached, 'seq', FAR)  3.05 us
    ppermute x1, starting transfers between devices, body(): far = lax.ppermute(kv, 'seq', FAR)  2.84 us
    pallas_call x2, Pallas kernels, body(): states += call(x, scale, bias, *c[:len(early)], *b[:len(early)])  2.8 us
    ppermute x1, waiting for transfers between devices, body(): far = lax.ppermute(cached, 'seq', FAR)  2.67 us
    pallas_call x2, Pallas kernels, body(): out = [call(bias, *c[len(early):], *blocks, *states, *out)]  1.82 us
    ppermute x1, starting transfers between devices, body(): b = [kv, near, far, lax.ppermute(far, 'seq', NEAR)]  1.72 us
  transfers between devices with their start and end apart: 9, of which 3 were waited for; matrix products, arithmetic and copies ran while one was open for 0% of the time, Pallas kernels for 15%

profile of v5, /device:TPU:0, one launch (start us, length us, event | category | flops | bytes accessed | tf_op | source)
XLA Modules:
  0.0 30.4 jit_solution(11781146732707450401)
XLA Ops:
  0.0 1.3 %first.1 = (bf16[64,640]{1,0:T(8,128)(2,1)S(1)}, bf16[4,128,128]{2,1,0:T(8,128)(2,1)S(1)}, bf16[64,2048]{1,0:T(8,128)(2,1)S(1)}, bf16[64,2048]{1,0:T(8,128)(2,1)S(1)}) custom-call(bf16[1,64,4096]{2,1,0:T(8,128)(2,1)} %refs_0_.1, s32[1,64,128]{2,1,0:T(8,128)} %refs_1_.1, bf16[1,64,256]{2,1,0:T(8,128)(2,1)} %refs_2_.1, s32[1,8,64]{2,1,0:T(8,128)} %bitcast.4, ...), custom_call_target="tpu_custom_call" | custom-call | tf_op jit(solution)/shard_map/first/pallas_call | solution.py:312
  1.3 3.0 %collective-permute-start.8 = (bf16[64,2048]{1,0:T(8,128)(2,1)S(1)}, bf16[64,2048]{1,0:T(8,128)(2,1)S(1)}, u32[]{:S(2)}, u32[]{:S(2)}) collective-permute-start(bf16[64,2048]{1,0:T(8,128)(2,1)S(1)} %get-tuple-element.24), channel_id=1, source_target_pairs={{0,16},{16,0},{1,17},{17,1},{2,18},{18,2},{3,19},{19,3},{4,20},{20... | collective-permute-start | bytes 786440 | tf_op jit(solution)/shard_map/ppermute | solution.py:347
  4.3 0.1 collective-permute-start.5
  4.4 3.0 %collective-permute-start = (bf16[4,128,128]{2,1,0:T(8,128)(2,1)S(1)}, bf16[4,128,128]{2,1,0:T(8,128)(2,1)S(1)}, u32[]{:S(2)}, u32[]{:S(2)}) collective-permute-start(bf16[4,128,128]{2,1,0:T(8,128)(2,1)S(1)} %get-tuple-element.17.refs_3_), channel_id=1, source_target_pairs={{0,8},{8,0},{4,12},{12,4},{1,9},{9,1},{5,13},{13,5},{2,10},{10,2},... | collective-permute-start | bytes 393224 | tf_op jit(solution)/shard_map/ppermute | solution.py:350
  7.4 1.5 %collective-permute-start.2 = (bf16[64,640]{1,0:T(8,128)(2,1)S(1)}, bf16[64,640]{1,0:T(8,128)(2,1)S(1)}, u32[]{:S(2)}, u32[]{:S(2)}) collective-permute-start(bf16[64,640]{1,0:T(8,128)(2,1)S(1)} %get-tuple-element.18), channel_id=1, source_target_pairs={{0,16},{16,0},{1,17},{17,1},{2,18},{18,2},{3,19},{19,3},{4,20},{20... | collective-permute-start | bytes 245768 | tf_op jit(solution)/shard_map/ppermute | solution.py:345
  8.9 1.6 %collective-permute-start.6 = (bf16[4,128,128]{2,1,0:T(8,128)(2,1)S(1)}, bf16[4,128,128]{2,1,0:T(8,128)(2,1)S(1)}, u32[]{:S(2)}, u32[]{:S(2)}) collective-permute-start(bf16[4,128,128]{2,1,0:T(8,128)(2,1)S(1)} %get-tuple-element.17.refs_3_), channel_id=1, source_target_pairs={{0,4},{4,0},{8,12},{12,8},{1,5},{5,1},{9,13},{13,9},{2,6},{6,2},{1... | collective-permute-start | bytes 393224 | tf_op jit(solution)/shard_map/ppermute | solution.py:349
  10.5 2.7 %collective-permute-done.refs_5_ = bf16[4,128,128]{2,1,0:T(8,128)(2,1)S(1)} collective-permute-done((bf16[4,128,128]{2,1,0:T(8,128)(2,1)S(1)}, bf16[4,128,128]{2,1,0:T(8,128)(2,1)S(1)}, u32[]{:S(2)}, u32[]{:S(2)}) %collective-permute-start) | collective-permute-done | bytes 131104 | tf_op jit(solution)/shard_map/ppermute | solution.py:350
  13.2 0.8 %collective-permute-start.1 = (bf16[4,128,128]{2,1,0:T(8,128)(2,1)S(1)}, bf16[4,128,128]{2,1,0:T(8,128)(2,1)S(1)}, u32[]{:S(2)}, u32[]{:S(2)}) collective-permute-start(bf16[4,128,128]{2,1,0:T(8,128)(2,1)S(1)} %collective-permute-done.refs_5_), channel_id=1, source_target_pairs={{0,4},{4,0},{8,12},{12,8},{1,5},{5,1},{9,13},{13,9},{2,6},{6,2},{1... | collective-permute-start | bytes 393224 | tf_op jit(solution)/shard_map/ppermute | solution.py:351
  13.9 4.0 %collective-permute-done.2 = bf16[64,640]{1,0:T(8,128)(2,1)S(1)} collective-permute-done((bf16[64,640]{1,0:T(8,128)(2,1)S(1)}, bf16[64,640]{1,0:T(8,128)(2,1)S(1)}, u32[]{:S(2)}, u32[]{:S(2)}) %collective-permute-start.2) | collective-permute-done | bytes 81952 | tf_op jit(solution)/shard_map/ppermute | solution.py:345
  18.0 2.8 %collective-permute-start.3 = (bf16[64,512]{1,0:T(8,128)(2,1)S(1)}, bf16[64,512]{1,0:T(8,128)(2,1)S(1)}, u32[]{:S(2)}, u32[]{:S(2)}) collective-permute-start(bf16[64,512]{1,0:T(8,128)(2,1)S(1)} %slice.8.refs_6_), channel_id=1, source_target_pairs={{0,8},{8,0},{4,12},{12,4},{1,9},{9,1},{5,13},{13,5},{2,10},{10,2},... | collective-permute-start | bytes 196616 | tf_op jit(solution)/shard_map/ppermute | solution.py:352
  20.8 0.0 collective-permute-done.6.refs_4_
  20.8 1.6 %collective-permute-start.7 = (bf16[64,512]{1,0:T(8,128)(2,1)S(1)}, bf16[64,512]{1,0:T(8,128)(2,1)S(1)}, u32[]{:S(2)}, u32[]{:S(2)}) collective-permute-start(bf16[64,512]{1,0:T(8,128)(2,1)S(1)} %slice.8.refs_6_), channel_id=1, source_target_pairs={{0,4},{4,0},{8,12},{12,8},{1,5},{5,1},{9,13},{13,9},{2,6},{6,2},{1... | collective-permute-start | bytes 196616 | tf_op jit(solution)/shard_map/ppermute | solution.py:353
  22.4 0.8 %collective-permute-done.3.refs_8_ = bf16[64,512]{1,0:T(8,128)(2,1)S(1)} collective-permute-done((bf16[64,512]{1,0:T(8,128)(2,1)S(1)}, bf16[64,512]{1,0:T(8,128)(2,1)S(1)}, u32[]{:S(2)}, u32[]{:S(2)}) %collective-permute-start.3) | collective-permute-done | bytes 65568 | tf_op jit(solution)/shard_map/ppermute | solution.py:352
  23.3 1.7 %collective-permute-start.4 = (bf16[64,512]{1,0:T(8,128)(2,1)S(1)}, bf16[64,512]{1,0:T(8,128)(2,1)S(1)}, u32[]{:S(2)}, u32[]{:S(2)}) collective-permute-start(bf16[64,512]{1,0:T(8,128)(2,1)S(1)} %collective-permute-done.3.refs_8_), channel_id=1, source_target_pairs={{0,4},{4,0},{8,12},{12,8},{1,5},{5,1},{9,13},{13,9},{2,6},{6,2},{1... | collective-permute-start | bytes 196616 | tf_op jit(solution)/shard_map/ppermute | solution.py:354
  25.6 0.1 bias.1.refs_2_.refs_0_
  25.7 0.0 collective-permute-done.7.refs_7_
  25.7 0.0 collective-permute-done.8.refs_0_
  25.7 1.4 %early.3 = (bf16[64,2048]{1,0:T(8,128)(2,1)S(1)}, f32[1024,128]{1,0:T(8,128)S(1)}, f32[1024,128]{1,0:T(8,128)S(1)}, f32[1024,128]{1,0:T(8,128)S(1)}) custom-call(bf16[64,2048]{1,0:T(8,128)(2,1)S(1)} %collective-permute-done.8.refs_0_, bf16[64,128]{1,0:T(8,128)(2,1)S(1)} %slice.9.refs_1_, bf16[768,128]{1,0:T(8,128)(2,1)S(1)} %bias.1.refs_2_.refs_0_, ...), custom_call_target="tpu_custom_call" | custom-call | tf_op jit(solution)/shard_map/early/pallas_call | solution.py:376
  27.1 0.0 collective-permute-done.5.refs_0_
  27.2 1.4 %early.2 = (bf16[64,2048]{1,0:T(8,128)(2,1)S(1)}, f32[1024,128]{1,0:T(8,128)S(1)}, f32[1024,128]{1,0:T(8,128)S(1)}, f32[1024,128]{1,0:T(8,128)S(1)}) custom-call(bf16[64,2048]{1,0:T(8,128)(2,1)S(1)} %collective-permute-done.5.refs_0_, bf16[64,128]{1,0:T(8,128)(2,1)S(1)} %slice.9.refs_1_, bf16[768,128]{1,0:T(8,128)(2,1)S(1)} %bias.1.refs_2_.refs_0_, ...), custom_call_target="tpu_custom_call" | custom-call | tf_op jit(solution)/shard_map/early/pallas_call | solution.py:376
  28.6 0.0 collective-permute-done.1.refs_1_
  28.6 1.7 %late.2.refs_11_ = bf16[1,64,4096]{2,1,0:T(8,128)(2,1)} custom-call(bf16[768,128]{1,0:T(8,128)(2,1)S(1)} %bias.1.refs_2_.refs_0_, bf16[4,128,128]{2,1,0:T(8,128)(2,1)S(1)} %collective-permute-done.1.refs_1_, bf16[64,2048]{1,0:T(8,128)(2,1)S(1)} %get-tuple-element.20.refs_2_.refs_3_, f32[1024,128]{1,0:T(8,128)S(1)} %get-tuple-element.21.refs_3_.refs_4_, ...), custom_call_target="tpu_custom_call" | custom-call | tf_op jit(solution)/shard_map/late/pallas_call | solution.py:408
  30.3 0.0 collective-permute-done.4.refs_2_
  30.3 0.1 late.3
  (3 shorter events, 0.0 us)
Async XLA Ops:
  1.3 24.5 %collective-permute-start.8 = (bf16[64,2048]{1,0:T(8,128)(2,1)S(1)}, bf16[64,2048]{1,0:T(8,128)(2,1)S(1)}, u32[]{:S(2)}, u32[]{:S(2)}) collective-permute-start(bf16[64,2048]{1,0:T(8,128)(2,1)S(1)} %get-tuple-element.24), channel_id=1, source_target_pairs={{0,16},{16,0},{1,17},{17,1},{2,18},{18,2},{3,19},{19,3},{4,20},{20... | collective-permute-start | bytes 786440 | tf_op jit(solution)/shard_map/ppermute | solution.py:347
  4.3 22.8 %collective-permute-start.5 = (bf16[64,2048]{1,0:T(8,128)(2,1)S(1)}, bf16[64,2048]{1,0:T(8,128)(2,1)S(1)}, u32[]{:S(2)}, u32[]{:S(2)}) collective-permute-start(bf16[64,2048]{1,0:T(8,128)(2,1)S(1)} %get-tuple-element.19), channel_id=1, source_target_pairs={{0,16},{16,0},{1,17},{17,1},{2,18},{18,2},{3,19},{19,3},{4,20},{20... | collective-permute-start | bytes 786440 | tf_op jit(solution)/shard_map/ppermute | solution.py:347
  4.4 8.8 %collective-permute-start = (bf16[4,128,128]{2,1,0:T(8,128)(2,1)S(1)}, bf16[4,128,128]{2,1,0:T(8,128)(2,1)S(1)}, u32[]{:S(2)}, u32[]{:S(2)}) collective-permute-start(bf16[4,128,128]{2,1,0:T(8,128)(2,1)S(1)} %get-tuple-element.17.refs_3_), channel_id=1, source_target_pairs={{0,8},{8,0},{4,12},{12,4},{1,9},{9,1},{5,13},{13,5},{2,10},{10,2},... | collective-permute-start | bytes 393224 | tf_op jit(solution)/shard_map/ppermute | solution.py:350
  7.4 10.6 %collective-permute-start.2 = (bf16[64,640]{1,0:T(8,128)(2,1)S(1)}, bf16[64,640]{1,0:T(8,128)(2,1)S(1)}, u32[]{:S(2)}, u32[]{:S(2)}) collective-permute-start(bf16[64,640]{1,0:T(8,128)(2,1)S(1)} %get-tuple-element.18), channel_id=1, source_target_pairs={{0,16},{16,0},{1,17},{17,1},{2,18},{18,2},{3,19},{19,3},{4,20},{20... | collective-permute-start | bytes 245768 | tf_op jit(solution)/shard_map/ppermute | solution.py:345
  8.9 11.9 %collective-permute-start.6 = (bf16[4,128,128]{2,1,0:T(8,128)(2,1)S(1)}, bf16[4,128,128]{2,1,0:T(8,128)(2,1)S(1)}, u32[]{:S(2)}, u32[]{:S(2)}) collective-permute-start(bf16[4,128,128]{2,1,0:T(8,128)(2,1)S(1)} %get-tuple-element.17.refs_3_), channel_id=1, source_target_pairs={{0,4},{4,0},{8,12},{12,8},{1,5},{5,1},{9,13},{13,9},{2,6},{6,2},{1... | collective-permute-start | bytes 393224 | tf_op jit(solution)/shard_map/ppermute | solution.py:349
  13.2 15.4 %collective-permute-start.1 = (bf16[4,128,128]{2,1,0:T(8,128)(2,1)S(1)}, bf16[4,128,128]{2,1,0:T(8,128)(2,1)S(1)}, u32[]{:S(2)}, u32[]{:S(2)}) collective-permute-start(bf16[4,128,128]{2,1,0:T(8,128)(2,1)S(1)} %collective-permute-done.refs_5_), channel_id=1, source_target_pairs={{0,4},{4,0},{8,12},{12,8},{1,5},{5,1},{9,13},{13,9},{2,6},{6,2},{1... | collective-permute-start | bytes 393224 | tf_op jit(solution)/shard_map/ppermute | solution.py:351
  18.0 5.3 %collective-permute-start.3 = (bf16[64,512]{1,0:T(8,128)(2,1)S(1)}, bf16[64,512]{1,0:T(8,128)(2,1)S(1)}, u32[]{:S(2)}, u32[]{:S(2)}) collective-permute-start(bf16[64,512]{1,0:T(8,128)(2,1)S(1)} %slice.8.refs_6_), channel_id=1, source_target_pairs={{0,8},{8,0},{4,12},{12,4},{1,9},{9,1},{5,13},{13,5},{2,10},{10,2},... | collective-permute-start | bytes 196616 | tf_op jit(solution)/shard_map/ppermute | solution.py:352
  20.8 4.9 %collective-permute-start.7 = (bf16[64,512]{1,0:T(8,128)(2,1)S(1)}, bf16[64,512]{1,0:T(8,128)(2,1)S(1)}, u32[]{:S(2)}, u32[]{:S(2)}) collective-permute-start(bf16[64,512]{1,0:T(8,128)(2,1)S(1)} %slice.8.refs_6_), channel_id=1, source_target_pairs={{0,4},{4,0},{8,12},{12,8},{1,5},{5,1},{9,13},{13,9},{2,6},{6,2},{1... | collective-permute-start | bytes 196616 | tf_op jit(solution)/shard_map/ppermute | solution.py:353
  23.3 7.1 %collective-permute-start.4 = (bf16[64,512]{1,0:T(8,128)(2,1)S(1)}, bf16[64,512]{1,0:T(8,128)(2,1)S(1)}, u32[]{:S(2)}, u32[]{:S(2)}) collective-permute-start(bf16[64,512]{1,0:T(8,128)(2,1)S(1)} %collective-permute-done.3.refs_8_), channel_id=1, source_target_pairs={{0,4},{4,0},{8,12},{12,8},{1,5},{5,1},{9,13},{13,9},{2,6},{6,2},{1... | collective-permute-start | bytes 196616 | tf_op jit(solution)/shard_map/ppermute | solution.py:354

commit v6 on v5

--- a/solution.py
+++ b/solution.py
@@ -360,16 +360,17 @@
     if mirror:
         first, states = 0, []
         most = len(early) * (held + rows)
+        whole = pl.cdiv(most, width) * width
         for x, n in zip(q, sizes):
             held_heads = max(1, n * kv_heads // heads)
             call = pl.pallas_call(
                 functools.partial(
-                    early_kernel, cs=len(early), bs=len(early), heads=heads, kv_heads=kv_heads, width=width, group=group, first=first
+                    early_kernel, cs=len(early), bs=len(early), heads=heads, kv_heads=kv_heads, width=width, group=2 * group, first=first
                 ),
                 out_shape=(jax.ShapeDtypeStruct((rows, n * width), bf16),) + (jax.ShapeDtypeStruct((n * rows, width), f32),) * 3,
                 in_specs=[VMEM] * (3 + 2 * len(early)),
                 out_specs=(VMEM,) * 4,
-                scratch_shapes=[pltpu.VMEM((held_heads, most, 2 * width), bf16), pltpu.VMEM((held_heads, most, width), bf16)],
+                scratch_shapes=[pltpu.VMEM((held_heads, whole, 2 * width), bf16), pltpu.VMEM((held_heads, whole, width), bf16)],
                 compiler_params=pltpu.CompilerParams(vmem_limit_bytes=limit),
                 name="early",
             )

time: 30.6 us -> 30.2 us (0.987)
  Pallas kernels: 5.94 us -> 5.55 us
    pallas_call x2, Pallas kernels: 2.8 us -> 2.41 us  [body(): states += call(x, scale, bias, *c[:len(early)], *b[:len(early)])]
  transfers between devices with their start and end apart: 9 -> 9, of which waited for: 3 -> 3; matrix products, arithmetic and copies ran while one was open for 0% -> 0% of each run, Pallas kernels for 15% -> 14%
where the time goes in v6:
time: 30.2 us; the launch traced here: 30 us
  starting transfers between devices  16.1 us (53%)
  waiting for transfers between devices  7.58 us (25%)
  Pallas kernels  5.55 us (18%)
  between operations  0.75 us (2%)
    ppermute x1, waiting for transfers between devices, body(): kv = lax.ppermute(kv, 'section', relay)  4.04 us
    ppermute x2, starting transfers between devices, body(): q = [lax.ppermute(x, 'section', relay) for x in q]  3.11 us
    ppermute x1, starting transfers between devices, body(): far = lax.ppermute(cached, 'seq', FAR)  3.05 us
    ppermute x1, starting transfers between devices, body(): far = lax.ppermute(kv, 'seq', FAR)  2.84 us
    ppermute x1, waiting for transfers between devices, body(): far = lax.ppermute(cached, 'seq', FAR)  2.67 us
    pallas_call x2, Pallas kernels, body(): states += call(x, scale, bias, *c[:len(early)], *b[:len(early)])  2.41 us
    pallas_call x2, Pallas kernels, body(): out = [call(bias, *c[len(early):], *blocks, *states, *out)]  1.82 us
    ppermute x1, starting transfers between devices, body(): b = [kv, near, far, lax.ppermute(far, 'seq', NEAR)]  1.72 us
  transfers between devices with their start and end apart: 9, of which 3 were waited for; matrix products, arithmetic and copies ran while one was open for 0% of the time, Pallas kernels for 14%

profile of v6, /device:TPU:0, one launch (start us, length us, event | category | flops | bytes accessed | tf_op | source)
XLA Modules:
  0.0 30.0 jit_solution(15360644745827516541)
XLA Ops:
  0.0 1.3 %first.1 = (bf16[64,640]{1,0:T(8,128)(2,1)S(1)}, bf16[4,128,128]{2,1,0:T(8,128)(2,1)S(1)}, bf16[64,2048]{1,0:T(8,128)(2,1)S(1)}, bf16[64,2048]{1,0:T(8,128)(2,1)S(1)}) custom-call(bf16[1,64,4096]{2,1,0:T(8,128)(2,1)} %refs_0_.1, s32[1,64,128]{2,1,0:T(8,128)} %refs_1_.1, bf16[1,64,256]{2,1,0:T(8,128)(2,1)} %refs_2_.1, s32[1,8,64]{2,1,0:T(8,128)} %bitcast.4, ...), custom_call_target="tpu_custom_call" | custom-call | tf_op jit(solution)/shard_map/first/pallas_call | solution.py:312
  1.3 3.0 %collective-permute-start.8 = (bf16[64,2048]{1,0:T(8,128)(2,1)S(1)}, bf16[64,2048]{1,0:T(8,128)(2,1)S(1)}, u32[]{:S(2)}, u32[]{:S(2)}) collective-permute-start(bf16[64,2048]{1,0:T(8,128)(2,1)S(1)} %get-tuple-element.24), channel_id=1, source_target_pairs={{0,16},{16,0},{1,17},{17,1},{2,18},{18,2},{3,19},{19,3},{4,20},{20... | collective-permute-start | bytes 786440 | tf_op jit(solution)/shard_map/ppermute | solution.py:347
  4.3 0.1 collective-permute-start.5
  4.4 3.0 %collective-permute-start = (bf16[4,128,128]{2,1,0:T(8,128)(2,1)S(1)}, bf16[4,128,128]{2,1,0:T(8,128)(2,1)S(1)}, u32[]{:S(2)}, u32[]{:S(2)}) collective-permute-start(bf16[4,128,128]{2,1,0:T(8,128)(2,1)S(1)} %get-tuple-element.17.refs_3_), channel_id=1, source_target_pairs={{0,8},{8,0},{4,12},{12,4},{1,9},{9,1},{5,13},{13,5},{2,10},{10,2},... | collective-permute-start | bytes 393224 | tf_op jit(solution)/shard_map/ppermute | solution.py:350
  7.4 1.5 %collective-permute-start.2 = (bf16[64,640]{1,0:T(8,128)(2,1)S(1)}, bf16[64,640]{1,0:T(8,128)(2,1)S(1)}, u32[]{:S(2)}, u32[]{:S(2)}) collective-permute-start(bf16[64,640]{1,0:T(8,128)(2,1)S(1)} %get-tuple-element.18), channel_id=1, source_target_pairs={{0,16},{16,0},{1,17},{17,1},{2,18},{18,2},{3,19},{19,3},{4,20},{20... | collective-permute-start | bytes 245768 | tf_op jit(solution)/shard_map/ppermute | solution.py:345
  8.9 1.6 %collective-permute-start.6 = (bf16[4,128,128]{2,1,0:T(8,128)(2,1)S(1)}, bf16[4,128,128]{2,1,0:T(8,128)(2,1)S(1)}, u32[]{:S(2)}, u32[]{:S(2)}) collective-permute-start(bf16[4,128,128]{2,1,0:T(8,128)(2,1)S(1)} %get-tuple-element.17.refs_3_), channel_id=1, source_target_pairs={{0,4},{4,0},{8,12},{12,8},{1,5},{5,1},{9,13},{13,9},{2,6},{6,2},{1... | collective-permute-start | bytes 393224 | tf_op jit(solution)/shard_map/ppermute | solution.py:349
  10.5 2.7 %collective-permute-done.refs_5_ = bf16[4,128,128]{2,1,0:T(8,128)(2,1)S(1)} collective-permute-done((bf16[4,128,128]{2,1,0:T(8,128)(2,1)S(1)}, bf16[4,128,128]{2,1,0:T(8,128)(2,1)S(1)}, u32[]{:S(2)}, u32[]{:S(2)}) %collective-permute-start) | collective-permute-done | bytes 131104 | tf_op jit(solution)/shard_map/ppermute | solution.py:350
  13.2 0.8 %collective-permute-start.1 = (bf16[4,128,128]{2,1,0:T(8,128)(2,1)S(1)}, bf16[4,128,128]{2,1,0:T(8,128)(2,1)S(1)}, u32[]{:S(2)}, u32[]{:S(2)}) collective-permute-start(bf16[4,128,128]{2,1,0:T(8,128)(2,1)S(1)} %collective-permute-done.refs_5_), channel_id=1, source_target_pairs={{0,4},{4,0},{8,12},{12,8},{1,5},{5,1},{9,13},{13,9},{2,6},{6,2},{1... | collective-permute-start | bytes 393224 | tf_op jit(solution)/shard_map/ppermute | solution.py:351
  13.9 4.0 %collective-permute-done.2 = bf16[64,640]{1,0:T(8,128)(2,1)S(1)} collective-permute-done((bf16[64,640]{1,0:T(8,128)(2,1)S(1)}, bf16[64,640]{1,0:T(8,128)(2,1)S(1)}, u32[]{:S(2)}, u32[]{:S(2)}) %collective-permute-start.2) | collective-permute-done | bytes 81952 | tf_op jit(solution)/shard_map/ppermute | solution.py:345
  18.0 2.8 %collective-permute-start.3 = (bf16[64,512]{1,0:T(8,128)(2,1)S(1)}, bf16[64,512]{1,0:T(8,128)(2,1)S(1)}, u32[]{:S(2)}, u32[]{:S(2)}) collective-permute-start(bf16[64,512]{1,0:T(8,128)(2,1)S(1)} %slice.8.refs_6_), channel_id=1, source_target_pairs={{0,8},{8,0},{4,12},{12,4},{1,9},{9,1},{5,13},{13,5},{2,10},{10,2},... | collective-permute-start | bytes 196616 | tf_op jit(solution)/shard_map/ppermute | solution.py:352
  20.8 0.0 collective-permute-done.6.refs_4_
  20.8 1.6 %collective-permute-start.7 = (bf16[64,512]{1,0:T(8,128)(2,1)S(1)}, bf16[64,512]{1,0:T(8,128)(2,1)S(1)}, u32[]{:S(2)}, u32[]{:S(2)}) collective-permute-start(bf16[64,512]{1,0:T(8,128)(2,1)S(1)} %slice.8.refs_6_), channel_id=1, source_target_pairs={{0,4},{4,0},{8,12},{12,8},{1,5},{5,1},{9,13},{13,9},{2,6},{6,2},{1... | collective-permute-start | bytes 196616 | tf_op jit(solution)/shard_map/ppermute | solution.py:353
  22.4 0.8 %collective-permute-done.3.refs_8_ = bf16[64,512]{1,0:T(8,128)(2,1)S(1)} collective-permute-done((bf16[64,512]{1,0:T(8,128)(2,1)S(1)}, bf16[64,512]{1,0:T(8,128)(2,1)S(1)}, u32[]{:S(2)}, u32[]{:S(2)}) %collective-permute-start.3) | collective-permute-done | bytes 65568 | tf_op jit(solution)/shard_map/ppermute | solution.py:352
  23.3 1.7 %collective-permute-start.4 = (bf16[64,512]{1,0:T(8,128)(2,1)S(1)}, bf16[64,512]{1,0:T(8,128)(2,1)S(1)}, u32[]{:S(2)}, u32[]{:S(2)}) collective-permute-start(bf16[64,512]{1,0:T(8,128)(2,1)S(1)} %collective-permute-done.3.refs_8_), channel_id=1, source_target_pairs={{0,4},{4,0},{8,12},{12,8},{1,5},{5,1},{9,13},{13,9},{2,6},{6,2},{1... | collective-permute-start | bytes 196616 | tf_op jit(solution)/shard_map/ppermute | solution.py:354
  25.6 0.1 bias.1.refs_2_.refs_0_
  25.7 0.0 collective-permute-done.7.refs_7_
  25.7 0.0 collective-permute-done.8.refs_0_
  25.7 1.2 %early.3 = (bf16[64,2048]{1,0:T(8,128)(2,1)S(1)}, f32[1024,128]{1,0:T(8,128)S(1)}, f32[1024,128]{1,0:T(8,128)S(1)}, f32[1024,128]{1,0:T(8,128)S(1)}) custom-call(bf16[64,2048]{1,0:T(8,128)(2,1)S(1)} %collective-permute-done.8.refs_0_, bf16[64,128]{1,0:T(8,128)(2,1)S(1)} %slice.9.refs_1_, bf16[768,128]{1,0:T(8,128)(2,1)S(1)} %bias.1.refs_2_.refs_0_, ...), custom_call_target="tpu_custom_call" | custom-call | tf_op jit(solution)/shard_map/early/pallas_call | solution.py:377
  26.9 0.0 collective-permute-done.5.refs_0_
  27.0 1.2 %early.2 = (bf16[64,2048]{1,0:T(8,128)(2,1)S(1)}, f32[1024,128]{1,0:T(8,128)S(1)}, f32[1024,128]{1,0:T(8,128)S(1)}, f32[1024,128]{1,0:T(8,128)S(1)}) custom-call(bf16[64,2048]{1,0:T(8,128)(2,1)S(1)} %collective-permute-done.5.refs_0_, bf16[64,128]{1,0:T(8,128)(2,1)S(1)} %slice.9.refs_1_, bf16[768,128]{1,0:T(8,128)(2,1)S(1)} %bias.1.refs_2_.refs_0_, ...), custom_call_target="tpu_custom_call" | custom-call | tf_op jit(solution)/shard_map/early/pallas_call | solution.py:377
  28.2 0.0 collective-permute-done.1.refs_1_
  28.2 1.7 %late.2.refs_11_ = bf16[1,64,4096]{2,1,0:T(8,128)(2,1)} custom-call(bf16[768,128]{1,0:T(8,128)(2,1)S(1)} %bias.1.refs_2_.refs_0_, bf16[4,128,128]{2,1,0:T(8,128)(2,1)S(1)} %collective-permute-done.1.refs_1_, bf16[64,2048]{1,0:T(8,128)(2,1)S(1)} %get-tuple-element.20.refs_2_.refs_3_, f32[1024,128]{1,0:T(8,128)S(1)} %get-tuple-element.21.refs_3_.refs_4_, ...), custom_call_target="tpu_custom_call" | custom-call | tf_op jit(solution)/shard_map/late/pallas_call | solution.py:409
  29.9 0.0 collective-permute-done.4.refs_2_
  29.9 0.1 late.3
  (3 shorter events, 0.0 us)
Async XLA Ops:
  1.3 24.5 %collective-permute-start.8 = (bf16[64,2048]{1,0:T(8,128)(2,1)S(1)}, bf16[64,2048]{1,0:T(8,128)(2,1)S(1)}, u32[]{:S(2)}, u32[]{:S(2)}) collective-permute-start(bf16[64,2048]{1,0:T(8,128)(2,1)S(1)} %get-tuple-element.24), channel_id=1, source_target_pairs={{0,16},{16,0},{1,17},{17,1},{2,18},{18,2},{3,19},{19,3},{4,20},{20... | collective-permute-start | bytes 786440 | tf_op jit(solution)/shard_map/ppermute | solution.py:347
  4.3 22.6 %collective-permute-start.5 = (bf16[64,2048]{1,0:T(8,128)(2,1)S(1)}, bf16[64,2048]{1,0:T(8,128)(2,1)S(1)}, u32[]{:S(2)}, u32[]{:S(2)}) collective-permute-start(bf16[64,2048]{1,0:T(8,128)(2,1)S(1)} %get-tuple-element.19), channel_id=1, source_target_pairs={{0,16},{16,0},{1,17},{17,1},{2,18},{18,2},{3,19},{19,3},{4,20},{20... | collective-permute-start | bytes 786440 | tf_op jit(solution)/shard_map/ppermute | solution.py:347
  4.4 8.8 %collective-permute-start = (bf16[4,128,128]{2,1,0:T(8,128)(2,1)S(1)}, bf16[4,128,128]{2,1,0:T(8,128)(2,1)S(1)}, u32[]{:S(2)}, u32[]{:S(2)}) collective-permute-start(bf16[4,128,128]{2,1,0:T(8,128)(2,1)S(1)} %get-tuple-element.17.refs_3_), channel_id=1, source_target_pairs={{0,8},{8,0},{4,12},{12,4},{1,9},{9,1},{5,13},{13,5},{2,10},{10,2},... | collective-permute-start | bytes 393224 | tf_op jit(solution)/shard_map/ppermute | solution.py:350
  7.4 10.6 %collective-permute-start.2 = (bf16[64,640]{1,0:T(8,128)(2,1)S(1)}, bf16[64,640]{1,0:T(8,128)(2,1)S(1)}, u32[]{:S(2)}, u32[]{:S(2)}) collective-permute-start(bf16[64,640]{1,0:T(8,128)(2,1)S(1)} %get-tuple-element.18), channel_id=1, source_target_pairs={{0,16},{16,0},{1,17},{17,1},{2,18},{18,2},{3,19},{19,3},{4,20},{20... | collective-permute-start | bytes 245768 | tf_op jit(solution)/shard_map/ppermute | solution.py:345
  8.9 11.9 %collective-permute-start.6 = (bf16[4,128,128]{2,1,0:T(8,128)(2,1)S(1)}, bf16[4,128,128]{2,1,0:T(8,128)(2,1)S(1)}, u32[]{:S(2)}, u32[]{:S(2)}) collective-permute-start(bf16[4,128,128]{2,1,0:T(8,128)(2,1)S(1)} %get-tuple-element.17.refs_3_), channel_id=1, source_target_pairs={{0,4},{4,0},{8,12},{12,8},{1,5},{5,1},{9,13},{13,9},{2,6},{6,2},{1... | collective-permute-start | bytes 393224 | tf_op jit(solution)/shard_map/ppermute | solution.py:349
  13.2 15.0 %collective-permute-start.1 = (bf16[4,128,128]{2,1,0:T(8,128)(2,1)S(1)}, bf16[4,128,128]{2,1,0:T(8,128)(2,1)S(1)}, u32[]{:S(2)}, u32[]{:S(2)}) collective-permute-start(bf16[4,128,128]{2,1,0:T(8,128)(2,1)S(1)} %collective-permute-done.refs_5_), channel_id=1, source_target_pairs={{0,4},{4,0},{8,12},{12,8},{1,5},{5,1},{9,13},{13,9},{2,6},{6,2},{1... | collective-permute-start | bytes 393224 | tf_op jit(solution)/shard_map/ppermute | solution.py:351
  18.0 5.3 %collective-permute-start.3 = (bf16[64,512]{1,0:T(8,128)(2,1)S(1)}, bf16[64,512]{1,0:T(8,128)(2,1)S(1)}, u32[]{:S(2)}, u32[]{:S(2)}) collective-permute-start(bf16[64,512]{1,0:T(8,128)(2,1)S(1)} %slice.8.refs_6_), channel_id=1, source_target_pairs={{0,8},{8,0},{4,12},{12,4},{1,9},{9,1},{5,13},{13,5},{2,10},{10,2},... | collective-permute-start | bytes 196616 | tf_op jit(solution)/shard_map/ppermute | solution.py:352
  20.8 4.9 %collective-permute-start.7 = (bf16[64,512]{1,0:T(8,128)(2,1)S(1)}, bf16[64,512]{1,0:T(8,128)(2,1)S(1)}, u32[]{:S(2)}, u32[]{:S(2)}) collective-permute-start(bf16[64,512]{1,0:T(8,128)(2,1)S(1)} %slice.8.refs_6_), channel_id=1, source_target_pairs={{0,4},{4,0},{8,12},{12,8},{1,5},{5,1},{9,13},{13,9},{2,6},{6,2},{1... | collective-permute-start | bytes 196616 | tf_op jit(solution)/shard_map/ppermute | solution.py:353
  23.3 6.7 %collective-permute-start.4 = (bf16[64,512]{1,0:T(8,128)(2,1)S(1)}, bf16[64,512]{1,0:T(8,128)(2,1)S(1)}, u32[]{:S(2)}, u32[]{:S(2)}) collective-permute-start(bf16[64,512]{1,0:T(8,128)(2,1)S(1)} %collective-permute-done.3.refs_8_), channel_id=1, source_target_pairs={{0,4},{4,0},{8,12},{12,8},{1,5},{5,1},{9,13},{13,9},{2,6},{6,2},{1... | collective-permute-start | bytes 196616 | tf_op jit(solution)/shard_map/ppermute | solution.py:354

commit v7 on v6

--- a/solution.py
+++ b/solution.py
@@ -305,9 +305,10 @@
     slots = range(count)
     if mirror:
         early, late = slots[:-1], slots[-1:]
+        early_b, late_b = slots[0::2], slots[1::2]
     else:
-        early, late = slots, ()
-    pieces = [(cached, d) for part in (early, late) for cached in (True, False) for d in part]
+        early, late, early_b, late_b = slots, (), slots, ()
+    pieces = [(cached, d) for part in ((early, early_b), (late, late_b)) for cached, group in zip((True, False), part) for d in group]
     sizes = [heads * n // sum(SHARES) for n in SHARES]
     kv, cached, *q = pl.pallas_call(
         functools.partial(first_kernel, width=width),
@@ -351,7 +352,7 @@
         c = [cached, near, far, lax.ppermute(far, "seq", NEAR)]
         far = lax.ppermute(kv, "seq", FAR)
         near = lax.ppermute(kv, "seq", NEAR)
-        b = [kv, near, far, lax.ppermute(far, "seq", NEAR)]
+        b = [kv, far, near, lax.ppermute(far, "seq", NEAR)]
     else:
         c = [lax.all_gather(cached, "seq", axis=0)]
         b = [lax.all_gather(kv, "seq", axis=0)]
@@ -359,26 +360,26 @@
     limit = (8 << 20) + keys * width * kv_heads * 8 + keys * group * rows * 12 + 4 * rows * features
     if mirror:
         first, states = 0, []
-        most = len(early) * (held + rows)
+        most = len(early) * held + len(early_b) * rows
         whole = pl.cdiv(most, width) * width
         for x, n in zip(q, sizes):
             held_heads = max(1, n * kv_heads // heads)
             call = pl.pallas_call(
                 functools.partial(
-                    early_kernel, cs=len(early), bs=len(early), heads=heads, kv_heads=kv_heads, width=width, group=2 * group, first=first
+                    early_kernel, cs=len(early), bs=len(early_b), heads=heads, kv_heads=kv_heads, width=width, group=2 * group, first=first
                 ),
                 out_shape=(jax.ShapeDtypeStruct((rows, n * width), bf16),) + (jax.ShapeDtypeStruct((n * rows, width), f32),) * 3,
-                in_specs=[VMEM] * (3 + 2 * len(early)),
+                in_specs=[VMEM] * (3 + len(early) + len(early_b)),
                 out_specs=(VMEM,) * 4,
                 scratch_shapes=[pltpu.VMEM((held_heads, whole, 2 * width), bf16), pltpu.VMEM((held_heads, whole, width), bf16)],
                 compiler_params=pltpu.CompilerParams(vmem_limit_bytes=limit),
                 name="early",
             )
-            states += call(x, scale, bias, *c[: len(early)], *b[: len(early)])
+            states += call(x, scale, bias, *c[: len(early)], *b[: len(early_b)])
             first += n
         out = []
         for lead in (True, False):
-            blocks = [] if lead else b[len(early) :]
+            blocks = [] if lead else b[len(early_b) :]
             fresh = len(late) * held + len(blocks) * rows
             padded = pl.cdiv(fresh, width) * width
             call = pl.pallas_call(

time: 30.2 us -> 29.9 us (0.990)
  Pallas kernels: 5.55 us -> 5.24 us
    pallas_call x2, Pallas kernels: 2.41 us -> 2.1 us  [body(): states += call(x, scale, bias, *c[:len(early)], *b[:len(early_b)])]
  transfers between devices with their start and end apart: 9 -> 9, of which waited for: 3 -> 3; matrix products, arithmetic and copies ran while one was open for 0% -> 0% of each run, Pallas kernels for 14% -> 13%
where the time goes in v7:
time: 29.9 us; the launch traced here: 29.7 us
  starting transfers between devices  16.1 us (54%)
  waiting for transfers between devices  7.58 us (25%)
  Pallas kernels  5.24 us (18%)
  between operations  0.74 us (2%)
    ppermute x1, waiting for transfers between devices, body(): kv = lax.ppermute(kv, 'section', relay)  4.04 us
    ppermute x2, starting transfers between devices, body(): q = [lax.ppermute(x, 'section', relay) for x in q]  3.11 us
    ppermute x1, starting transfers between devices, body(): far = lax.ppermute(cached, 'seq', FAR)  3.05 us
    ppermute x1, starting transfers between devices, body(): far = lax.ppermute(kv, 'seq', FAR)  2.84 us
    ppermute x1, waiting for transfers between devices, body(): far = lax.ppermute(cached, 'seq', FAR)  2.67 us
    pallas_call x2, Pallas kernels, body(): states += call(x, scale, bias, *c[:len(early)], *b[:len(early_b)])  2.1 us
    pallas_call x2, Pallas kernels, body(): out = [call(bias, *c[len(early):], *blocks, *states, *out)]  1.82 us
    ppermute x1, starting transfers between devices, body(): b = [kv, far, near, lax.ppermute(far, 'seq', NEAR)]  1.72 us
  transfers between devices with their start and end apart: 9, of which 3 were waited for; matrix products, arithmetic and copies ran while one was open for 0% of the time, Pallas kernels for 13%

profile of v7, /device:TPU:0, one launch (start us, length us, event | category | flops | bytes accessed | tf_op | source)
XLA Modules:
  0.0 29.7 jit_solution(6374153889903120123)
XLA Ops:
  0.0 1.3 %first.1 = (bf16[64,640]{1,0:T(8,128)(2,1)S(1)}, bf16[4,128,128]{2,1,0:T(8,128)(2,1)S(1)}, bf16[64,2048]{1,0:T(8,128)(2,1)S(1)}, bf16[64,2048]{1,0:T(8,128)(2,1)S(1)}) custom-call(bf16[1,64,4096]{2,1,0:T(8,128)(2,1)} %refs_0_.1, s32[1,64,128]{2,1,0:T(8,128)} %refs_1_.1, bf16[1,64,256]{2,1,0:T(8,128)(2,1)} %refs_2_.1, s32[1,8,64]{2,1,0:T(8,128)} %bitcast.4, ...), custom_call_target="tpu_custom_call" | custom-call | tf_op jit(solution)/shard_map/first/pallas_call | solution.py:313
  1.3 3.0 %collective-permute-start.8 = (bf16[64,2048]{1,0:T(8,128)(2,1)S(1)}, bf16[64,2048]{1,0:T(8,128)(2,1)S(1)}, u32[]{:S(2)}, u32[]{:S(2)}) collective-permute-start(bf16[64,2048]{1,0:T(8,128)(2,1)S(1)} %get-tuple-element.24), channel_id=1, source_target_pairs={{0,16},{16,0},{1,17},{17,1},{2,18},{18,2},{3,19},{19,3},{4,20},{20... | collective-permute-start | bytes 786440 | tf_op jit(solution)/shard_map/ppermute | solution.py:348
  4.3 0.1 collective-permute-start.6
  4.4 3.0 %collective-permute-start = (bf16[4,128,128]{2,1,0:T(8,128)(2,1)S(1)}, bf16[4,128,128]{2,1,0:T(8,128)(2,1)S(1)}, u32[]{:S(2)}, u32[]{:S(2)}) collective-permute-start(bf16[4,128,128]{2,1,0:T(8,128)(2,1)S(1)} %get-tuple-element.17.refs_3_), channel_id=1, source_target_pairs={{0,8},{8,0},{4,12},{12,4},{1,9},{9,1},{5,13},{13,5},{2,10},{10,2},... | collective-permute-start | bytes 393224 | tf_op jit(solution)/shard_map/ppermute | solution.py:351
  7.4 1.5 %collective-permute-start.2 = (bf16[64,640]{1,0:T(8,128)(2,1)S(1)}, bf16[64,640]{1,0:T(8,128)(2,1)S(1)}, u32[]{:S(2)}, u32[]{:S(2)}) collective-permute-start(bf16[64,640]{1,0:T(8,128)(2,1)S(1)} %get-tuple-element.18), channel_id=1, source_target_pairs={{0,16},{16,0},{1,17},{17,1},{2,18},{18,2},{3,19},{19,3},{4,20},{20... | collective-permute-start | bytes 245768 | tf_op jit(solution)/shard_map/ppermute | solution.py:346
  8.9 1.6 %collective-permute-start.7 = (bf16[4,128,128]{2,1,0:T(8,128)(2,1)S(1)}, bf16[4,128,128]{2,1,0:T(8,128)(2,1)S(1)}, u32[]{:S(2)}, u32[]{:S(2)}) collective-permute-start(bf16[4,128,128]{2,1,0:T(8,128)(2,1)S(1)} %get-tuple-element.17.refs_3_), channel_id=1, source_target_pairs={{0,4},{4,0},{8,12},{12,8},{1,5},{5,1},{9,13},{13,9},{2,6},{6,2},{1... | collective-permute-start | bytes 393224 | tf_op jit(solution)/shard_map/ppermute | solution.py:350
  10.5 2.7 %collective-permute-done.refs_5_ = bf16[4,128,128]{2,1,0:T(8,128)(2,1)S(1)} collective-permute-done((bf16[4,128,128]{2,1,0:T(8,128)(2,1)S(1)}, bf16[4,128,128]{2,1,0:T(8,128)(2,1)S(1)}, u32[]{:S(2)}, u32[]{:S(2)}) %collective-permute-start) | collective-permute-done | bytes 131104 | tf_op jit(solution)/shard_map/ppermute | solution.py:351
  13.2 0.8 %collective-permute-start.1 = (bf16[4,128,128]{2,1,0:T(8,128)(2,1)S(1)}, bf16[4,128,128]{2,1,0:T(8,128)(2,1)S(1)}, u32[]{:S(2)}, u32[]{:S(2)}) collective-permute-start(bf16[4,128,128]{2,1,0:T(8,128)(2,1)S(1)} %collective-permute-done.refs_5_), channel_id=1, source_target_pairs={{0,4},{4,0},{8,12},{12,8},{1,5},{5,1},{9,13},{13,9},{2,6},{6,2},{1... | collective-permute-start | bytes 393224 | tf_op jit(solution)/shard_map/ppermute | solution.py:352
  13.9 4.0 %collective-permute-done.2 = bf16[64,640]{1,0:T(8,128)(2,1)S(1)} collective-permute-done((bf16[64,640]{1,0:T(8,128)(2,1)S(1)}, bf16[64,640]{1,0:T(8,128)(2,1)S(1)}, u32[]{:S(2)}, u32[]{:S(2)}) %collective-permute-start.2) | collective-permute-done | bytes 81952 | tf_op jit(solution)/shard_map/ppermute | solution.py:346
  18.0 2.8 %collective-permute-start.4 = (bf16[64,512]{1,0:T(8,128)(2,1)S(1)}, bf16[64,512]{1,0:T(8,128)(2,1)S(1)}, u32[]{:S(2)}, u32[]{:S(2)}) collective-permute-start(bf16[64,512]{1,0:T(8,128)(2,1)S(1)} %slice.8.refs_6_), channel_id=1, source_target_pairs={{0,8},{8,0},{4,12},{12,4},{1,9},{9,1},{5,13},{13,5},{2,10},{10,2},... | collective-permute-start | bytes 196616 | tf_op jit(solution)/shard_map/ppermute | solution.py:353
  20.8 0.0 collective-permute-done.7.refs_4_
  20.8 1.6 %collective-permute-start.3 = (bf16[64,512]{1,0:T(8,128)(2,1)S(1)}, bf16[64,512]{1,0:T(8,128)(2,1)S(1)}, u32[]{:S(2)}, u32[]{:S(2)}) collective-permute-start(bf16[64,512]{1,0:T(8,128)(2,1)S(1)} %slice.8.refs_6_), channel_id=1, source_target_pairs={{0,4},{4,0},{8,12},{12,8},{1,5},{5,1},{9,13},{13,9},{2,6},{6,2},{1... | collective-permute-start | bytes 196616 | tf_op jit(solution)/shard_map/ppermute | solution.py:354
  22.4 0.8 %collective-permute-done.4.refs_7_ = bf16[64,512]{1,0:T(8,128)(2,1)S(1)} collective-permute-done((bf16[64,512]{1,0:T(8,128)(2,1)S(1)}, bf16[64,512]{1,0:T(8,128)(2,1)S(1)}, u32[]{:S(2)}, u32[]{:S(2)}) %collective-permute-start.4) | collective-permute-done | bytes 65568 | tf_op jit(solution)/shard_map/ppermute | solution.py:353
  23.3 1.7 %collective-permute-start.5 = (bf16[64,512]{1,0:T(8,128)(2,1)S(1)}, bf16[64,512]{1,0:T(8,128)(2,1)S(1)}, u32[]{:S(2)}, u32[]{:S(2)}) collective-permute-start(bf16[64,512]{1,0:T(8,128)(2,1)S(1)} %collective-permute-done.4.refs_7_), channel_id=1, source_target_pairs={{0,4},{4,0},{8,12},{12,8},{1,5},{5,1},{9,13},{13,9},{2,6},{6,2},{1... | collective-permute-start | bytes 196616 | tf_op jit(solution)/shard_map/ppermute | solution.py:355
  25.6 0.1 bias.1.refs_2_.refs_0_
  25.7 0.0 collective-permute-done.8.refs_0_
  25.7 1.1 %early.3 = (bf16[64,2048]{1,0:T(8,128)(2,1)S(1)}, f32[1024,128]{1,0:T(8,128)S(1)}, f32[1024,128]{1,0:T(8,128)S(1)}, f32[1024,128]{1,0:T(8,128)S(1)}) custom-call(bf16[64,2048]{1,0:T(8,128)(2,1)S(1)} %collective-permute-done.8.refs_0_, bf16[64,128]{1,0:T(8,128)(2,1)S(1)} %slice.9.refs_1_, bf16[768,128]{1,0:T(8,128)(2,1)S(1)} %bias.1.refs_2_.refs_0_, ...), custom_call_target="tpu_custom_call" | custom-call | tf_op jit(solution)/shard_map/early/pallas_call | solution.py:378
  26.8 0.0 collective-permute-done.6.refs_0_
  26.8 1.0 %early.2 = (bf16[64,2048]{1,0:T(8,128)(2,1)S(1)}, f32[1024,128]{1,0:T(8,128)S(1)}, f32[1024,128]{1,0:T(8,128)S(1)}, f32[1024,128]{1,0:T(8,128)S(1)}) custom-call(bf16[64,2048]{1,0:T(8,128)(2,1)S(1)} %collective-permute-done.6.refs_0_, bf16[64,128]{1,0:T(8,128)(2,1)S(1)} %slice.9.refs_1_, bf16[768,128]{1,0:T(8,128)(2,1)S(1)} %bias.1.refs_2_.refs_0_, ...), custom_call_target="tpu_custom_call" | custom-call | tf_op jit(solution)/shard_map/early/pallas_call | solution.py:378
  27.8 0.0 collective-permute-done.1.refs_1_
  27.9 1.7 %late.2.refs_12_ = bf16[1,64,4096]{2,1,0:T(8,128)(2,1)} custom-call(bf16[768,128]{1,0:T(8,128)(2,1)S(1)} %bias.1.refs_2_.refs_0_, bf16[4,128,128]{2,1,0:T(8,128)(2,1)S(1)} %collective-permute-done.1.refs_1_, bf16[64,2048]{1,0:T(8,128)(2,1)S(1)} %get-tuple-element.20.refs_2_.refs_4_, f32[1024,128]{1,0:T(8,128)S(1)} %get-tuple-element.21.refs_3_.refs_5_, ...), custom_call_target="tpu_custom_call" | custom-call | tf_op jit(solution)/shard_map/late/pallas_call | solution.py:410
  29.6 0.0 collective-permute-done.3.refs_2_
  29.6 0.0 collective-permute-done.5.refs_3_
  29.6 0.1 late.3
  (3 shorter events, 0.0 us)
Async XLA Ops:
  1.3 24.5 %collective-permute-start.8 = (bf16[64,2048]{1,0:T(8,128)(2,1)S(1)}, bf16[64,2048]{1,0:T(8,128)(2,1)S(1)}, u32[]{:S(2)}, u32[]{:S(2)}) collective-permute-start(bf16[64,2048]{1,0:T(8,128)(2,1)S(1)} %get-tuple-element.24), channel_id=1, source_target_pairs={{0,16},{16,0},{1,17},{17,1},{2,18},{18,2},{3,19},{19,3},{4,20},{20... | collective-permute-start | bytes 786440 | tf_op jit(solution)/shard_map/ppermute | solution.py:348
  4.3 22.5 %collective-permute-start.6 = (bf16[64,2048]{1,0:T(8,128)(2,1)S(1)}, bf16[64,2048]{1,0:T(8,128)(2,1)S(1)}, u32[]{:S(2)}, u32[]{:S(2)}) collective-permute-start(bf16[64,2048]{1,0:T(8,128)(2,1)S(1)} %get-tuple-element.19), channel_id=1, source_target_pairs={{0,16},{16,0},{1,17},{17,1},{2,18},{18,2},{3,19},{19,3},{4,20},{20... | collective-permute-start | bytes 786440 | tf_op jit(solution)/shard_map/ppermute | solution.py:348
  4.4 8.8 %collective-permute-start = (bf16[4,128,128]{2,1,0:T(8,128)(2,1)S(1)}, bf16[4,128,128]{2,1,0:T(8,128)(2,1)S(1)}, u32[]{:S(2)}, u32[]{:S(2)}) collective-permute-start(bf16[4,128,128]{2,1,0:T(8,128)(2,1)S(1)} %get-tuple-element.17.refs_3_), channel_id=1, source_target_pairs={{0,8},{8,0},{4,12},{12,4},{1,9},{9,1},{5,13},{13,5},{2,10},{10,2},... | collective-permute-start | bytes 393224 | tf_op jit(solution)/shard_map/ppermute | solution.py:351
  7.4 10.6 %collective-permute-start.2 = (bf16[64,640]{1,0:T(8,128)(2,1)S(1)}, bf16[64,640]{1,0:T(8,128)(2,1)S(1)}, u32[]{:S(2)}, u32[]{:S(2)}) collective-permute-start(bf16[64,640]{1,0:T(8,128)(2,1)S(1)} %get-tuple-element.18), channel_id=1, source_target_pairs={{0,16},{16,0},{1,17},{17,1},{2,18},{18,2},{3,19},{19,3},{4,20},{20... | collective-permute-start | bytes 245768 | tf_op jit(solution)/shard_map/ppermute | solution.py:346
  8.9 11.9 %collective-permute-start.7 = (bf16[4,128,128]{2,1,0:T(8,128)(2,1)S(1)}, bf16[4,128,128]{2,1,0:T(8,128)(2,1)S(1)}, u32[]{:S(2)}, u32[]{:S(2)}) collective-permute-start(bf16[4,128,128]{2,1,0:T(8,128)(2,1)S(1)} %get-tuple-element.17.refs_3_), channel_id=1, source_target_pairs={{0,4},{4,0},{8,12},{12,8},{1,5},{5,1},{9,13},{13,9},{2,6},{6,2},{1... | collective-permute-start | bytes 393224 | tf_op jit(solution)/shard_map/ppermute | solution.py:350
  13.2 14.7 %collective-permute-start.1 = (bf16[4,128,128]{2,1,0:T(8,128)(2,1)S(1)}, bf16[4,128,128]{2,1,0:T(8,128)(2,1)S(1)}, u32[]{:S(2)}, u32[]{:S(2)}) collective-permute-start(bf16[4,128,128]{2,1,0:T(8,128)(2,1)S(1)} %collective-permute-done.refs_5_), channel_id=1, source_target_pairs={{0,4},{4,0},{8,12},{12,8},{1,5},{5,1},{9,13},{13,9},{2,6},{6,2},{1... | collective-permute-start | bytes 393224 | tf_op jit(solution)/shard_map/ppermute | solution.py:352
  18.0 5.3 %collective-permute-start.4 = (bf16[64,512]{1,0:T(8,128)(2,1)S(1)}, bf16[64,512]{1,0:T(8,128)(2,1)S(1)}, u32[]{:S(2)}, u32[]{:S(2)}) collective-permute-start(bf16[64,512]{1,0:T(8,128)(2,1)S(1)} %slice.8.refs_6_), channel_id=1, source_target_pairs={{0,8},{8,0},{4,12},{12,4},{1,9},{9,1},{5,13},{13,5},{2,10},{10,2},... | collective-permute-start | bytes 196616 | tf_op jit(solution)/shard_map/ppermute | solution.py:353
  20.8 8.8 %collective-permute-start.3 = (bf16[64,512]{1,0:T(8,128)(2,1)S(1)}, bf16[64,512]{1,0:T(8,128)(2,1)S(1)}, u32[]{:S(2)}, u32[]{:S(2)}) collective-permute-start(bf16[64,512]{1,0:T(8,128)(2,1)S(1)} %slice.8.refs_6_), channel_id=1, source_target_pairs={{0,4},{4,0},{8,12},{12,8},{1,5},{5,1},{9,13},{13,9},{2,6},{6,2},{1... | collective-permute-start | bytes 196616 | tf_op jit(solution)/shard_map/ppermute | solution.py:354
  23.3 6.3 %collective-permute-start.5 = (bf16[64,512]{1,0:T(8,128)(2,1)S(1)}, bf16[64,512]{1,0:T(8,128)(2,1)S(1)}, u32[]{:S(2)}, u32[]{:S(2)}) collective-permute-start(bf16[64,512]{1,0:T(8,128)(2,1)S(1)} %collective-permute-done.4.refs_7_), channel_id=1, source_target_pairs={{0,4},{4,0},{8,12},{12,8},{1,5},{5,1},{9,13},{13,9},{2,6},{6,2},{1... | collective-permute-start | bytes 196616 | tf_op jit(solution)/shard_map/ppermute | solution.py:355
